TPU v7x, 32 devices: a whole 2x2x4 slice. The times are simulated.
32 devices in a mesh: win: 2 (over x), wide: 8 (over z, y), narrow: 2 (over core).
Axes of the slice: x: 2, y: 2, z: 4, core: 2. Of those that a mesh axis runs over, the one named last changes fastest.
Arguments:
- window_data: float32 [384, 128, 256], P(('win', 'wide'), 'narrow'), parts along dimension 0, may hold values from -6 to 6
- factor_one: float32 [256, 48], P(('win', 'narrow')), parts along dimension 0, may hold values from -0.5 to 0.5
- factor_two: float32 [512, 48], P('win'), parts along dimension 0, may hold values from -0.375 to 0.375
- factor_three: float32 [384, 48], P(('win', 'wide')), parts along dimension 0, may hold values from -0.4375 to 0.4375
Outputs:
- basis_one: float32 [256, 48], P(('win', 'narrow')), parts along dimension 0
- basis_two: float32 [512, 48], P('win'), parts along dimension 0
- basis_three: float32 [384, 48], P(('win', 'wide')), parts along dimension 0
- core_unfolded: float32 [48, 4608], P(None, ('win', 'wide', 'narrow')), parts along dimension 1
There are 2 independent parts, one for each index of `win`. A program takes and returns all parts, laid end to end along the dimension named above; each array names one. Nothing has to cross between parts.
All inputs are finite; a program needn't handle non-finite values.
Results may differ from a plain program's by a relative error of at most 0.0003.
Values sent between devices are 32-bit elements; how exact they have to be, the bound alone decides.
No kernel may reach another device: no remote copies, remote signals or barrier semaphores. Data moves between devices by JAX's collectives and lax.ppermute only.
A program may use at most 64 MiB of HBM per device.

v0:
```python
import jax
import jax.numpy as jnp
from jax import lax
from jax.sharding import PartitionSpec as P

highest = lax.Precision.HIGHEST


def contract(form, left, right):
    return jnp.einsum(form, left, right, precision=highest)


def orthonormal(basis, gram):
    lower = jnp.linalg.cholesky(gram)
    return lax.linalg.triangular_solve(lower, basis, left_side=False, lower=True, transpose_a=True)


def full_core(partial_value):
    flat = partial_value.reshape(
        partial_value.shape[0], partial_value.shape[1] * partial_value.shape[2]
    )
    shares = lax.psum_scatter(flat, ("wide", "narrow"), scatter_dimension=1, tiled=True)
    whole = lax.all_gather(shares, ("wide", "narrow"), axis=1, tiled=True)
    return whole.reshape(partial_value.shape)


def on_device(window_data, factor_one, factor_two, factor_three):
    rank = factor_one.shape[1]
    along_two = contract("kij,jb->kib", window_data, factor_two)
    unfold_part = contract("kib,kc->ibc", along_two, factor_three).reshape(
        along_two.shape[1], rank * rank
    )
    unfold_rows = lax.psum_scatter(unfold_part, "wide", scatter_dimension=1, tiled=True)
    weights_one = lax.psum(jnp.dot(unfold_rows.T, factor_one, precision=highest), "narrow")
    product_one = lax.psum(jnp.dot(unfold_rows, weights_one, precision=highest), "wide")
    gram_one = lax.psum(jnp.dot(product_one.T, product_one, precision=highest), "narrow")
    basis_one = orthonormal(product_one, gram_one)
    along_one = contract("kij,ia->kaj", window_data, basis_one)
    core_two = full_core(
        contract("kab,kc->abc", contract("kaj,jb->kab", along_one, factor_two), factor_three)
    )
    spread_two = contract("abc,kc->kab", core_two, factor_three)
    product_two = lax.psum(contract("kaj,kab->jb", along_one, spread_two), ("wide", "narrow"))
    basis_two = orthonormal(product_two, jnp.dot(product_two.T, product_two, precision=highest))
    along_new = contract("kij,jb->kib", window_data, basis_two)
    unfold_three = contract("kib,ia->kab", along_new, basis_one)
    core_three = full_core(contract("kab,kc->abc", unfold_three, factor_three))
    product_three = lax.psum(contract("kab,abc->kc", unfold_three, core_three), "narrow")
    gram_three = lax.psum(jnp.dot(product_three.T, product_three, precision=highest), "wide")
    basis_three = orthonormal(product_three, gram_three)
    core_part = contract("kab,kc->abc", unfold_three, basis_three).reshape(rank, rank * rank)
    core_shares = lax.psum_scatter(core_part, ("wide", "narrow"), scatter_dimension=1, tiled=True)
    return (basis_one, basis_two, basis_three, core_shares)


def solution(mesh):
    return jax.shard_map(
        on_device,
        mesh=mesh,
        in_specs=(
            P(("win", "wide"), "narrow", None),
            P(("win", "narrow"), None),
            P("win", None),
            P(("win", "wide"), None),
        ),
        out_specs=(
            P(("win", "narrow"), None),
            P("win", None),
            P(("win", "wide"), None),
            P(None, ("win", "wide", "narrow")),
        ),
        check_vma=False,
    )
```

profile of v0, /device:TPU:0, one launch (start us, length us, event | category | flops | bytes accessed | tf_op | source)
XLA Modules:
  0.0 505.6 jit_solution(5925950153966513324)
XLA Ops:
  7.2 1.3 copy-done
  8.6 3.1 fusion.12
  11.7 2.2 fusion.3
  13.9 67.9 %reduce-scatter.11.cloned.1.call-done = f32[64,288]{0,1:T(8,128)} async-done(((f32[64,2304]{0,1:T(8,128)}), f32[64,288]{0,1:T(8,128)}) %reduce-scatter.11.cloned.1.call-update) | async-done | bytes 73744 | tf_op jit(solution)/shard_map/reduce_scatter | solution.py:33
  81.9 1.2 fusion.34
  83.1 3.5 psum.42
  86.6 1.1 fusion.35
  87.7 34.9 %psum.43 = f32[64,48]{0,1:T(8,128)S(1)} all-reduce(f32[64,48]{0,1:T(8,128)S(1)} %fusion.35), channel_id=1, replica_groups=mesh['win'=2,'wide'=8,'narrow'=2] {'wide'}, use_global_device_ids=true, to_apply=%region_2.0 | all-reduce | flops 3072 | bytes 24576 | tf_op jit(solution)/shard_map/psum | solution.py:35
  122.8 3.4 psum.44
  126.3 4.4 cholesky.59
  130.7 0.6 compare_reduce_fusion.2
  131.4 0.7 fusion.14
  132.0 3.7 custom-call.11
  136.0 1.1 convolution_bitcast_fusion
  137.1 1.6 fusion
  138.7 3.1 fusion.31
  141.8 2.7 copy.45
  144.6 55.5 %reduce-scatter.13.cloned.1.call-done = f32[144,48]{1,0:T(8,128)} async-done(((f32[2304,48]{1,0:T(8,128)}), f32[144,48]{1,0:T(8,128)}) %reduce-scatter.13.cloned.1.call-update) | async-done | bytes 27664
  200.1 1.0 copy.40
  201.0 21.8 %all-gather = f32[16,144,48]{1,2,0:T(8,128)S(1)} all-gather(f32[1,144,48]{1,2,0:T(8,128)S(1)} %bitcast.116), channel_id=1, replica_groups=mesh['win'=2,'wide'=8,'narrow'=2] {'wide','narrow'}, dimensions={0}, use_global_device_ids=true | all-gather | bytes 470016 | tf_op jit(solution)/shard_map/all_gather | solution.py:23
  223.3 1.2 reshape.47
  224.4 2.7 reshape.42
  227.2 4.7 convolution_bitcast_fusion.3
  231.9 1.2 convolution_bitcast_fusion.4
  233.1 57.9 %psum.45 = f32[256,48]{0,1:T(8,128)S(1)} all-reduce(f32[256,48]{0,1:T(8,128)S(1)} %convolution_bitcast_fusion.4), channel_id=1, replica_groups=mesh['win'=2,'wide'=8,'narrow'=2] {'wide','narrow'}, use_global_device_ids=true, to_apply=%region_7.0 | all-reduce | flops 12288 | bytes 98304 | tf_op jit(solution)/shard_map/psum | solution.py:43
  291.3 4.4 cholesky.70
  296.4 0.7 fusion.15
  297.0 3.7 custom-call.12
  301.0 2.3 convolution_bitcast_fusion.2
  303.3 2.1 convolution_bitcast_fusion.1
  305.5 2.0 fusion.7
  307.5 1.5 copy.46
  309.1 55.5 %reduce-scatter.15.cloned.1.call-done = f32[144,48]{1,0:T(8,128)} async-done(((f32[2304,48]{1,0:T(8,128)}), f32[144,48]{1,0:T(8,128)}) %reduce-scatter.15.cloned.1.call-update) | async-done | bytes 27664
  364.6 1.0 copy.42
  365.5 21.8 %all-gather.1 = f32[16,144,48]{1,2,0:T(8,128)S(1)} all-gather(f32[1,144,48]{1,2,0:T(8,128)S(1)} %bitcast.117), channel_id=1, replica_groups=mesh['win'=2,'wide'=8,'narrow'=2] {'wide','narrow'}, dimensions={0}, use_global_device_ids=true | all-gather | bytes 470016 | tf_op jit(solution)/shard_map/all_gather | solution.py:23
  387.8 1.1 reshape.49
  388.9 1.7 reshape.44
  390.7 1.2 convolution_bitcast_fusion.5
  391.9 3.5 psum.46
  395.6 33.0 %psum.47 = f32[48,48]{0,1:T(8,128)S(1)} all-reduce(f32[48,48]{0,1:T(8,128)S(1)} %fusion.38), channel_id=1, replica_groups=mesh['win'=2,'wide'=8,'narrow'=2] {'wide'}, use_global_device_ids=true, to_apply=%region_10.12 | all-reduce | flops 2304 | bytes 18432 | tf_op jit(solution)/shard_map/psum | solution.py:49
  428.7 4.4 cholesky.81
  433.1 0.6 compare_reduce_fusion
  433.8 0.7 fusion.16
  434.4 3.7 custom-call.13
  438.3 2.0 fusion.5
  440.3 1.5 copy.47
  441.9 55.6 %reduce-scatter.17.cloned.1.call-done = f32[144,48]{1,0:T(8,128)} async-done(((f32[2304,48]{1,0:T(8,128)}), f32[144,48]{1,0:T(8,128)}) %reduce-scatter.17.cloned.1.call-update) | async-done | bytes 27664
  497.5 1.6 copy.44
  (41 shorter events, 3.4 us)
Async XLA Ops:
  7.2 1.4 copy-start
  7.2 4.5 copy-start.3
  7.2 74.7 %reduce-scatter.11.cloned.1.call-start = ((), (), s32[]{:S(2)}) async-start(), calls=%async_computation.4 | async-start | bytes 1327104 | tf_op jit(solution)/shard_map/reduce_scatter | solution.py:33
  11.7 70.2 %copy-start.7 = (f32[64,48]{0,1:T(8,128)S(1)}, f32[64,48]{0,1:T(8,128)}, u32[]{:S(2)}) copy-start(f32[64,48]{0,1:T(8,128)} %param.6) | copy-start | bytes 36868
  13.9 186.2 %reduce-scatter.13.cloned.1.call-start = ((), (), s32[]{:S(2)}) async-start(), calls=%async_computation.5 | async-start | bytes 1253376
  135.9 1.1 copy-start.1
  136.0 1.1 copy-start.5
  144.5 220.0 %reduce-scatter.15.cloned.1.call-start = ((), (), s32[]{:S(2)}) async-start(), calls=%async_computation.6 | async-start | bytes 1253376
  297.0 6.3 %copy-start.2 = (f32[64,48]{0,1:T(8,128)S(1)}, f32[64,48]{0,1:T(8,128)}, u32[]{:S(2)}) copy-start(f32[64,48]{0,1:T(8,128)} %copy-done.1) | copy-start | bytes 36868
  301.0 4.5 copy-start.4
  309.0 188.4 %reduce-scatter.17.cloned.1.call-start = ((), (), s32[]{:S(2)}) async-start(), calls=%async_computation.7 | async-start | bytes 1253376
  438.3 3.6 copy-start.6
Sparse Core Ops, SparseCore 0:
  14.0 67.8 reduce-scatter.10
  144.7 55.3 reduce-scatter.12
  309.1 55.3 reduce-scatter.14
  442.0 55.4 reduce-scatter.16
where the time goes:
time: 506 us
  waiting for transfers between devices  235 us (46%)
  blocking collectives  180 us (36%)
  matrix products  30.3 us (6%)
  other arithmetic  28.2 us (6%)
  local copies, waits for them, and re-layouts  18.5 us (4%)
  between operations  14.1 us (3%)
    unnamed x7, waiting for transfers between devices  167 us
    reduce_scatter x1, waiting for transfers between devices, on_device(): lax.psum_scatter(unfold_part, 'wide', scatter_dimension=1, tiled=True)  67.9 us
    psum x1, blocking collectives, on_device(): lax.psum(contract('kaj,kab->jb', along_one, spread_two), ('wide', 'narrow'))  57.9 us
    all_gather x2, blocking collectives, full_core(): whole = lax.all_gather(shares, ('wide', 'narrow'), axis=1, tiled=True)  43.6 us
    psum x1, blocking collectives, on_device(): lax.psum(jnp.dot(unfold_rows, weights_one, precision=highest), 'wide')  34.9 us
    psum x1, blocking collectives, on_device(): lax.psum(jnp.dot(product_three.T, product_three, precision=highest), 'wide')  33 us
    dot_general x12, matrix products, contract(): return jnp.einsum(form, left, right, precision=highest)  26.7 us
    another operation x9, other arithmetic, orthonormal(): lower = jnp.linalg.cholesky(gram)  15.2 us
  transfers between devices with their start and end apart: 4, of which 4 were waited for; matrix products, arithmetic and copies ran while one was open for 0% of the time, Pallas kernels for 0%

commit v1 on v0

v1 whole, which is shorter than its diff:
```python
import jax
import jax.numpy as jnp
from jax import lax
from jax.sharding import PartitionSpec as P

highest = lax.Precision.HIGHEST
fine = lax.Precision.HIGH
group = ("wide", "narrow")


def contract(form, left, right, precision=fine):
    return jnp.einsum(form, left, right, precision=precision)


def total(part, axis):
    size = lax.axis_size(axis)
    if size & (size - 1):
        return lax.psum(part, axis)
    step = 1
    while step < size:
        part = part + lax.ppermute(part, axis, [(at, at ^ step) for at in range(size)])
        step *= 2
    return part


def orthonormal(product_t):
    gram = jnp.einsum("an,bn->ab", product_t, product_t, precision=highest)
    lower = jnp.linalg.cholesky(gram)
    return lax.linalg.triangular_solve(lower, product_t, left_side=True, lower=True)


def swap(value):
    return lax.ppermute(value, "narrow", [(0, 1), (1, 0)])


def on_device(window_data, factor_one, factor_two, factor_three):
    wide = lax.axis_size("wide")
    narrow = lax.axis_size("narrow")
    count = wide * narrow
    depth, rows, cols = window_data.shape
    rank = factor_one.shape[1]
    share = -(-rank // count)
    spare = share * count - rank
    half = depth // narrow
    core_at = lax.axis_index("narrow")

    own = lax.dynamic_slice_in_dim(window_data, core_at * half, half, 0)
    sent = lax.dynamic_slice_in_dim(window_data, (1 - core_at) * half, half, 0)
    other = swap(sent)
    factor_other = swap(factor_one)

    two_t = jnp.pad(factor_two.T, ((0, spare), (0, 0)))
    along = contract("bj,kij->bki", two_t, window_data).reshape(count, share, depth * rows)
    three_own = lax.dynamic_slice_in_dim(factor_three, core_at * half, half, 0)
    three_flat = jnp.broadcast_to(three_own.reshape(1, 1, half * rank), (count, 1, half * rank))
    packed = jnp.concatenate([along.reshape(count, -1), three_flat.reshape(count, -1)], axis=1)
    width = packed.shape[1]
    full = -(-width // 1024) * 1024
    packed = jnp.pad(packed, ((0, 0), (0, full - width))).reshape(count, full // 128, 128)
    got = lax.all_to_all(packed, group, 0, 0, tiled=True).reshape(count, full)
    three = got[:, share * depth * rows : width].reshape(wide, depth, rank)
    got = got[:, : share * depth * rows].reshape(wide, narrow, share, depth, rows)
    first = jnp.where(core_at == 0, factor_one, factor_other)
    second = jnp.where(core_at == 0, factor_other, factor_one)
    one = jnp.stack([first, second])
    unfold = contract("wnbki,wkc->bcni", got, three)
    weights = contract("bcni,nia->bca", unfold, one)
    product = contract("bcni,bca->ani", unfold, weights).reshape(rank, narrow * rows)
    product = total(total(product, "narrow"), "wide")
    one_t = orthonormal(product)

    one_pad = jnp.pad(one_t, ((0, spare), (0, 0)))
    one_own = lax.dynamic_slice_in_dim(one_pad, core_at * rows, rows, 1)
    one_other = lax.dynamic_slice_in_dim(one_pad, (1 - core_at) * rows, rows, 1)
    along = contract("ai,kij->akj", one_own, own) + contract("ai,kij->akj", one_other, other)
    got = lax.all_to_all(
        along.reshape(count, share * half * cols // 128, 128), group, 0, 0, tiled=True
    ).reshape(count, share, half, cols)
    three = three.reshape(count, half, rank)
    unfold = contract("dakj,dkc->acj", got, three)
    weights = contract("acj,jb->acb", unfold, factor_two)
    product = contract("acj,acb->bj", unfold, weights)
    product = total(total(product, "narrow"), "wide")
    two_t = orthonormal(product)

    unfold = contract("dakj,bj->dakb", got, two_t)
    weights = contract("dakb,dkc->abc", unfold, three)
    product = contract("dakb,abc->cdk", unfold, weights).reshape(rank, count * half)
    product = total(total(product, "narrow"), "wide")
    three_t = orthonormal(product)
    core = contract("dakb,cdk->abc", unfold, three_t.reshape(rank, count, half))
    core = core.reshape(share, count, rank * rank // count).transpose(1, 0, 2)
    core = lax.all_to_all(core, group, 0, 0, tiled=True)
    core = core.reshape(count * share, rank * rank // count)[:rank]
    basis_three = lax.dynamic_slice_in_dim(three_t, lax.axis_index("wide") * depth, depth, 1).T
    return (one_own[:rank].T, two_t.T, basis_three, core)


def solution(mesh):
    return jax.shard_map(
        on_device,
        mesh=mesh,
        in_specs=(
            P(("win", "wide"), "narrow", None),
            P(("win", "narrow"), None),
            P("win", None),
            P(("win", "wide"), None),
        ),
        out_specs=(
            P(("win", "narrow"), None),
            P("win", None),
            P(("win", "wide"), None),
            P(None, ("win", "wide", "narrow")),
        ),
        check_vma=False,
    )
```

time: 506 us -> 141 us (0.28)
  blocking collectives: 180 us -> 0 us
  waiting for transfers between devices: 235 us -> 60.9 us
  starting transfers between devices: 0.16 us -> 33.2 us
  matrix products: 30.3 us -> 7.83 us
  between operations: 14.1 us -> 1.11 us
  local copies, waits for them, and re-layouts: 18.5 us -> 8.72 us
    unnamed x7 -> x0, waiting for transfers between devices: 167 us -> none
    psum x6 -> x0, blocking collectives: 136 us -> none  [the longest x1 57.9 us: on_device(): lax.psum(contract('kaj,kab->jb', along_one, spread_two), ('wide', 'narrow'))]
    reduce_scatter x1 -> x0, waiting for transfers between devices: 67.9 us -> none  [on_device(): lax.psum_scatter(unfold_part, 'wide', scatter_dimension=1, tiled=True)]
    all_gather x2 -> x0, blocking collectives: 43.6 us -> none  [full_core(): whole = lax.all_gather(shares, ('wide', 'narrow'), axis=1, tiled=True)]
    all_to_all x0 -> x3, waiting for transfers between devices: none -> 31.9 us  [the longest x1 15.2 us: on_device(): lax.all_to_all(along.reshape(count, share * half * cols // 128, 128), gro...]
    ppermute x0 -> x14, waiting for transfers between devices: none -> 29.1 us  [the longest x12 28.2 us: total(): lax.ppermute(part, axis, [(at, at ^ step) for at in range(size)])]
    dot_general x17 -> x16, matrix products: 29.6 us -> 7 us  [the longest x13 6.33 us: contract(): return jnp.einsum(form, left, right, precision=precision)]
    all_to_all x0 -> x3, starting transfers between devices: none -> 17 us  [the longest x1 7.41 us: on_device(): got = lax.all_to_all(packed, group, 0, 0, tiled=True).reshape(count, full)]
  transfers between devices with their start and end apart: 4 -> 17, of which waited for: 4 -> 16; matrix products, arithmetic and copies ran while one was open for 0% -> 9% of each run, Pallas kernels for 0% -> 0%
where the time goes in v1:
time: 141 us
  waiting for transfers between devices  60.9 us (43%)
  starting transfers between devices  33.2 us (24%)
  other arithmetic  29 us (21%)
  local copies, waits for them, and re-layouts  8.72 us (6%)
  matrix products  7.83 us (6%)
    ppermute x12, waiting for transfers between devices, total(): lax.ppermute(part, axis, [(at, at ^ step) for at in range(size)])  28.2 us
    ppermute x12, starting transfers between devices, total(): lax.ppermute(part, axis, [(at, at ^ step) for at in range(size)])  15.6 us
    all_to_all x1, waiting for transfers between devices, on_device(): lax.all_to_all(along.reshape(count, share * half * cols // 128, 128), gro...  15.2 us
    another operation x9, other arithmetic, orthonormal(): lower = jnp.linalg.cholesky(gram)  15.2 us
    another operation x6, other arithmetic, orthonormal(): lax.linalg.triangular_solve(lower, product_t, left_side=True, lower=True)  13 us
    all_to_all x1, waiting for transfers between devices, on_device(): got = lax.all_to_all(packed, group, 0, 0, tiled=True).reshape(count, full)  10.8 us
    all_to_all x1, starting transfers between devices, on_device(): got = lax.all_to_all(packed, group, 0, 0, tiled=True).reshape(count, full)  7.41 us
    dot_general x13, matrix products, contract(): return jnp.einsum(form, left, right, precision=precision)  6.33 us
  transfers between devices with their start and end apart: 17, of which 16 were waited for; matrix products, arithmetic and copies ran while one was open for 9% of the time, Pallas kernels for 0%

profile of v1, /device:TPU:0, one launch (start us, length us, event | category | flops | bytes accessed | tf_op | source)
XLA Modules:
  0.0 140.8 jit_solution(18440317858961333171)
XLA Ops:
  0.7 0.8 constant_dynamic-slice_fusion.1
  2.1 2.0 %fusion.14 = f32[48,24,64]{2,0,1:T(8,128)S(1)} fusion(f32[24,64,256]{2,1,0:T(8,128)S(1)} %copy-done, f32[256,48]{0,1:T(8,128)} %param.7), kind=kOutput, calls=%fused_computation.26 | convolution fusion | flops 113246208 | bytes 1916928 | tf_op jit(solution)/shard_map/bj,kij->bki/dot_general | solution.py:12
  4.6 0.8 copy.52
  5.4 7.4 %all-to-all-start = ((f32[16,48,128]{2,1,0:T(8,128)}), f32[16,48,128]{2,1,0:T(8,128)S(1)}, u32[]{:S(2)}, u32[]{:S(2)}) async-start(f32[16,48,128]{2,1,0:T(8,128)} %bitcast.54), calls=%async_computation | async-start | bytes 786432 | tf_op jit(solution)/shard_map/all_to_all | solution.py:60
  13.3 0.9 collective-permute-done
  14.2 10.8 %all-to-all-done = f32[16,48,128]{2,1,0:T(8,128)S(1)} async-done(((f32[16,48,128]{2,1,0:T(8,128)}), f32[16,48,128]{2,1,0:T(8,128)S(1)}, u32[]{:S(2)}, u32[]{:S(2)}) %all-to-all-start) | async-done | bytes 393248 | tf_op jit(solution)/shard_map/all_to_all | solution.py:60
  26.4 1.1 collective-permute-done.1
  27.5 0.7 collective-permute-start.2
  28.2 3.2 %collective-permute-done.2 = f32[48,128]{1,0:T(8,128)S(1)} collective-permute-done((f32[48,128]{1,0:T(8,128)S(1)}, f32[48,128]{1,0:T(8,128)S(1)}, u32[]{:S(2)}, u32[]{:S(2)}) %collective-permute-start.2) | collective-permute-done | bytes 24608 | tf_op jit(solution)/shard_map/ppermute | solution.py:21
  31.4 0.9 collective-permute-start.3
  32.3 2.9 %collective-permute-done.3 = f32[48,128]{1,0:T(8,128)S(1)} collective-permute-done((f32[48,128]{1,0:T(8,128)S(1)}, f32[48,128]{1,0:T(8,128)S(1)}, u32[]{:S(2)}, u32[]{:S(2)}) %collective-permute-start.3) | collective-permute-done | bytes 24608 | tf_op jit(solution)/shard_map/ppermute | solution.py:21
  35.2 1.7 %collective-permute-start.4 = (f32[48,128]{1,0:T(8,128)S(1)}, f32[48,128]{1,0:T(8,128)S(1)}, u32[]{:S(2)}, u32[]{:S(2)}) collective-permute-start(f32[48,128]{1,0:T(8,128)S(1)} %add.73), channel_id=1, source_target_pairs={{0,8},{2,10},{4,12},{6,14},{8,0},{10,2},{12,4},{14,6},{1,9},{3,11}... | collective-permute-start | bytes 73736 | tf_op jit(solution)/shard_map/ppermute | solution.py:21
  37.1 2.9 %collective-permute-done.4 = f32[48,128]{1,0:T(8,128)S(1)} collective-permute-done((f32[48,128]{1,0:T(8,128)S(1)}, f32[48,128]{1,0:T(8,128)S(1)}, u32[]{:S(2)}, u32[]{:S(2)}) %collective-permute-start.4) | collective-permute-done | bytes 24608 | tf_op jit(solution)/shard_map/ppermute | solution.py:21
  40.2 4.4 %cholesky.59 = f32[48,48]{1,0:T(8,128)S(1)} custom-call(f32[48,48]{1,0:T(8,128)S(1)} %fusion.29), custom_call_target="Cholesky" | custom-call | tf_op jit(solution)/shard_map/jit(cholesky)/cholesky | solution.py:28
  44.6 0.6 compare_reduce_fusion.2
  45.2 0.7 fusion.16
  45.9 3.7 %custom-call.11 = f32[1,48,48]{1,2,0:T(8,128)S(1)} custom-call(f32[1,48,48]{2,1,0:T(8,128)S(1)} %fusion.16), custom_call_target="InvertDiagBlocksLowerTriangular" | custom-call | tf_op jit(solution)/shard_map/triangular_solve | solution.py:29
  51.1 0.9 reshape.68
  52.0 3.8 %all-to-all-start.1 = ((f32[16,72,128]{2,1,0:T(8,128)}), f32[16,72,128]{2,1,0:T(8,128)S(1)}, u32[]{:S(2)}, u32[]{:S(2)}) async-start(f32[16,72,128]{2,1,0:T(8,128)} %reshape.68), calls=%async_computation.1 | async-start | bytes 1179648 | tf_op jit(solution)/shard_map/all_to_all | solution.py:76
  55.9 15.2 %all-to-all-done.1 = f32[16,72,128]{2,1,0:T(8,128)S(1)} async-done(((f32[16,72,128]{2,1,0:T(8,128)}), f32[16,72,128]{2,1,0:T(8,128)S(1)}, u32[]{:S(2)}, u32[]{:S(2)}) %all-to-all-start.1) | async-done | bytes 589856 | tf_op jit(solution)/shard_map/all_to_all | solution.py:76
  72.4 1.0 collective-permute-done.6
  73.4 1.3 collective-permute-start.7
  74.7 2.9 %collective-permute-done.7 = f32[48,256]{1,0:T(8,128)S(1)} collective-permute-done((f32[48,256]{1,0:T(8,128)S(1)}, f32[48,256]{1,0:T(8,128)S(1)}, u32[]{:S(2)}, u32[]{:S(2)}) %collective-permute-start.7) | collective-permute-done | bytes 49184 | tf_op jit(solution)/shard_map/ppermute | solution.py:21
  77.6 1.9 %collective-permute-start.8 = (f32[48,256]{1,0:T(8,128)S(1)}, f32[48,256]{1,0:T(8,128)S(1)}, u32[]{:S(2)}, u32[]{:S(2)}) collective-permute-start(f32[48,256]{1,0:T(8,128)S(1)} %add.80), channel_id=1, source_target_pairs={{0,4},{2,6},{4,0},{6,2},{8,12},{10,14},{12,8},{14,10},{1,5},{3,7},... | collective-permute-start | bytes 147464 | tf_op jit(solution)/shard_map/ppermute | solution.py:21
  79.5 2.3 %collective-permute-done.8 = f32[48,256]{1,0:T(8,128)S(1)} collective-permute-done((f32[48,256]{1,0:T(8,128)S(1)}, f32[48,256]{1,0:T(8,128)S(1)}, u32[]{:S(2)}, u32[]{:S(2)}) %collective-permute-start.8) | collective-permute-done | bytes 49184 | tf_op jit(solution)/shard_map/ppermute | solution.py:21
  81.8 2.8 %collective-permute-start.9 = (f32[48,256]{1,0:T(8,128)S(1)}, f32[48,256]{1,0:T(8,128)S(1)}, u32[]{:S(2)}, u32[]{:S(2)}) collective-permute-start(f32[48,256]{1,0:T(8,128)S(1)} %add.81), channel_id=1, source_target_pairs={{0,8},{2,10},{4,12},{6,14},{8,0},{10,2},{12,4},{14,6},{1,9},{3,11}... | collective-permute-start | bytes 147464 | tf_op jit(solution)/shard_map/ppermute | solution.py:21
  84.7 2.2 %collective-permute-done.9 = f32[48,256]{1,0:T(8,128)S(1)} collective-permute-done((f32[48,256]{1,0:T(8,128)S(1)}, f32[48,256]{1,0:T(8,128)S(1)}, u32[]{:S(2)}, u32[]{:S(2)}) %collective-permute-start.9) | collective-permute-done | bytes 49184 | tf_op jit(solution)/shard_map/ppermute | solution.py:21
  87.1 4.4 %cholesky.70 = f32[48,48]{1,0:T(8,128)S(1)} custom-call(f32[48,48]{1,0:T(8,128)S(1)} %fusion.24), custom_call_target="Cholesky" | custom-call | tf_op jit(solution)/shard_map/jit(cholesky)/cholesky | solution.py:28
  91.5 0.6 compare_reduce_fusion.1
  92.2 0.7 fusion.17
  92.8 3.7 %custom-call.12 = f32[1,48,48]{1,2,0:T(8,128)S(1)} custom-call(f32[1,48,48]{2,1,0:T(8,128)S(1)} %fusion.17), custom_call_target="InvertDiagBlocksLowerTriangular" | custom-call | tf_op jit(solution)/shard_map/triangular_solve | solution.py:29
  98.2 1.3 collective-permute-done.10
  99.5 1.3 collective-permute-start.11
  100.8 3.7 %collective-permute-done.11 = f32[48,192]{0,1:T(8,128)S(1)} collective-permute-done((f32[48,192]{0,1:T(8,128)S(1)}, f32[48,192]{0,1:T(8,128)S(1)}, u32[]{:S(2)}, u32[]{:S(2)}) %collective-permute-start.11) | collective-permute-done | bytes 36896 | tf_op jit(solution)/shard_map/ppermute | solution.py:21
  104.5 1.9 %collective-permute-start.12 = (f32[48,192]{0,1:T(8,128)S(1)}, f32[48,192]{0,1:T(8,128)S(1)}, u32[]{:S(2)}, u32[]{:S(2)}) collective-permute-start(f32[48,192]{0,1:T(8,128)S(1)} %add.84), channel_id=1, source_target_pairs={{0,4},{2,6},{4,0},{6,2},{8,12},{10,14},{12,8},{14,10},{1,5},{3,7},... | collective-permute-start | bytes 110600 | tf_op jit(solution)/shard_map/ppermute | solution.py:21
  106.3 2.8 %collective-permute-done.12 = f32[48,192]{0,1:T(8,128)S(1)} collective-permute-done((f32[48,192]{0,1:T(8,128)S(1)}, f32[48,192]{0,1:T(8,128)S(1)}, u32[]{:S(2)}, u32[]{:S(2)}) %collective-permute-start.12) | collective-permute-done | bytes 36896 | tf_op jit(solution)/shard_map/ppermute | solution.py:21
  109.2 2.8 %collective-permute-start.13 = (f32[48,192]{0,1:T(8,128)S(1)}, f32[48,192]{0,1:T(8,128)S(1)}, u32[]{:S(2)}, u32[]{:S(2)}) collective-permute-start(f32[48,192]{0,1:T(8,128)S(1)} %add.85), channel_id=1, source_target_pairs={{0,8},{2,10},{4,12},{6,14},{8,0},{10,2},{12,4},{14,6},{1,9},{3,11}... | collective-permute-start | bytes 110600 | tf_op jit(solution)/shard_map/ppermute | solution.py:21
  111.9 0.7 dynamic-slice_bitcast_fusion.1
  112.6 2.1 %collective-permute-done.13 = f32[48,192]{0,1:T(8,128)S(1)} collective-permute-done((f32[48,192]{0,1:T(8,128)S(1)}, f32[48,192]{0,1:T(8,128)S(1)}, u32[]{:S(2)}, u32[]{:S(2)}) %collective-permute-start.13) | collective-permute-done | bytes 36896 | tf_op jit(solution)/shard_map/ppermute | solution.py:21
  115.2 4.4 %cholesky.81 = f32[48,48]{1,0:T(8,128)S(1)} custom-call(f32[48,48]{1,0:T(8,128)S(1)} %fusion.21), custom_call_target="Cholesky" | custom-call | tf_op jit(solution)/shard_map/jit(cholesky)/cholesky | solution.py:28
  120.2 0.7 fusion.18
  120.9 3.7 %custom-call.13 = f32[1,48,48]{1,2,0:T(8,128)S(1)} custom-call(f32[1,48,48]{2,1,0:T(8,128)S(1)} %fusion.18), custom_call_target="InvertDiagBlocksLowerTriangular" | custom-call | tf_op jit(solution)/shard_map/triangular_solve | solution.py:29
  125.6 0.7 reshape.96
  126.4 5.8 %all-to-all-start.2 = ((f32[16,1,432]{2,1,0:T(1,128)}), f32[16,1,432]{2,1,0:T(1,128)S(1)}, u32[]{:S(2)}, u32[]{:S(2)}) async-start(f32[16,1,432]{2,1,0:T(1,128)} %reshape.96), calls=%async_computation.2 | async-start | bytes 65536 | tf_op jit(solution)/shard_map/all_to_all | solution.py:93
  132.2 0.7 copy.30
  132.9 5.9 %all-to-all-done.2 = f32[16,1,432]{2,1,0:T(1,128)S(1)} async-done(((f32[16,1,432]{2,1,0:T(1,128)}), f32[16,1,432]{2,1,0:T(1,128)S(1)}, u32[]{:S(2)}, u32[]{:S(2)}) %all-to-all-start.2) | async-done | bytes 27680 | tf_op jit(solution)/shard_map/all_to_all | solution.py:93
  139.3 0.7 reduce.4
  140.1 0.6 reshape.73
  (81 shorter events, 11.2 us)
Async XLA Ops:
  0.6 1.4 %copy-start = (f32[24,64,256]{2,1,0:T(8,128)S(1)}, f32[24,64,256]{2,1,0:T(8,128)}, u32[]{:S(2)}) copy-start(f32[24,64,256]{2,1,0:T(8,128)} %param.5) | copy-start | bytes 4718596
  4.5 8.3 %copy-start.3 = (f32[64,48]{0,1:T(8,128)S(1)}, f32[64,48]{0,1:T(8,128)}, u32[]{:S(2)}) copy-start(f32[64,48]{0,1:T(8,128)} %param.6) | copy-start | bytes 36868
  5.4 19.6 %all-to-all-start = ((f32[16,48,128]{2,1,0:T(8,128)}), f32[16,48,128]{2,1,0:T(8,128)S(1)}, u32[]{:S(2)}, u32[]{:S(2)}) async-start(f32[16,48,128]{2,1,0:T(8,128)} %bitcast.54), calls=%async_computation | async-start | bytes 786432 | tf_op jit(solution)/shard_map/all_to_all | solution.py:60
  12.8 1.3 collective-permute-start
  26.3 1.2 collective-permute-start.1
  27.5 3.8 %collective-permute-start.2 = (f32[48,128]{1,0:T(8,128)S(1)}, f32[48,128]{1,0:T(8,128)S(1)}, u32[]{:S(2)}, u32[]{:S(2)}) collective-permute-start(f32[48,128]{1,0:T(8,128)S(1)} %add.71), channel_id=1, source_target_pairs={{0,2},{2,0},{4,6},{6,4},{8,10},{10,8},{12,14},{14,12},{1,3},{3,1},... | collective-permute-start | bytes 73736 | tf_op jit(solution)/shard_map/ppermute | solution.py:21
  31.4 3.8 %collective-permute-start.3 = (f32[48,128]{1,0:T(8,128)S(1)}, f32[48,128]{1,0:T(8,128)S(1)}, u32[]{:S(2)}, u32[]{:S(2)}) collective-permute-start(f32[48,128]{1,0:T(8,128)S(1)} %add.72), channel_id=1, source_target_pairs={{0,4},{2,6},{4,0},{6,2},{8,12},{10,14},{12,8},{14,10},{1,5},{3,7},... | collective-permute-start | bytes 73736 | tf_op jit(solution)/shard_map/ppermute | solution.py:21
  35.2 4.7 %collective-permute-start.4 = (f32[48,128]{1,0:T(8,128)S(1)}, f32[48,128]{1,0:T(8,128)S(1)}, u32[]{:S(2)}, u32[]{:S(2)}) collective-permute-start(f32[48,128]{1,0:T(8,128)S(1)} %add.73), channel_id=1, source_target_pairs={{0,8},{2,10},{4,12},{6,14},{8,0},{10,2},{12,4},{14,6},{1,9},{3,11}... | collective-permute-start | bytes 73736 | tf_op jit(solution)/shard_map/ppermute | solution.py:21
  37.0 13.3 %collective-permute-start.5 = (f32[12,64,256]{2,1,0:T(8,128)S(1)}, f32[12,64,256]{2,1,0:T(8,128)S(1)}, u32[]{:S(2)}, u32[]{:S(2)}) collective-permute-start(f32[12,64,256]{2,1,0:T(8,128)S(1)} %constant_dynamic-slice_fusion), channel_id=1, source_target_pairs={{0,1},{1,0},{2,3},{3,2},{4,5},{5,4},{6,7},{7,6},{8,9},{9,8},{10,11... | collective-permute-start | bytes 2359304 | tf_op jit(solution)/shard_map/ppermute | solution.py:33
  52.0 19.1 %all-to-all-start.1 = ((f32[16,72,128]{2,1,0:T(8,128)}), f32[16,72,128]{2,1,0:T(8,128)S(1)}, u32[]{:S(2)}, u32[]{:S(2)}) async-start(f32[16,72,128]{2,1,0:T(8,128)} %reshape.68), calls=%async_computation.1 | async-start | bytes 1179648 | tf_op jit(solution)/shard_map/all_to_all | solution.py:76
  55.8 15.8 %copy-start.2 = (f32[256,48]{0,1:T(8,128)S(1)}, f32[256,48]{0,1:T(8,128)}, u32[]{:S(2)}) copy-start(f32[256,48]{0,1:T(8,128)} %param.7) | copy-start | bytes 147460
  72.1 1.3 collective-permute-start.6
  73.4 4.2 %collective-permute-start.7 = (f32[48,256]{1,0:T(8,128)S(1)}, f32[48,256]{1,0:T(8,128)S(1)}, u32[]{:S(2)}, u32[]{:S(2)}) collective-permute-start(f32[48,256]{1,0:T(8,128)S(1)} %add.79), channel_id=1, source_target_pairs={{0,2},{2,0},{4,6},{6,4},{8,10},{10,8},{12,14},{14,12},{1,3},{3,1},... | collective-permute-start | bytes 147464 | tf_op jit(solution)/shard_map/ppermute | solution.py:21
  77.6 4.2 %collective-permute-start.8 = (f32[48,256]{1,0:T(8,128)S(1)}, f32[48,256]{1,0:T(8,128)S(1)}, u32[]{:S(2)}, u32[]{:S(2)}) collective-permute-start(f32[48,256]{1,0:T(8,128)S(1)} %add.80), channel_id=1, source_target_pairs={{0,4},{2,6},{4,0},{6,2},{8,12},{10,14},{12,8},{14,10},{1,5},{3,7},... | collective-permute-start | bytes 147464 | tf_op jit(solution)/shard_map/ppermute | solution.py:21
  81.8 5.1 %collective-permute-start.9 = (f32[48,256]{1,0:T(8,128)S(1)}, f32[48,256]{1,0:T(8,128)S(1)}, u32[]{:S(2)}, u32[]{:S(2)}) collective-permute-start(f32[48,256]{1,0:T(8,128)S(1)} %add.81), channel_id=1, source_target_pairs={{0,8},{2,10},{4,12},{6,14},{8,0},{10,2},{12,4},{14,6},{1,9},{3,11}... | collective-permute-start | bytes 147464 | tf_op jit(solution)/shard_map/ppermute | solution.py:21
  96.8 7.7 %copy-start.1 = (f32[48,256]{1,0:T(8,128)}, f32[48,256]{1,0:T(8,128)S(1)}, u32[]{:S(2)}) copy-start(f32[48,256]{1,0:T(8,128)S(1)} %fusion.22) | copy-start | bytes 147460
  98.1 1.4 collective-permute-start.10
  99.5 4.9 %collective-permute-start.11 = (f32[48,192]{0,1:T(8,128)S(1)}, f32[48,192]{0,1:T(8,128)S(1)}, u32[]{:S(2)}, u32[]{:S(2)}) collective-permute-start(f32[48,192]{0,1:T(8,128)S(1)} %add.83), channel_id=1, source_target_pairs={{0,2},{2,0},{4,6},{6,4},{8,10},{10,8},{12,14},{14,12},{1,3},{3,1},... | collective-permute-start | bytes 110600 | tf_op jit(solution)/shard_map/ppermute | solution.py:21
  104.5 4.7 %collective-permute-start.12 = (f32[48,192]{0,1:T(8,128)S(1)}, f32[48,192]{0,1:T(8,128)S(1)}, u32[]{:S(2)}, u32[]{:S(2)}) collective-permute-start(f32[48,192]{0,1:T(8,128)S(1)} %add.84), channel_id=1, source_target_pairs={{0,4},{2,6},{4,0},{6,2},{8,12},{10,14},{12,8},{14,10},{1,5},{3,7},... | collective-permute-start | bytes 110600 | tf_op jit(solution)/shard_map/ppermute | solution.py:21
  109.2 5.6 %collective-permute-start.13 = (f32[48,192]{0,1:T(8,128)S(1)}, f32[48,192]{0,1:T(8,128)S(1)}, u32[]{:S(2)}, u32[]{:S(2)}) collective-permute-start(f32[48,192]{0,1:T(8,128)S(1)} %add.85), channel_id=1, source_target_pairs={{0,8},{2,10},{4,12},{6,14},{8,0},{10,2},{12,4},{14,6},{1,9},{3,11}... | collective-permute-start | bytes 110600 | tf_op jit(solution)/shard_map/ppermute | solution.py:21
  126.4 12.4 %all-to-all-start.2 = ((f32[16,1,432]{2,1,0:T(1,128)}), f32[16,1,432]{2,1,0:T(1,128)S(1)}, u32[]{:S(2)}, u32[]{:S(2)}) async-start(f32[16,1,432]{2,1,0:T(1,128)} %reshape.96), calls=%async_computation.2 | async-start | bytes 65536 | tf_op jit(solution)/shard_map/all_to_all | solution.py:93

commit v2 on v1

--- a/solution.py
+++ b/solution.py
@@ -1,11 +1,17 @@
 import jax
 import jax.numpy as jnp
 from jax import lax
+from jax.experimental import pallas as pl
+from jax.experimental.pallas import tpu as pltpu
 from jax.sharding import PartitionSpec as P
 
 highest = lax.Precision.HIGHEST
 fine = lax.Precision.HIGH
 group = ("wide", "narrow")
+lanes = 128
+nn = (((1,), (0,)), ((), ()))
+nt = (((1,), (1,)), ((), ()))
+tn = (((0,), (0,)), ((), ()))
 
 
 def contract(form, left, right, precision=fine):
@@ -23,17 +29,80 @@
     return part
 
 
-def orthonormal(product_t):
-    gram = jnp.einsum("an,bn->ab", product_t, product_t, precision=highest)
-    lower = jnp.linalg.cholesky(gram)
-    return lax.linalg.triangular_solve(lower, product_t, left_side=True, lower=True)
-
-
 def swap(value):
     return lax.ppermute(value, "narrow", [(0, 1), (1, 0)])
 
 
-def on_device(window_data, factor_one, factor_two, factor_three):
+def dot(left, right, dims=nn):
+    return lax.dot_general(
+        left, right, dims, precision=highest, preferred_element_type=jnp.float32
+    )
+
+
+def split(value):
+    high = value.astype(jnp.bfloat16)
+    return high, (value - high.astype(jnp.float32)).astype(jnp.bfloat16)
+
+
+def dot3(left, right, dims=nn):
+    left_high, left_low = left if isinstance(left, tuple) else split(left)
+    right_high, right_low = right if isinstance(right, tuple) else split(right)
+
+    def one(a, b):
+        return lax.dot_general(a, b, dims, preferred_element_type=jnp.float32)
+
+    return one(left_high, right_high) + (one(left_high, right_low) + one(left_low, right_high))
+
+
+def eliminate(table, rank):
+    width = table.shape[1]
+    row = lax.broadcasted_iota(jnp.int32, (8, width), 0)
+    tiles = [table[8 * at : 8 * at + 8] for at in range(rank // 8)]
+    for at in range(rank // 8):
+        live = tiles[at:]
+        columns = [
+            [jnp.broadcast_to(x[:, 8 * at + k : 8 * at + k + 1], (8, width)) for x in live]
+            for k in range(8)
+        ]
+        for j in range(8):
+            heads = [jnp.broadcast_to(columns[k][0][j : j + 1], (8, width)) for k in range(j, 8)]
+            inverse = 1.0 / heads[0]
+            scale = [x * inverse for x in columns[j]]
+            scale[0] = jnp.where(row > j, scale[0], 0.0)
+            for k in range(j + 1, 8):
+                columns[k] = [x - y * heads[k - j] for x, y in zip(columns[k], scale)]
+            lead = jnp.broadcast_to(live[0][j : j + 1], (8, width))
+            live = [x - y * lead for x, y in zip(live, scale)]
+        tiles[at:] = live
+    return jnp.concatenate(tiles, axis=0)
+
+
+def orthonormal(part):
+    rank, size = part.shape
+    width = -(-2 * rank // lanes) * lanes
+    below = jnp.zeros((width - rank, size), part.dtype)
+    gram = dot(part, jnp.concatenate([part, below]), nt)
+    row = lax.broadcasted_iota(jnp.int32, (rank, width), 0)
+    lane = lax.broadcasted_iota(jnp.int32, (rank, width), 1)
+    table = eliminate(jnp.where(lane == row + rank, 1.0, gram), rank)
+    pivots = jnp.sum(jnp.where(lane == row, table, 0.0), axis=1, keepdims=True)
+    table = jnp.where(lane < rank, 0.0, table * lax.rsqrt(pivots))
+    padded = [jnp.zeros((rank, size), part.dtype), part]
+    if width > 2 * rank:
+        padded.append(jnp.zeros((width - 2 * rank, size), part.dtype))
+    return dot(table, jnp.concatenate(padded))
+
+
+def orthonormal_body(part, out):
+    out[...] = orthonormal(part[...])
+
+
+def call(body, shapes, *operands, **settings):
+    shapes = [jax.ShapeDtypeStruct(shape, jnp.float32) for shape in shapes]
+    return pl.pallas_call(body, out_shape=shapes, **settings)(*operands)
+
+
+def general(window_data, factor_one, factor_two, factor_three):
     wide = lax.axis_size("wide")
     narrow = lax.axis_size("narrow")
     count = wide * narrow
@@ -67,7 +136,7 @@
     weights = contract("bcni,nia->bca", unfold, one)
     product = contract("bcni,bca->ani", unfold, weights).reshape(rank, narrow * rows)
     product = total(total(product, "narrow"), "wide")
-    one_t = orthonormal(product)
+    one_t = call(orthonormal_body, [product.shape], product)[0]
 
     one_pad = jnp.pad(one_t, ((0, spare), (0, 0)))
     one_own = lax.dynamic_slice_in_dim(one_pad, core_at * rows, rows, 1)
@@ -81,19 +150,262 @@
     weights = contract("acj,jb->acb", unfold, factor_two)
     product = contract("acj,acb->bj", unfold, weights)
     product = total(total(product, "narrow"), "wide")
-    two_t = orthonormal(product)
+    two_t = call(orthonormal_body, [product.shape], product)[0]
 
     unfold = contract("dakj,bj->dakb", got, two_t)
     weights = contract("dakb,dkc->abc", unfold, three)
     product = contract("dakb,abc->cdk", unfold, weights).reshape(rank, count * half)
     product = total(total(product, "narrow"), "wide")
-    three_t = orthonormal(product)
+    three_t = call(orthonormal_body, [product.shape], product)[0]
     core = contract("dakb,cdk->abc", unfold, three_t.reshape(rank, count, half))
     core = core.reshape(share, count, rank * rank // count).transpose(1, 0, 2)
     core = lax.all_to_all(core, group, 0, 0, tiled=True)
     core = core.reshape(count * share, rank * rank // count)[:rank]
     basis_three = lax.dynamic_slice_in_dim(three_t, lax.axis_index("wide") * depth, depth, 1).T
     return (one_own[:rank].T, two_t.T, basis_three, core)
+
+
+def pack_one(field, two, three, out, *, share, half, count):
+    at = pl.program_id(0)
+    steps, rows, cols = field.shape[1:]
+    rank = two.shape[0]
+    slots = share + 1
+    two_high, two_low = split(two[...])
+    both = jnp.concatenate([two_high, two_low])
+    for q in range(steps):
+        high, low = split(field[:, q].reshape(2 * rows, cols))
+        first = lax.dot_general(both, high, nt, preferred_element_type=jnp.float32)
+        second = lax.dot_general(two_high, low, nt, preferred_element_type=jnp.float32)
+        along = first[:rank] + (first[rank:] + second)
+        for s in range(share):
+            start = (at * steps + q) * slots + s
+            out[pl.ds(start, count, stride=half * slots), :] = along[s * count : (s + 1) * count]
+
+    @pl.when(at == 0)
+    def _():
+        first = three[:half]
+        second = three[half:]
+        room = jnp.zeros((half, lanes // 2 - rank), jnp.float32)
+        both = jnp.concatenate([first, room, second, room], axis=1)
+        for d in range(count):
+            out[pl.ds(d * half * slots + share, half, stride=slots), :] = both
+
+
+def work_one(got, own, other, out, three, *, share, half, count):
+    rank = own.shape[1]
+    slots = share + 1
+    size = count * half
+    at = lax.axis_index("narrow")
+    low = jnp.where(at == 0, own[...], other[...])
+    high = jnp.where(at == 0, other[...], own[...])
+    one = jnp.concatenate([low, high])
+    table = got[pl.ds(share, size, stride=slots), :]
+    row = lax.broadcasted_iota(jnp.int32, (size, lanes), 0)
+    odd = (row // half) % 2 == 1
+    part = lanes // 2
+    three[...] = jnp.where(odd, pltpu.roll(table, part, 1), table)[:, :rank]
+    table = jnp.concatenate([jnp.where(odd, 0.0, table), jnp.where(odd, table, 0.0)], axis=1)
+    table = split(table)
+    lane = lax.broadcasted_iota(jnp.int32, (rank, lanes), 1)
+    pieces = []
+    for s in range(share):
+        value = dot3(table, got[pl.ds(s, size, stride=slots), :], tn)
+        first = value[:rank] + pltpu.roll(value[part : part + rank], part, 1)
+        second = (
+            pltpu.roll(value[2 * part : 2 * part + rank], part, 1)
+            + value[3 * part : 3 * part + rank]
+        )
+        pieces.append(jnp.where(lane < part, first, second))
+    unfold = split(jnp.concatenate(pieces))
+    out[...] = dot3(dot3(unfold, one), unfold, tn)
+
+
+def pack_two(part, own, other, basis, out, *, share, half, count):
+    rows, cols = own.shape[1:]
+    value = orthonormal(part[...])
+    basis[...] = value
+    slots = share * (cols // lanes)
+    at = lax.axis_index("narrow")
+    value = split(jnp.where(at == 0, value, pltpu.roll(value, rows, 1)))
+    both = jnp.concatenate(value)
+    rank = part.shape[0]
+    for k in range(half):
+        high, low = split(jnp.concatenate([own[k], other[k]]))
+        first = lax.dot_general(both, high, nn, preferred_element_type=jnp.float32)
+        second = lax.dot_general(value[0], low, nn, preferred_element_type=jnp.float32)
+        along = first[:rank] + (first[rank:] + second)
+        for s in range(share):
+            for h in range(cols // lanes):
+                start = k * slots + s * (cols // lanes) + h
+                out[pl.ds(start, count, stride=half * slots), :] = along[
+                    s * count : (s + 1) * count, h * lanes : (h + 1) * lanes
+                ]
+
+
+def taken(got, s, parts, slots, size):
+    return jnp.concatenate(
+        [got[pl.ds(s * parts + h, size, stride=slots), :] for h in range(parts)], axis=1
+    )
+
+
+def work_two(got, two, three, out, *, share, half, count):
+    parts = two.shape[0] // lanes
+    size = count * half
+    table = split(three[...])
+    unfold = split(
+        jnp.concatenate(
+            [
+                dot3(table, taken(got, s, parts, share * parts, size), tn)
+                for s in range(share)
+            ]
+        )
+    )
+    out[...] = dot3(dot3(unfold, two[...]), unfold, tn)
+
+
+def work_three(part, got, three, basis, out, sent, room, *, share, half, count):
+    rank, cols = part.shape
+    parts = cols // lanes
+    size = count * half
+    tall = -(-size // lanes)
+    pitch = sent.shape[0] // count
+    value = orthonormal(part[...])
+    basis[...] = value
+    for h in range(parts):
+        room[h * rank : (h + 1) * rank, :] = value[:, h * lanes : (h + 1) * lanes]
+    second = split(
+        jnp.concatenate(
+            [
+                jnp.concatenate(
+                    [room[pl.ds(h * rank + b, count, stride=share), :] for h in range(parts)],
+                    axis=1,
+                )
+                for b in range(share)
+            ]
+        )
+    )
+    table = split(three[...])
+    result = None
+    for s in range(share):
+        value = dot3(second, taken(got, s, parts, share * parts, size), nt)
+        for b in range(share):
+            for h in range(tall):
+                wide = min(lanes, size - h * lanes)
+                start = (b * share + s) * tall + h
+                sent[pl.ds(start, count, stride=pitch), :wide] = value[
+                    b * count : (b + 1) * count, h * lanes : h * lanes + wide
+                ]
+        value = split(value)
+        term = dot3(dot3(value, table), value, tn)
+        result = term if result is None else result + term
+    out[...] = result
+
+
+def finish(part, got, basis, core, *, share, half, count):
+    rank, size = part.shape
+    tall = -(-size // lanes)
+    pitch = got.shape[0] // count
+    value = orthonormal(part[...])
+    basis[...] = value
+    value = split(value)
+    for b in range(share):
+        rows = []
+        for s in range(share):
+            pieces = []
+            for h in range(tall):
+                wide = min(lanes, size - h * lanes)
+                start = (b * share + s) * tall + h
+                pieces.append(got[pl.ds(start, count, stride=pitch), :][:, :wide])
+            rows.append(jnp.concatenate(pieces, axis=1))
+        core[:, b * rank : (b + 1) * rank] = dot3(jnp.concatenate(rows), value, nt)
+
+
+def exchange(value, count):
+    rows = value.shape[0]
+    value = value.reshape(count, rows // count, lanes)
+    return lax.all_to_all(value, group, 0, 0, tiled=True).reshape(rows, lanes)
+
+
+def special(window_data, factor_one, factor_two, factor_three):
+    wide = lax.axis_size("wide")
+    count = wide * lax.axis_size("narrow")
+    depth, rows, cols = window_data.shape
+    rank = factor_one.shape[1]
+    share = rank // count
+    half = depth // 2
+    size = count * half
+    facts = {"share": share, "half": half, "count": count}
+    core_at = lax.axis_index("narrow")
+
+    def stage(body):
+        def run(*refs):
+            body(*refs, **facts)
+
+        run.__name__ = body.__name__
+        return run
+
+    steps = 3 if half % 3 == 0 else 1
+    slots = share + 1
+    packed = pl.pallas_call(
+        stage(pack_one),
+        grid=(steps,),
+        in_specs=[
+            pl.BlockSpec((2, half // steps, rows, cols), lambda at: (0, at, 0, 0)),
+            pl.BlockSpec((rank, cols), lambda at: (0, 0)),
+            pl.BlockSpec((depth, rank), lambda at: (0, 0)),
+        ],
+        out_specs=pl.BlockSpec((size * slots, lanes), lambda at: (0, 0)),
+        out_shape=jax.ShapeDtypeStruct((size * slots, lanes), jnp.float32),
+    )(window_data.reshape(2, half, rows, cols), factor_two.T, factor_three)
+    got = exchange(packed, count)
+    own = lax.dynamic_slice_in_dim(window_data, core_at * half, half, 0)
+    other = swap(lax.dynamic_slice_in_dim(window_data, (1 - core_at) * half, half, 0))
+    product, three = call(
+        stage(work_one), [(rank, 2 * rows), (size, rank)], got, factor_one, swap(factor_one)
+    )
+    product = total(total(product, "narrow"), "wide")
+
+    parts = cols // lanes
+    one_t, packed = call(
+        stage(pack_two), [product.shape, (size * share * parts, lanes)], product, own, other
+    )
+    got = exchange(packed, count)
+    (product,) = call(stage(work_two), [(rank, cols)], got, factor_two, three)
+    product = total(total(product, "narrow"), "wide")
+
+    pitch = -(-share * share * -(-size // lanes) // 8) * 8
+    two_t, product, sent = call(
+        stage(work_three),
+        [product.shape, (rank, size), (count * pitch, lanes)],
+        product,
+        got,
+        three,
+        scratch_shapes=[pltpu.VMEM((parts * rank, lanes), jnp.float32)],
+    )
+    got = exchange(sent, count)
+    product = total(total(product, "narrow"), "wide")
+    three_t, core = call(stage(finish), [product.shape, (rank, share * rank)], product, got)
+    basis_one = lax.dynamic_slice_in_dim(one_t, core_at * rows, rows, 1).T
+    basis_three = lax.dynamic_slice_in_dim(three_t, lax.axis_index("wide") * depth, depth, 1).T
+    return (basis_one, two_t.T, basis_three, core)
+
+
+def on_device(window_data, factor_one, factor_two, factor_three):
+    count = lax.axis_size("wide") * lax.axis_size("narrow")
+    depth, rows, cols = window_data.shape
+    rank = factor_one.shape[1]
+    fits = (
+        lax.axis_size("narrow") == 2
+        and rank % count == 0
+        and count % 8 == 0
+        and depth % 2 == 0
+        and (depth // 2) * (rank // count + 1) % 8 == 0
+        and (depth // 2) * (rank // count) * (cols // lanes) % 8 == 0
+        and 2 * rows == lanes
+        and 2 * rank <= lanes
+        and cols % lanes == 0
+    )
+    return (special if fits else general)(window_data, factor_one, factor_two, factor_three)
 
 
 def solution(mesh):

time: 141 us -> 120 us (0.85)
  other arithmetic: 29 us -> 4.25 us
  Pallas kernels: 0 us -> 21.7 us
  waiting for transfers between devices: 60.9 us -> 50.9 us
  matrix products: 7.83 us -> 0 us
    another operation x16 -> x0, other arithmetic: 28.1 us -> none  [the longest x9 15.2 us: orthonormal(): lower = jnp.linalg.cholesky(gram)]
    pallas_call x0 -> x6, Pallas kernels: none -> 21.7 us  [the longest x5 18.1 us: call(): return pl.pallas_call(body, out_shape=shapes, **settings)(*operands)]
    all_to_all x3, waiting for transfers between devices: 31.9 us -> 23.3 us  [exchange(): return lax.all_to_all(value, group, 0, 0, tiled=True).reshape(rows, lanes)]
    dot_general x16 -> x0, matrix products: 7 us -> none  [the longest x13 6.33 us: contract(): return jnp.einsum(form, left, right, precision=precision)]
    add x12, other arithmetic: 0.1 us -> 4.25 us  [total(): part + lax.ppermute(part, axis, [(at, at ^ step) for at in range(size)])]
    ppermute x12, waiting for transfers between devices: 28.2 us -> 25.9 us  [total(): lax.ppermute(part, axis, [(at, at ^ step) for at in range(size)])]
    reshape x10 -> x0, local copies, waits for them, and re-layouts: 2.18 us -> none  [the longest x1 0.9 us: on_device(): along.reshape(count, share * half * cols // 128, 128)]
    unnamed x14 -> x23, local copies, waits for them, and re-layouts: 3.01 us -> 4.72 us
  transfers between devices with their start and end apart: 17 -> 17, of which waited for: 16 -> 15; matrix products, arithmetic and copies ran while one was open for 9% -> 5% of each run, Pallas kernels for 0% -> 2%
where the time goes in v2:
time: 120 us; the launch traced here: 119 us
  waiting for transfers between devices  50.9 us (42%)
  starting transfers between devices  33.9 us (28%)
  Pallas kernels  21.7 us (18%)
  local copies, waits for them, and re-layouts  7.33 us (6%)
  other arithmetic  4.25 us (4%)
    ppermute x12, waiting for transfers between devices, total(): lax.ppermute(part, axis, [(at, at ^ step) for at in range(size)])  25.9 us
    all_to_all x3, waiting for transfers between devices, exchange(): return lax.all_to_all(value, group, 0, 0, tiled=True).reshape(rows, lanes)  23.3 us
    pallas_call x5, Pallas kernels, call(): return pl.pallas_call(body, out_shape=shapes, **settings)(*operands)  18.1 us
    ppermute x12, starting transfers between devices, total(): lax.ppermute(part, axis, [(at, at ^ step) for at in range(size)])  17.2 us
    all_to_all x3, starting transfers between devices, exchange(): return lax.all_to_all(value, group, 0, 0, tiled=True).reshape(rows, lanes)  16.1 us
    unnamed x23, local copies, waits for them, and re-layouts  4.72 us
    add x12, other arithmetic, total(): part + lax.ppermute(part, axis, [(at, at ^ step) for at in range(size)])  4.25 us
    pallas_call x1, Pallas kernels, special(): pl.pallas_call(stage(pack_one), grid=(steps,), in_specs=[pl.BlockSpec((2,...  3.62 us
  transfers between devices with their start and end apart: 17, of which 15 were waited for; matrix products, arithmetic and copies ran while one was open for 5% of the time, Pallas kernels for 2%

profile of v2, /device:TPU:0, one launch (start us, length us, event | category | flops | bytes accessed | tf_op | source)
XLA Modules:
  0.0 118.8 jit_solution(8763218819154882894)
XLA Ops:
  0.6 3.6 %shard_map.75 = f32[768,128]{1,0:T(8,128)} custom-call(f32[2,12,64,256]{3,2,1,0:T(8,128)} %bitcast.13, f32[48,256]{1,0:T(8,128)} %bitcast.21, f32[24,48]{1,0:T(8,128)} %refs_2_.1), custom_call_target="tpu_custom_call" | custom-call | tf_op jit(solution)/shard_map/pallas_call | solution.py:349
  4.3 7.4 %all-to-all-start = ((f32[16,48,128]{2,1,0:T(8,128)}), f32[16,48,128]{2,1,0:T(8,128)S(1)}, u32[]{:S(2)}, u32[]{:S(2)}) async-start(f32[16,48,128]{2,1,0:T(8,128)} %bitcast.17), calls=%async_computation | async-start | bytes 786432 | tf_op jit(solution)/shard_map/all_to_all | solution.py:326
  11.7 1.1 constant_dynamic-slice_fusion
  13.4 1.7 %collective-permute-done.refs_2_ = f32[64,48]{1,0:T(8,128)S(1)} collective-permute-done((f32[64,48]{1,0:T(8,128)S(1)}, f32[64,48]{1,0:T(8,128)S(1)}, u32[]{:S(2)}, u32[]{:S(2)}) %collective-permute-start) | collective-permute-done | bytes 12320 | tf_op jit(solution)/shard_map/ppermute | solution.py:33
  15.1 8.7 %all-to-all-done = f32[16,48,128]{2,1,0:T(8,128)S(1)} async-done(((f32[16,48,128]{2,1,0:T(8,128)}), f32[16,48,128]{2,1,0:T(8,128)S(1)}, u32[]{:S(2)}, u32[]{:S(2)}) %all-to-all-start) | async-done | bytes 393248 | tf_op jit(solution)/shard_map/all_to_all | solution.py:326
  23.9 0.8 copy-done.2
  24.6 2.7 %shard_map.76 = (f32[48,128]{1,0:T(8,128)}, f32[192,48]{1,0:T(8,128)}) custom-call(f32[768,128]{1,0:T(8,128)} %bitcast.16, f32[64,48]{1,0:T(8,128)} %copy-done.6, f32[64,48]{1,0:T(8,128)} %copy-done.7), custom_call_target="tpu_custom_call" | custom-call | tf_op jit(solution)/shard_map/pallas_call | solution.py:102
  27.5 1.3 %collective-permute-done.1 = f32[48,128]{1,0:T(8,128)S(1)} collective-permute-done((f32[48,128]{1,0:T(8,128)}, f32[48,128]{1,0:T(8,128)S(1)}, u32[]{:S(2)}, u32[]{:S(2)}) %collective-permute-start.1) | collective-permute-done | bytes 24608 | tf_op jit(solution)/shard_map/ppermute | solution.py:27
  28.8 0.7 add.48
  29.5 0.7 collective-permute-start.2
  30.2 3.2 %collective-permute-done.2 = f32[48,128]{1,0:T(8,128)S(1)} collective-permute-done((f32[48,128]{1,0:T(8,128)S(1)}, f32[48,128]{1,0:T(8,128)S(1)}, u32[]{:S(2)}, u32[]{:S(2)}) %collective-permute-start.2) | collective-permute-done | bytes 24608 | tf_op jit(solution)/shard_map/ppermute | solution.py:27
  33.4 0.9 collective-permute-start.3
  34.3 2.9 %collective-permute-done.3 = f32[48,128]{1,0:T(8,128)S(1)} collective-permute-done((f32[48,128]{1,0:T(8,128)S(1)}, f32[48,128]{1,0:T(8,128)S(1)}, u32[]{:S(2)}, u32[]{:S(2)}) %collective-permute-start.3) | collective-permute-done | bytes 24608 | tf_op jit(solution)/shard_map/ppermute | solution.py:27
  37.2 1.7 %collective-permute-start.4 = (f32[48,128]{1,0:T(8,128)S(1)}, f32[48,128]{1,0:T(8,128)S(1)}, u32[]{:S(2)}, u32[]{:S(2)}) collective-permute-start(f32[48,128]{1,0:T(8,128)S(1)} %add.50), channel_id=1, source_target_pairs={{0,8},{2,10},{4,12},{6,14},{8,0},{10,2},{12,4},{14,6},{1,9},{3,11}... | collective-permute-start | bytes 73736 | tf_op jit(solution)/shard_map/ppermute | solution.py:27
  38.9 3.0 %collective-permute-done.4 = f32[48,128]{1,0:T(8,128)S(1)} collective-permute-done((f32[48,128]{1,0:T(8,128)S(1)}, f32[48,128]{1,0:T(8,128)S(1)}, u32[]{:S(2)}, u32[]{:S(2)}) %collective-permute-start.4) | collective-permute-done | bytes 24608 | tf_op jit(solution)/shard_map/ppermute | solution.py:27
  41.9 0.6 add.51.refs_0_
  42.5 0.9 copy-done.3
  43.5 4.4 %shard_map.77 = (f32[48,128]{1,0:T(8,128)}, f32[1152,128]{1,0:T(8,128)}) custom-call(f32[48,128]{1,0:T(8,128)} %add.51.refs_0_, f32[12,64,256]{2,1,0:T(8,128)} %get-tuple-element.27.refs_1_, f32[12,64,256]{2,1,0:T(8,128)} %copy-done.3), custom_call_target="tpu_custom_call" | custom-call | tf_op jit(solution)/shard_map/pallas_call | solution.py:102
  47.8 3.7 %all-to-all-start.1 = ((f32[16,72,128]{2,1,0:T(8,128)}), f32[16,72,128]{2,1,0:T(8,128)S(1)}, u32[]{:S(2)}, u32[]{:S(2)}) async-start(f32[16,72,128]{2,1,0:T(8,128)} %bitcast.19), calls=%async_computation.1 | async-start | bytes 1179648 | tf_op jit(solution)/shard_map/all_to_all | solution.py:326
  51.5 0.8 copy.10.refs_1_
  52.3 14.6 %all-to-all-done.1 = f32[16,72,128]{2,1,0:T(8,128)S(1)} async-done(((f32[16,72,128]{2,1,0:T(8,128)}), f32[16,72,128]{2,1,0:T(8,128)S(1)}, u32[]{:S(2)}, u32[]{:S(2)}) %all-to-all-start.1) | async-done | bytes 589856 | tf_op jit(solution)/shard_map/all_to_all | solution.py:326
  66.9 0.8 copy-done.1
  67.7 2.5 %shard_map.78 = f32[48,256]{1,0:T(8,128)} custom-call(f32[1152,128]{1,0:T(8,128)} %bitcast.14, f32[256,48]{1,0:T(8,128)} %copy.10.refs_1_, f32[192,48]{1,0:T(8,128)} %get-tuple-element.16.refs_2_), custom_call_target="tpu_custom_call" | custom-call | tf_op jit(solution)/shard_map/pallas_call | solution.py:102
  70.5 1.2 %collective-permute-done.6 = f32[48,256]{1,0:T(8,128)S(1)} collective-permute-done((f32[48,256]{1,0:T(8,128)}, f32[48,256]{1,0:T(8,128)S(1)}, u32[]{:S(2)}, u32[]{:S(2)}) %collective-permute-start.6) | collective-permute-done | bytes 49184 | tf_op jit(solution)/shard_map/ppermute | solution.py:27
  71.7 0.8 add.55
  72.5 1.2 %collective-permute-start.7 = (f32[48,256]{1,0:T(8,128)S(1)}, f32[48,256]{1,0:T(8,128)S(1)}, u32[]{:S(2)}, u32[]{:S(2)}) collective-permute-start(f32[48,256]{1,0:T(8,128)S(1)} %add.55), channel_id=1, source_target_pairs={{0,2},{2,0},{4,6},{6,4},{8,10},{10,8},{12,14},{14,12},{1,3},{3,1},... | collective-permute-start | bytes 147464 | tf_op jit(solution)/shard_map/ppermute | solution.py:27
  73.7 2.9 %collective-permute-done.7 = f32[48,256]{1,0:T(8,128)S(1)} collective-permute-done((f32[48,256]{1,0:T(8,128)S(1)}, f32[48,256]{1,0:T(8,128)S(1)}, u32[]{:S(2)}, u32[]{:S(2)}) %collective-permute-start.7) | collective-permute-done | bytes 49184 | tf_op jit(solution)/shard_map/ppermute | solution.py:27
  76.6 1.9 %collective-permute-start.8 = (f32[48,256]{1,0:T(8,128)S(1)}, f32[48,256]{1,0:T(8,128)S(1)}, u32[]{:S(2)}, u32[]{:S(2)}) collective-permute-start(f32[48,256]{1,0:T(8,128)S(1)} %add.56), channel_id=1, source_target_pairs={{0,4},{2,6},{4,0},{6,2},{8,12},{10,14},{12,8},{14,10},{1,5},{3,7},... | collective-permute-start | bytes 147464 | tf_op jit(solution)/shard_map/ppermute | solution.py:27
  78.5 2.2 %collective-permute-done.8 = f32[48,256]{1,0:T(8,128)S(1)} collective-permute-done((f32[48,256]{1,0:T(8,128)S(1)}, f32[48,256]{1,0:T(8,128)S(1)}, u32[]{:S(2)}, u32[]{:S(2)}) %collective-permute-start.8) | collective-permute-done | bytes 49184 | tf_op jit(solution)/shard_map/ppermute | solution.py:27
  80.7 2.8 %collective-permute-start.9 = (f32[48,256]{1,0:T(8,128)S(1)}, f32[48,256]{1,0:T(8,128)S(1)}, u32[]{:S(2)}, u32[]{:S(2)}) collective-permute-start(f32[48,256]{1,0:T(8,128)S(1)} %add.57), channel_id=1, source_target_pairs={{0,8},{2,10},{4,12},{6,14},{8,0},{10,2},{12,4},{14,6},{1,9},{3,11}... | collective-permute-start | bytes 147464 | tf_op jit(solution)/shard_map/ppermute | solution.py:27
  83.5 2.3 %collective-permute-done.9 = f32[48,256]{1,0:T(8,128)S(1)} collective-permute-done((f32[48,256]{1,0:T(8,128)S(1)}, f32[48,256]{1,0:T(8,128)S(1)}, u32[]{:S(2)}, u32[]{:S(2)}) %collective-permute-start.9) | collective-permute-done | bytes 49184 | tf_op jit(solution)/shard_map/ppermute | solution.py:27
  85.8 0.6 add.58.refs_0_
  86.4 4.9 %shard_map.79 = (f32[48,256]{1,0:T(8,128)}, f32[48,192]{1,0:T(8,128)}, f32[384,128]{1,0:T(8,128)}) custom-call(f32[48,256]{1,0:T(8,128)} %add.58.refs_0_, f32[1152,128]{1,0:T(8,128)} %bitcast.15, f32[192,48]{1,0:T(8,128)} %get-tuple-element.16.refs_2_), custom_call_target="tpu_custom_call" | custom-call | tf_op jit(solution)/shard_map/pallas_call | solution.py:102
  91.4 5.0 %all-to-all-start.2 = ((f32[16,24,128]{2,1,0:T(8,128)}), f32[16,24,128]{2,1,0:T(8,128)S(1)}, u32[]{:S(2)}, u32[]{:S(2)}) async-start(f32[16,24,128]{2,1,0:T(8,128)} %bitcast.20), calls=%async_computation.2 | async-start | bytes 393216 | tf_op jit(solution)/shard_map/all_to_all | solution.py:326
  96.7 1.1 collective-permute-done.10
  97.8 0.8 add.59
  98.6 1.9 %collective-permute-start.11 = (f32[48,192]{1,0:T(8,128)S(1)}, f32[48,192]{1,0:T(8,128)S(1)}, u32[]{:S(2)}, u32[]{:S(2)}) collective-permute-start(f32[48,192]{1,0:T(8,128)S(1)} %add.59), channel_id=1, source_target_pairs={{0,2},{2,0},{4,6},{6,4},{8,10},{10,8},{12,14},{14,12},{1,3},{3,1},... | collective-permute-start | bytes 110600 | tf_op jit(solution)/shard_map/ppermute | solution.py:27
  100.5 2.4 %collective-permute-done.11 = f32[48,192]{1,0:T(8,128)S(1)} collective-permute-done((f32[48,192]{1,0:T(8,128)S(1)}, f32[48,192]{1,0:T(8,128)S(1)}, u32[]{:S(2)}, u32[]{:S(2)}) %collective-permute-start.11) | collective-permute-done | bytes 36896 | tf_op jit(solution)/shard_map/ppermute | solution.py:27
  102.9 2.2 %collective-permute-start.12 = (f32[48,192]{1,0:T(8,128)S(1)}, f32[48,192]{1,0:T(8,128)S(1)}, u32[]{:S(2)}, u32[]{:S(2)}) collective-permute-start(f32[48,192]{1,0:T(8,128)S(1)} %add.60), channel_id=1, source_target_pairs={{0,4},{2,6},{4,0},{6,2},{8,12},{10,14},{12,8},{14,10},{1,5},{3,7},... | collective-permute-start | bytes 110600 | tf_op jit(solution)/shard_map/ppermute | solution.py:27
  105.1 2.1 %collective-permute-done.12 = f32[48,192]{1,0:T(8,128)S(1)} collective-permute-done((f32[48,192]{1,0:T(8,128)S(1)}, f32[48,192]{1,0:T(8,128)S(1)}, u32[]{:S(2)}, u32[]{:S(2)}) %collective-permute-start.12) | collective-permute-done | bytes 36896 | tf_op jit(solution)/shard_map/ppermute | solution.py:27
  107.2 3.1 %collective-permute-start.13 = (f32[48,192]{1,0:T(8,128)S(1)}, f32[48,192]{1,0:T(8,128)S(1)}, u32[]{:S(2)}, u32[]{:S(2)}) collective-permute-start(f32[48,192]{1,0:T(8,128)S(1)} %add.61), channel_id=1, source_target_pairs={{0,8},{2,10},{4,12},{6,14},{8,0},{10,2},{12,4},{14,6},{1,9},{3,11}... | collective-permute-start | bytes 110600 | tf_op jit(solution)/shard_map/ppermute | solution.py:27
  110.3 0.7 dynamic-slice_bitcast_fusion.1
  111.0 1.4 %collective-permute-done.13 = f32[48,192]{1,0:T(8,128)S(1)} collective-permute-done((f32[48,192]{1,0:T(8,128)S(1)}, f32[48,192]{1,0:T(8,128)S(1)}, u32[]{:S(2)}, u32[]{:S(2)}) %collective-permute-start.13) | collective-permute-done | bytes 36896 | tf_op jit(solution)/shard_map/ppermute | solution.py:27
  112.4 0.6 add.62.refs_0_
  113.0 0.7 copy-done.4
  113.7 3.6 %shard_map.80 = (f32[48,192]{1,0:T(8,128)}, f32[48,144]{1,0:T(8,128)}) custom-call(f32[48,192]{1,0:T(8,128)} %add.62.refs_0_, f32[384,128]{1,0:T(8,128)} %bitcast.18), custom_call_target="tpu_custom_call" | custom-call | tf_op jit(solution)/shard_map/pallas_call | solution.py:102
  117.3 0.9 dynamic-slice_bitcast_fusion
  118.1 0.7 copy.11
  (30 shorter events, 1.5 us)
Async XLA Ops:
  0.6 11.1 %copy-start = (f32[24,64,256]{2,1,0:T(8,128)S(1)}, f32[24,64,256]{2,1,0:T(8,128)}, u32[]{:S(2)}) copy-start(f32[24,64,256]{2,1,0:T(8,128)} %param.4) | copy-start | bytes 4718596
  4.3 19.6 %all-to-all-start = ((f32[16,48,128]{2,1,0:T(8,128)}), f32[16,48,128]{2,1,0:T(8,128)S(1)}, u32[]{:S(2)}, u32[]{:S(2)}) async-start(f32[16,48,128]{2,1,0:T(8,128)} %bitcast.17), calls=%async_computation | async-start | bytes 786432 | tf_op jit(solution)/shard_map/all_to_all | solution.py:326
  11.7 1.5 %copy-start.8 = (f32[64,48]{0,1:T(8,128)S(1)}, f32[64,48]{0,1:T(8,128)}, u32[]{:S(2)}) copy-start(f32[64,48]{0,1:T(8,128)} %param.5) | copy-start | bytes 36868
  12.8 29.8 %collective-permute-start.5 = (f32[12,64,256]{2,1,0:T(8,128)S(1)}, f32[12,64,256]{2,1,0:T(8,128)S(1)}, u32[]{:S(2)}, u32[]{:S(2)}) collective-permute-start(f32[12,64,256]{2,1,0:T(8,128)S(1)} %get-tuple-element.26), channel_id=1, source_target_pairs={{0,1},{1,0},{2,3},{3,2},{4,5},{5,4},{6,7},{7,6},{8,9},{9,8},{10,11... | collective-permute-start | bytes 2359304 | tf_op jit(solution)/shard_map/ppermute | solution.py:33
  13.2 10.6 %copy-start.6 = (f32[64,48]{1,0:T(8,128)}, f32[64,48]{1,0:T(8,128)S(1)}, u32[]{:S(2)}) copy-start(f32[64,48]{1,0:T(8,128)S(1)} %copy.9.refs_1_) | copy-start | bytes 36868
  13.3 1.9 %collective-permute-start = (f32[64,48]{1,0:T(8,128)S(1)}, f32[64,48]{1,0:T(8,128)S(1)}, u32[]{:S(2)}, u32[]{:S(2)}) collective-permute-start(f32[64,48]{1,0:T(8,128)S(1)} %copy.9.refs_1_), channel_id=1, source_target_pairs={{0,1},{1,0},{2,3},{3,2},{4,5},{5,4},{6,7},{7,6},{8,9},{9,8},{10,11... | collective-permute-start | bytes 36872 | tf_op jit(solution)/shard_map/ppermute | solution.py:33
  15.1 8.7 %copy-start.7 = (f32[64,48]{1,0:T(8,128)}, f32[64,48]{1,0:T(8,128)S(1)}, u32[]{:S(2)}) copy-start(f32[64,48]{1,0:T(8,128)S(1)} %collective-permute-done.refs_2_) | copy-start | bytes 36868
  23.8 0.8 copy-start.2
  27.4 24.2 %copy-start.5 = (f32[256,48]{0,1:T(8,128)S(1)}, f32[256,48]{0,1:T(8,128)}, u32[]{:S(2)}) copy-start(f32[256,48]{0,1:T(8,128)} %param.6) | copy-start | bytes 147460
  27.4 1.4 %collective-permute-start.1 = (f32[48,128]{1,0:T(8,128)}, f32[48,128]{1,0:T(8,128)S(1)}, u32[]{:S(2)}, u32[]{:S(2)}) collective-permute-start(f32[48,128]{1,0:T(8,128)} %get-tuple-element.13), channel_id=1, source_target_pairs={{0,1},{1,0},{2,3},{3,2},{4,5},{5,4},{6,7},{7,6},{8,9},{9,8},{10,11... | collective-permute-start | bytes 73736 | tf_op jit(solution)/shard_map/ppermute | solution.py:27
  29.5 3.8 %collective-permute-start.2 = (f32[48,128]{1,0:T(8,128)S(1)}, f32[48,128]{1,0:T(8,128)S(1)}, u32[]{:S(2)}, u32[]{:S(2)}) collective-permute-start(f32[48,128]{1,0:T(8,128)S(1)} %add.48), channel_id=1, source_target_pairs={{0,2},{2,0},{4,6},{6,4},{8,10},{10,8},{12,14},{14,12},{1,3},{3,1},... | collective-permute-start | bytes 73736 | tf_op jit(solution)/shard_map/ppermute | solution.py:27
  33.4 3.8 %collective-permute-start.3 = (f32[48,128]{1,0:T(8,128)S(1)}, f32[48,128]{1,0:T(8,128)S(1)}, u32[]{:S(2)}, u32[]{:S(2)}) collective-permute-start(f32[48,128]{1,0:T(8,128)S(1)} %add.49), channel_id=1, source_target_pairs={{0,4},{2,6},{4,0},{6,2},{8,12},{10,14},{12,8},{14,10},{1,5},{3,7},... | collective-permute-start | bytes 73736 | tf_op jit(solution)/shard_map/ppermute | solution.py:27
  37.2 4.7 %collective-permute-start.4 = (f32[48,128]{1,0:T(8,128)S(1)}, f32[48,128]{1,0:T(8,128)S(1)}, u32[]{:S(2)}, u32[]{:S(2)}) collective-permute-start(f32[48,128]{1,0:T(8,128)S(1)} %add.50), channel_id=1, source_target_pairs={{0,8},{2,10},{4,12},{6,14},{8,0},{10,2},{12,4},{14,6},{1,9},{3,11}... | collective-permute-start | bytes 73736 | tf_op jit(solution)/shard_map/ppermute | solution.py:27
  42.5 0.9 copy-start.3
  47.8 19.1 %all-to-all-start.1 = ((f32[16,72,128]{2,1,0:T(8,128)}), f32[16,72,128]{2,1,0:T(8,128)S(1)}, u32[]{:S(2)}, u32[]{:S(2)}) async-start(f32[16,72,128]{2,1,0:T(8,128)} %bitcast.19), calls=%async_computation.1 | async-start | bytes 1179648 | tf_op jit(solution)/shard_map/all_to_all | solution.py:326
  52.3 58.1 %copy-start.9 = (f32[48,128]{1,0:T(8,128)S(1)}, f32[48,128]{1,0:T(8,128)}, u32[]{:S(2)}) copy-start(f32[48,128]{1,0:T(8,128)} %get-tuple-element.14) | copy-start | bytes 73732
  66.9 0.8 copy-start.1
  70.2 1.4 %collective-permute-start.6 = (f32[48,256]{1,0:T(8,128)}, f32[48,256]{1,0:T(8,128)S(1)}, u32[]{:S(2)}, u32[]{:S(2)}) collective-permute-start(f32[48,256]{1,0:T(8,128)} %shard_map.78), channel_id=1, source_target_pairs={{0,1},{1,0},{2,3},{3,2},{4,5},{5,4},{6,7},{7,6},{8,9},{9,8},{10,11... | collective-permute-start | bytes 147464 | tf_op jit(solution)/shard_map/ppermute | solution.py:27
  72.5 4.1 %collective-permute-start.7 = (f32[48,256]{1,0:T(8,128)S(1)}, f32[48,256]{1,0:T(8,128)S(1)}, u32[]{:S(2)}, u32[]{:S(2)}) collective-permute-start(f32[48,256]{1,0:T(8,128)S(1)} %add.55), channel_id=1, source_target_pairs={{0,2},{2,0},{4,6},{6,4},{8,10},{10,8},{12,14},{14,12},{1,3},{3,1},... | collective-permute-start | bytes 147464 | tf_op jit(solution)/shard_map/ppermute | solution.py:27
  76.6 4.2 %collective-permute-start.8 = (f32[48,256]{1,0:T(8,128)S(1)}, f32[48,256]{1,0:T(8,128)S(1)}, u32[]{:S(2)}, u32[]{:S(2)}) collective-permute-start(f32[48,256]{1,0:T(8,128)S(1)} %add.56), channel_id=1, source_target_pairs={{0,4},{2,6},{4,0},{6,2},{8,12},{10,14},{12,8},{14,10},{1,5},{3,7},... | collective-permute-start | bytes 147464 | tf_op jit(solution)/shard_map/ppermute | solution.py:27
  80.7 5.1 %collective-permute-start.9 = (f32[48,256]{1,0:T(8,128)S(1)}, f32[48,256]{1,0:T(8,128)S(1)}, u32[]{:S(2)}, u32[]{:S(2)}) collective-permute-start(f32[48,256]{1,0:T(8,128)S(1)} %add.57), channel_id=1, source_target_pairs={{0,8},{2,10},{4,12},{6,14},{8,0},{10,2},{12,4},{14,6},{1,9},{3,11}... | collective-permute-start | bytes 147464 | tf_op jit(solution)/shard_map/ppermute | solution.py:27
  91.4 21.7 %all-to-all-start.2 = ((f32[16,24,128]{2,1,0:T(8,128)}), f32[16,24,128]{2,1,0:T(8,128)S(1)}, u32[]{:S(2)}, u32[]{:S(2)}) async-start(f32[16,24,128]{2,1,0:T(8,128)} %bitcast.20), calls=%async_computation.2 | async-start | bytes 393216 | tf_op jit(solution)/shard_map/all_to_all | solution.py:326
  96.3 1.5 %collective-permute-start.10 = (f32[48,192]{1,0:T(8,128)}, f32[48,192]{1,0:T(8,128)S(1)}, u32[]{:S(2)}, u32[]{:S(2)}) collective-permute-start(f32[48,192]{1,0:T(8,128)} %get-tuple-element.18), channel_id=1, source_target_pairs={{0,1},{1,0},{2,3},{3,2},{4,5},{5,4},{6,7},{7,6},{8,9},{9,8},{10,11... | collective-permute-start | bytes 110600 | tf_op jit(solution)/shard_map/ppermute | solution.py:27
  98.6 4.3 %collective-permute-start.11 = (f32[48,192]{1,0:T(8,128)S(1)}, f32[48,192]{1,0:T(8,128)S(1)}, u32[]{:S(2)}, u32[]{:S(2)}) collective-permute-start(f32[48,192]{1,0:T(8,128)S(1)} %add.59), channel_id=1, source_target_pairs={{0,2},{2,0},{4,6},{6,4},{8,10},{10,8},{12,14},{14,12},{1,3},{3,1},... | collective-permute-start | bytes 110600 | tf_op jit(solution)/shard_map/ppermute | solution.py:27
  102.9 4.3 %collective-permute-start.12 = (f32[48,192]{1,0:T(8,128)S(1)}, f32[48,192]{1,0:T(8,128)S(1)}, u32[]{:S(2)}, u32[]{:S(2)}) collective-permute-start(f32[48,192]{1,0:T(8,128)S(1)} %add.60), channel_id=1, source_target_pairs={{0,4},{2,6},{4,0},{6,2},{8,12},{10,14},{12,8},{14,10},{1,5},{3,7},... | collective-permute-start | bytes 110600 | tf_op jit(solution)/shard_map/ppermute | solution.py:27
  107.2 5.2 %collective-permute-start.13 = (f32[48,192]{1,0:T(8,128)S(1)}, f32[48,192]{1,0:T(8,128)S(1)}, u32[]{:S(2)}, u32[]{:S(2)}) collective-permute-start(f32[48,192]{1,0:T(8,128)S(1)} %add.61), channel_id=1, source_target_pairs={{0,8},{2,10},{4,12},{6,14},{8,0},{10,2},{12,4},{14,6},{1,9},{3,11}... | collective-permute-start | bytes 110600 | tf_op jit(solution)/shard_map/ppermute | solution.py:27
  113.0 0.7 copy-start.4

commit v3 on v2

--- a/solution.py
+++ b/solution.py
@@ -97,9 +97,21 @@
     out[...] = orthonormal(part[...])
 
 
-def call(body, shapes, *operands, **settings):
-    shapes = [jax.ShapeDtypeStruct(shape, jnp.float32) for shape in shapes]
-    return pl.pallas_call(body, out_shape=shapes, **settings)(*operands)
+def call(body, shapes, *operands, far=(), out_far=False, **settings):
+    near = pl.BlockSpec(memory_space=pltpu.VMEM)
+    away = pl.BlockSpec(memory_space=pl.ANY)
+    placed = [
+        x if at in far else pltpu.with_memory_space_constraint(x, pltpu.VMEM)
+        for at, x in enumerate(operands)
+    ]
+    kind = jax.ShapeDtypeStruct if out_far else pltpu.VMEM
+    return pl.pallas_call(
+        body,
+        in_specs=[away if at in far else near for at in range(len(operands))],
+        out_specs=[near] * len(shapes),
+        out_shape=[kind(shape, jnp.float32) for shape in shapes],
+        **settings,
+    )(*placed)
 
 
 def general(window_data, factor_one, factor_two, factor_three):
@@ -165,30 +177,47 @@
     return (one_own[:rank].T, two_t.T, basis_three, core)
 
 
-def pack_one(field, two, three, out, *, share, half, count):
-    at = pl.program_id(0)
-    steps, rows, cols = field.shape[1:]
+def pack_one(field, two_far, three_far, out, room, two, three, arrived, landed, *, share, half, count):
+    chunks, _, steps, rows, cols = room.shape
     rank = two.shape[0]
     slots = share + 1
+
+    def fetch(at, h):
+        source = field.at[pl.ds(h * half + at * steps, steps)]
+        return pltpu.make_async_copy(source, room.at[at, h], arrived.at[at, h])
+
+    copies = [
+        pltpu.make_async_copy(three_far, three, landed.at[0]),
+        pltpu.make_async_copy(two_far, two, landed.at[1]),
+    ]
+    for copy in copies:
+        copy.start()
+    for at in range(chunks):
+        for h in range(2):
+            fetch(at, h).start()
+    copies[0].wait()
+    first = three[:half]
+    second = three[half:]
+    empty = jnp.zeros((half, lanes // 2 - rank), jnp.float32)
+    both = jnp.concatenate([first, empty, second, empty], axis=1)
+    for d in range(count):
+        out[pl.ds(d * half * slots + share, half, stride=slots), :] = both
+    copies[1].wait()
     two_high, two_low = split(two[...])
     both = jnp.concatenate([two_high, two_low])
-    for q in range(steps):
-        high, low = split(field[:, q].reshape(2 * rows, cols))
-        first = lax.dot_general(both, high, nt, preferred_element_type=jnp.float32)
-        second = lax.dot_general(two_high, low, nt, preferred_element_type=jnp.float32)
-        along = first[:rank] + (first[rank:] + second)
-        for s in range(share):
-            start = (at * steps + q) * slots + s
-            out[pl.ds(start, count, stride=half * slots), :] = along[s * count : (s + 1) * count]
-
-    @pl.when(at == 0)
-    def _():
-        first = three[:half]
-        second = three[half:]
-        room = jnp.zeros((half, lanes // 2 - rank), jnp.float32)
-        both = jnp.concatenate([first, room, second, room], axis=1)
-        for d in range(count):
-            out[pl.ds(d * half * slots + share, half, stride=slots), :] = both
+    for at in range(chunks):
+        for h in range(2):
+            fetch(at, h).wait()
+        for q in range(steps):
+            high, low = split(room[at, :, q].reshape(2 * rows, cols))
+            first = lax.dot_general(both, high, nt, preferred_element_type=jnp.float32)
+            second = lax.dot_general(two_high, low, nt, preferred_element_type=jnp.float32)
+            along = first[:rank] + (first[rank:] + second)
+            for s in range(share):
+                start = (at * steps + q) * slots + s
+                out[pl.ds(start, count, stride=half * slots), :] = along[
+                    s * count : (s + 1) * count
+                ]
 
 
 def work_one(got, own, other, out, three, *, share, half, count):
@@ -220,17 +249,29 @@
     out[...] = dot3(dot3(unfold, one), unfold, tn)
 
 
-def pack_two(part, own, other, basis, out, *, share, half, count):
-    rows, cols = own.shape[1:]
+def pack_two(part, field, other, basis, out, room, arrived, *, share, half, count):
+    rows, cols = other.shape[1:]
+    at = lax.axis_index("narrow")
+    own = pltpu.make_async_copy(
+        field.at[pl.ds(at * half, half)],
+        room.at[:, pl.ds(pl.multiple_of(at * rows, 8), rows), :],
+        arrived.at[0],
+    )
+    rest = pltpu.make_async_copy(
+        other, room.at[:, pl.ds(pl.multiple_of((1 - at) * rows, 8), rows), :], arrived.at[1]
+    )
+    own.start()
+    rest.start()
     value = orthonormal(part[...])
     basis[...] = value
     slots = share * (cols // lanes)
-    at = lax.axis_index("narrow")
-    value = split(jnp.where(at == 0, value, pltpu.roll(value, rows, 1)))
+    value = split(value)
     both = jnp.concatenate(value)
     rank = part.shape[0]
+    own.wait()
+    rest.wait()
     for k in range(half):
-        high, low = split(jnp.concatenate([own[k], other[k]]))
+        high, low = split(room[k])
         first = lax.dot_general(both, high, nn, preferred_element_type=jnp.float32)
         second = lax.dot_general(value[0], low, nn, preferred_element_type=jnp.float32)
         along = first[:rank] + (first[rank:] + second)
@@ -301,12 +342,14 @@
     out[...] = result
 
 
-def finish(part, got, basis, core, *, share, half, count):
+def finish(part, got, basis, core, room, *, share, half, count):
     rank, size = part.shape
     tall = -(-size // lanes)
     pitch = got.shape[0] // count
     value = orthonormal(part[...])
-    basis[...] = value
+    room[...] = value.T
+    depth = basis.shape[0]
+    basis[...] = room[pl.ds(pl.multiple_of(lax.axis_index("wide") * depth, 8), depth), :]
     value = split(value)
     for b in range(share):
         rows = []
@@ -344,22 +387,26 @@
         run.__name__ = body.__name__
         return run
 
-    steps = 3 if half % 3 == 0 else 1
+    chunks = 3 if half % 3 == 0 else 1
     slots = share + 1
-    packed = pl.pallas_call(
+    (packed,) = call(
         stage(pack_one),
-        grid=(steps,),
-        in_specs=[
-            pl.BlockSpec((2, half // steps, rows, cols), lambda at: (0, at, 0, 0)),
-            pl.BlockSpec((rank, cols), lambda at: (0, 0)),
-            pl.BlockSpec((depth, rank), lambda at: (0, 0)),
+        [(size * slots, lanes)],
+        window_data,
+        factor_two.T,
+        factor_three,
+        far=(0, 1, 2),
+        scratch_shapes=[
+            pltpu.VMEM((chunks, 2, half // chunks, rows, cols), jnp.float32),
+            pltpu.VMEM((rank, cols), jnp.float32),
+            pltpu.VMEM((depth, rank), jnp.float32),
+            pltpu.SemaphoreType.DMA((chunks, 2)),
+            pltpu.SemaphoreType.DMA((2,)),
         ],
-        out_specs=pl.BlockSpec((size * slots, lanes), lambda at: (0, 0)),
-        out_shape=jax.ShapeDtypeStruct((size * slots, lanes), jnp.float32),
-    )(window_data.reshape(2, half, rows, cols), factor_two.T, factor_three)
+    )
     got = exchange(packed, count)
-    own = lax.dynamic_slice_in_dim(window_data, core_at * half, half, 0)
-    other = swap(lax.dynamic_slice_in_dim(window_data, (1 - core_at) * half, half, 0))
+    field, _ = lax.optimization_barrier((window_data, packed))
+    other = swap(lax.dynamic_slice_in_dim(field, (1 - core_at) * half, half, 0))
     product, three = call(
         stage(work_one), [(rank, 2 * rows), (size, rank)], got, factor_one, swap(factor_one)
     )
@@ -367,7 +414,16 @@
 
     parts = cols // lanes
     one_t, packed = call(
-        stage(pack_two), [product.shape, (size * share * parts, lanes)], product, own, other
+        stage(pack_two),
+        [product.shape, (size * share * parts, lanes)],
+        product,
+        window_data,
+        other,
+        far=(1, 2),
+        scratch_shapes=[
+            pltpu.VMEM((half, 2 * rows, cols), jnp.float32),
+            pltpu.SemaphoreType.DMA((2,)),
+        ],
     )
     got = exchange(packed, count)
     (product,) = call(stage(work_two), [(rank, cols)], got, factor_two, three)
@@ -384,9 +440,15 @@
     )
     got = exchange(sent, count)
     product = total(total(product, "narrow"), "wide")
-    three_t, core = call(stage(finish), [product.shape, (rank, share * rank)], product, got)
+    basis_three, core = call(
+        stage(finish),
+        [(depth, rank), (rank, share * rank)],
+        product,
+        got,
+        out_far=True,
+        scratch_shapes=[pltpu.VMEM((size, rank), jnp.float32)],
+    )
     basis_one = lax.dynamic_slice_in_dim(one_t, core_at * rows, rows, 1).T
-    basis_three = lax.dynamic_slice_in_dim(three_t, lax.axis_index("wide") * depth, depth, 1).T
     return (basis_one, two_t.T, basis_three, core)
 
 
@@ -398,7 +460,7 @@
         lax.axis_size("narrow") == 2
         and rank % count == 0
         and count % 8 == 0
-        and depth % 2 == 0
+        and depth % 8 == 0
         and (depth // 2) * (rank // count + 1) % 8 == 0
         and (depth // 2) * (rank // count) * (cols // lanes) % 8 == 0
         and 2 * rows == lanes

time: 120 us -> 104 us (0.87)
  Pallas kernels: 21.7 us -> 15 us
  other arithmetic: 4.25 us -> 0.08 us
  local copies, waits for them, and re-layouts: 7.33 us -> 3.31 us
    pallas_call x6, Pallas kernels: 21.7 us -> 15 us  [call(): pl.pallas_call(body, in_specs=[away if at in far else near for at in rang...]
    add x12, other arithmetic: 4.25 us -> 0.08 us  [total(): part + lax.ppermute(part, axis, [(at, at ^ step) for at in range(size)])]
    unnamed x23 -> x11, local copies, waits for them, and re-layouts: 4.72 us -> 1.68 us
  transfers between devices with their start and end apart: 17 -> 17, of which waited for: 15 -> 15; matrix products, arithmetic and copies ran while one was open for 5% -> 2% of each run, Pallas kernels for 2% -> 1%
where the time goes in v3:
time: 104 us
  waiting for transfers between devices  51.4 us (49%)
  starting transfers between devices  33.4 us (32%)
  Pallas kernels  15 us (14%)
  local copies, waits for them, and re-layouts  3.31 us (3%)
    ppermute x12, waiting for transfers between devices, total(): lax.ppermute(part, axis, [(at, at ^ step) for at in range(size)])  25.5 us
    all_to_all x3, waiting for transfers between devices, exchange(): return lax.all_to_all(value, group, 0, 0, tiled=True).reshape(rows, lanes)  23.9 us
    ppermute x12, starting transfers between devices, total(): lax.ppermute(part, axis, [(at, at ^ step) for at in range(size)])  16.7 us
    all_to_all x3, starting transfers between devices, exchange(): return lax.all_to_all(value, group, 0, 0, tiled=True).reshape(rows, lanes)  16.1 us
    pallas_call x6, Pallas kernels, call(): pl.pallas_call(body, in_specs=[away if at in far else near for at in rang...  15 us
  transfers between devices with their start and end apart: 17, of which 15 were waited for; matrix products, arithmetic and copies ran while one was open for 2% of the time, Pallas kernels for 1%

profile of v3, /device:TPU:0, one launch (start us, length us, event | category | flops | bytes accessed | tf_op | source)
XLA Modules:
  0.0 103.9 jit_solution(14551896313363872266)
XLA Ops:
  0.6 0.0 copy-start
  0.6 3.1 %shard_map.75 = f32[768,128]{1,0:T(8,128)} custom-call(f32[24,64,256]{2,1,0:T(8,128)} %refs_1_.3, f32[48,256]{1,0:T(8,128)} %bitcast.15, f32[24,48]{1,0:T(8,128)} %refs_2_.1), custom_call_target="tpu_custom_call" | custom-call | tf_op jit(solution)/shard_map/pallas_call | solution.py:108
  3.7 0.0 copy-start.3
  3.7 7.4 %all-to-all-start = ((f32[16,48,128]{2,1,0:T(8,128)}), f32[16,48,128]{2,1,0:T(8,128)S(1)}, u32[]{:S(2)}, u32[]{:S(2)}) async-start(f32[16,48,128]{2,1,0:T(8,128)} %bitcast.1), calls=%async_computation | async-start | bytes 786432 | tf_op jit(solution)/shard_map/all_to_all | solution.py:369
  11.2 0.9 constant_dynamic-slice_fusion
  12.1 0.4 collective-permute-start.5
  12.5 0.1 copy.9.refs_1_
  12.6 0.1 collective-permute-start
  12.7 1.9 %collective-permute-done.refs_2_ = f32[64,48]{1,0:T(8,128)S(1)} collective-permute-done((f32[64,48]{1,0:T(8,128)S(1)}, f32[64,48]{1,0:T(8,128)S(1)}, u32[]{:S(2)}, u32[]{:S(2)}) %collective-permute-start) | collective-permute-done | bytes 12320 | tf_op jit(solution)/shard_map/ppermute | solution.py:33
  14.7 8.6 %all-to-all-done = f32[16,48,128]{2,1,0:T(8,128)S(1)} async-done(((f32[16,48,128]{2,1,0:T(8,128)}), f32[16,48,128]{2,1,0:T(8,128)S(1)}, u32[]{:S(2)}, u32[]{:S(2)}) %all-to-all-start) | async-done | bytes 393248 | tf_op jit(solution)/shard_map/all_to_all | solution.py:369
  23.3 1.1 %shard_map.76 = (f32[48,128]{1,0:T(8,128)S(1)}, f32[192,48]{1,0:T(8,128)S(1)}) custom-call(f32[768,128]{1,0:T(8,128)S(1)} %bitcast.13, f32[64,48]{1,0:T(8,128)S(1)} %copy.9.refs_1_, f32[64,48]{1,0:T(8,128)S(1)} %collective-permute-done.refs_2_), custom_call_target="tpu_custom_call" | custom-call | tf_op jit(solution)/shard_map/pallas_call | solution.py:108
  24.4 0.1 collective-permute-start.1
  24.6 1.1 %collective-permute-done.1 = f32[48,128]{1,0:T(8,128)S(1)} collective-permute-done((f32[48,128]{1,0:T(8,128)S(1)}, f32[48,128]{1,0:T(8,128)S(1)}, u32[]{:S(2)}, u32[]{:S(2)}) %collective-permute-start.1) | collective-permute-done | bytes 24608 | tf_op jit(solution)/shard_map/ppermute | solution.py:27
  25.6 0.7 collective-permute-start.2
  26.3 3.2 %collective-permute-done.2 = f32[48,128]{1,0:T(8,128)S(1)} collective-permute-done((f32[48,128]{1,0:T(8,128)S(1)}, f32[48,128]{1,0:T(8,128)S(1)}, u32[]{:S(2)}, u32[]{:S(2)}) %collective-permute-start.2) | collective-permute-done | bytes 24608 | tf_op jit(solution)/shard_map/ppermute | solution.py:27
  29.5 0.9 collective-permute-start.3
  30.4 2.9 %collective-permute-done.3 = f32[48,128]{1,0:T(8,128)S(1)} collective-permute-done((f32[48,128]{1,0:T(8,128)S(1)}, f32[48,128]{1,0:T(8,128)S(1)}, u32[]{:S(2)}, u32[]{:S(2)}) %collective-permute-start.3) | collective-permute-done | bytes 24608 | tf_op jit(solution)/shard_map/ppermute | solution.py:27
  33.3 1.7 %collective-permute-start.4 = (f32[48,128]{1,0:T(8,128)S(1)}, f32[48,128]{1,0:T(8,128)S(1)}, u32[]{:S(2)}, u32[]{:S(2)}) collective-permute-start(f32[48,128]{1,0:T(8,128)S(1)} %add.44), channel_id=1, source_target_pairs={{0,8},{2,10},{4,12},{6,14},{8,0},{10,2},{12,4},{14,6},{1,9},{3,11}... | collective-permute-start | bytes 73736 | tf_op jit(solution)/shard_map/ppermute | solution.py:27
  35.0 3.0 %collective-permute-done.4 = f32[48,128]{1,0:T(8,128)S(1)} collective-permute-done((f32[48,128]{1,0:T(8,128)S(1)}, f32[48,128]{1,0:T(8,128)S(1)}, u32[]{:S(2)}, u32[]{:S(2)}) %collective-permute-start.4) | collective-permute-done | bytes 24608 | tf_op jit(solution)/shard_map/ppermute | solution.py:27
  38.0 0.0 collective-permute-done.5.refs_2_
  38.1 0.9 copy-done.1
  38.9 4.0 %shard_map.77 = (f32[48,128]{1,0:T(8,128)S(1)}, f32[1152,128]{1,0:T(8,128)}) custom-call(f32[48,128]{1,0:T(8,128)S(1)} %add.45.refs_0_, f32[24,64,256]{2,1,0:T(8,128)} %refs_1_.3, f32[12,64,256]{2,1,0:T(8,128)} %copy-done.1), custom_call_target="tpu_custom_call" | custom-call | tf_op jit(solution)/shard_map/pallas_call | solution.py:108
  43.0 3.7 %all-to-all-start.1 = ((f32[16,72,128]{2,1,0:T(8,128)}), f32[16,72,128]{2,1,0:T(8,128)S(1)}, u32[]{:S(2)}, u32[]{:S(2)}) async-start(f32[16,72,128]{2,1,0:T(8,128)} %bitcast.4), calls=%async_computation.1 | async-start | bytes 1179648 | tf_op jit(solution)/shard_map/all_to_all | solution.py:369
  46.7 0.1 copy.10.refs_1_
  46.8 15.3 %all-to-all-done.1 = f32[16,72,128]{2,1,0:T(8,128)S(1)} async-done(((f32[16,72,128]{2,1,0:T(8,128)}), f32[16,72,128]{2,1,0:T(8,128)S(1)}, u32[]{:S(2)}, u32[]{:S(2)}) %all-to-all-start.1) | async-done | bytes 589856 | tf_op jit(solution)/shard_map/all_to_all | solution.py:369
  62.1 0.7 shard_map.78
  62.8 0.3 collective-permute-start.6
  63.1 1.0 collective-permute-done.6
  64.1 1.3 %collective-permute-start.7 = (f32[48,256]{1,0:T(8,128)S(1)}, f32[48,256]{1,0:T(8,128)S(1)}, u32[]{:S(2)}, u32[]{:S(2)}) collective-permute-start(f32[48,256]{1,0:T(8,128)S(1)} %add.48), channel_id=1, source_target_pairs={{0,2},{2,0},{4,6},{6,4},{8,10},{10,8},{12,14},{14,12},{1,3},{3,1},... | collective-permute-start | bytes 147464 | tf_op jit(solution)/shard_map/ppermute | solution.py:27
  65.4 2.9 %collective-permute-done.7 = f32[48,256]{1,0:T(8,128)S(1)} collective-permute-done((f32[48,256]{1,0:T(8,128)S(1)}, f32[48,256]{1,0:T(8,128)S(1)}, u32[]{:S(2)}, u32[]{:S(2)}) %collective-permute-start.7) | collective-permute-done | bytes 49184 | tf_op jit(solution)/shard_map/ppermute | solution.py:27
  68.3 1.9 %collective-permute-start.8 = (f32[48,256]{1,0:T(8,128)S(1)}, f32[48,256]{1,0:T(8,128)S(1)}, u32[]{:S(2)}, u32[]{:S(2)}) collective-permute-start(f32[48,256]{1,0:T(8,128)S(1)} %add.49), channel_id=1, source_target_pairs={{0,4},{2,6},{4,0},{6,2},{8,12},{10,14},{12,8},{14,10},{1,5},{3,7},... | collective-permute-start | bytes 147464 | tf_op jit(solution)/shard_map/ppermute | solution.py:27
  70.1 2.3 %collective-permute-done.8 = f32[48,256]{1,0:T(8,128)S(1)} collective-permute-done((f32[48,256]{1,0:T(8,128)S(1)}, f32[48,256]{1,0:T(8,128)S(1)}, u32[]{:S(2)}, u32[]{:S(2)}) %collective-permute-start.8) | collective-permute-done | bytes 49184 | tf_op jit(solution)/shard_map/ppermute | solution.py:27
  72.4 2.8 %collective-permute-start.9 = (f32[48,256]{1,0:T(8,128)S(1)}, f32[48,256]{1,0:T(8,128)S(1)}, u32[]{:S(2)}, u32[]{:S(2)}) collective-permute-start(f32[48,256]{1,0:T(8,128)S(1)} %add.50), channel_id=1, source_target_pairs={{0,8},{2,10},{4,12},{6,14},{8,0},{10,2},{12,4},{14,6},{1,9},{3,11}... | collective-permute-start | bytes 147464 | tf_op jit(solution)/shard_map/ppermute | solution.py:27
  75.2 2.3 %collective-permute-done.9 = f32[48,256]{1,0:T(8,128)S(1)} collective-permute-done((f32[48,256]{1,0:T(8,128)S(1)}, f32[48,256]{1,0:T(8,128)S(1)}, u32[]{:S(2)}, u32[]{:S(2)}) %collective-permute-start.9) | collective-permute-done | bytes 49184 | tf_op jit(solution)/shard_map/ppermute | solution.py:27
  77.5 3.5 %shard_map.79 = (f32[48,256]{1,0:T(8,128)S(1)}, f32[48,192]{1,0:T(8,128)S(1)}, f32[384,128]{1,0:T(8,128)}) custom-call(f32[48,256]{1,0:T(8,128)S(1)} %add.51.refs_0_, f32[1152,128]{1,0:T(8,128)S(1)} %bitcast.12, f32[192,48]{1,0:T(8,128)S(1)} %get-tuple-element.18.refs_2_), custom_call_target="tpu_custom_call" | custom-call | tf_op jit(solution)/shard_map/pallas_call | solution.py:108
  81.0 5.0 %all-to-all-start.2 = ((f32[16,24,128]{2,1,0:T(8,128)}), f32[16,24,128]{2,1,0:T(8,128)S(1)}, u32[]{:S(2)}, u32[]{:S(2)}) async-start(f32[16,24,128]{2,1,0:T(8,128)} %bitcast.7), calls=%async_computation.2 | async-start | bytes 393216 | tf_op jit(solution)/shard_map/all_to_all | solution.py:369
  85.9 0.4 collective-permute-start.10
  86.3 0.9 collective-permute-done.10
  87.3 1.9 %collective-permute-start.11 = (f32[48,192]{1,0:T(8,128)S(1)}, f32[48,192]{1,0:T(8,128)S(1)}, u32[]{:S(2)}, u32[]{:S(2)}) collective-permute-start(f32[48,192]{1,0:T(8,128)S(1)} %add.52), channel_id=1, source_target_pairs={{0,2},{2,0},{4,6},{6,4},{8,10},{10,8},{12,14},{14,12},{1,3},{3,1},... | collective-permute-start | bytes 110600 | tf_op jit(solution)/shard_map/ppermute | solution.py:27
  89.2 2.9 %collective-permute-done.11 = f32[48,192]{1,0:T(8,128)S(1)} collective-permute-done((f32[48,192]{1,0:T(8,128)S(1)}, f32[48,192]{1,0:T(8,128)S(1)}, u32[]{:S(2)}, u32[]{:S(2)}) %collective-permute-start.11) | collective-permute-done | bytes 36896 | tf_op jit(solution)/shard_map/ppermute | solution.py:27
  92.0 2.1 %collective-permute-start.12 = (f32[48,192]{1,0:T(8,128)S(1)}, f32[48,192]{1,0:T(8,128)S(1)}, u32[]{:S(2)}, u32[]{:S(2)}) collective-permute-start(f32[48,192]{1,0:T(8,128)S(1)} %add.53), channel_id=1, source_target_pairs={{0,4},{2,6},{4,0},{6,2},{8,12},{10,14},{12,8},{14,10},{1,5},{3,7},... | collective-permute-start | bytes 110600 | tf_op jit(solution)/shard_map/ppermute | solution.py:27
  94.2 2.1 %collective-permute-done.12 = f32[48,192]{1,0:T(8,128)S(1)} collective-permute-done((f32[48,192]{1,0:T(8,128)S(1)}, f32[48,192]{1,0:T(8,128)S(1)}, u32[]{:S(2)}, u32[]{:S(2)}) %collective-permute-start.12) | collective-permute-done | bytes 36896 | tf_op jit(solution)/shard_map/ppermute | solution.py:27
  96.3 2.7 %collective-permute-start.13 = (f32[48,192]{1,0:T(8,128)S(1)}, f32[48,192]{1,0:T(8,128)S(1)}, u32[]{:S(2)}, u32[]{:S(2)}) collective-permute-start(f32[48,192]{1,0:T(8,128)S(1)} %add.54), channel_id=1, source_target_pairs={{0,8},{2,10},{4,12},{6,14},{8,0},{10,2},{12,4},{14,6},{1,9},{3,11}... | collective-permute-start | bytes 110600 | tf_op jit(solution)/shard_map/ppermute | solution.py:27
  99.0 0.7 dynamic-slice_bitcast_fusion
  99.6 0.6 copy.11
  100.3 1.0 %collective-permute-done.13 = f32[48,192]{1,0:T(8,128)S(1)} collective-permute-done((f32[48,192]{1,0:T(8,128)S(1)}, f32[48,192]{1,0:T(8,128)S(1)}, u32[]{:S(2)}, u32[]{:S(2)}) %collective-permute-start.13) | collective-permute-done | bytes 36896 | tf_op jit(solution)/shard_map/ppermute | solution.py:27
  101.3 0.0 all-to-all-done.2
  101.3 2.6 %shard_map.80 = (f32[24,48]{1,0:T(8,128)}, f32[48,144]{1,0:T(8,128)}) custom-call(f32[48,192]{1,0:T(8,128)S(1)} %add.55.refs_0_, f32[384,128]{1,0:T(8,128)S(1)} %bitcast.14), custom_call_target="tpu_custom_call" | custom-call | tf_op jit(solution)/shard_map/pallas_call | solution.py:108
  (17 shorter events, 0.1 us)
Async XLA Ops:
  0.6 10.5 %copy-start = (f32[24,64,256]{2,1,0:T(8,128)S(1)}, f32[24,64,256]{2,1,0:T(8,128)}, u32[]{:S(2)}) copy-start(f32[24,64,256]{2,1,0:T(8,128)} %refs_1_.3) | copy-start | bytes 4718596
  3.7 8.8 %copy-start.3 = (f32[64,48]{0,1:T(8,128)S(1)}, f32[64,48]{0,1:T(8,128)}, u32[]{:S(2)}) copy-start(f32[64,48]{0,1:T(8,128)} %param.5) | copy-start | bytes 36868
  3.7 19.6 %all-to-all-start = ((f32[16,48,128]{2,1,0:T(8,128)}), f32[16,48,128]{2,1,0:T(8,128)S(1)}, u32[]{:S(2)}, u32[]{:S(2)}) async-start(f32[16,48,128]{2,1,0:T(8,128)} %bitcast.1), calls=%async_computation | async-start | bytes 786432 | tf_op jit(solution)/shard_map/all_to_all | solution.py:369
  12.1 25.9 %collective-permute-start.5 = (f32[12,64,256]{2,1,0:T(8,128)}, f32[12,64,256]{2,1,0:T(8,128)S(1)}, u32[]{:S(2)}, u32[]{:S(2)}) collective-permute-start(f32[12,64,256]{2,1,0:T(8,128)} %constant_dynamic-slice_fusion), channel_id=1, source_target_pairs={{0,1},{1,0},{2,3},{3,2},{4,5},{5,4},{6,7},{7,6},{8,9},{9,8},{10,11... | collective-permute-start | bytes 2359304 | tf_op jit(solution)/shard_map/ppermute | solution.py:33
  12.6 2.1 %collective-permute-start = (f32[64,48]{1,0:T(8,128)S(1)}, f32[64,48]{1,0:T(8,128)S(1)}, u32[]{:S(2)}, u32[]{:S(2)}) collective-permute-start(f32[64,48]{1,0:T(8,128)S(1)} %copy.9.refs_1_), channel_id=1, source_target_pairs={{0,1},{1,0},{2,3},{3,2},{4,5},{5,4},{6,7},{7,6},{8,9},{9,8},{10,11... | collective-permute-start | bytes 36872 | tf_op jit(solution)/shard_map/ppermute | solution.py:33
  24.4 1.2 %collective-permute-start.1 = (f32[48,128]{1,0:T(8,128)S(1)}, f32[48,128]{1,0:T(8,128)S(1)}, u32[]{:S(2)}, u32[]{:S(2)}) collective-permute-start(f32[48,128]{1,0:T(8,128)S(1)} %get-tuple-element.14), channel_id=1, source_target_pairs={{0,1},{1,0},{2,3},{3,2},{4,5},{5,4},{6,7},{7,6},{8,9},{9,8},{10,11... | collective-permute-start | bytes 73736 | tf_op jit(solution)/shard_map/ppermute | solution.py:27
  25.6 3.8 %collective-permute-start.2 = (f32[48,128]{1,0:T(8,128)S(1)}, f32[48,128]{1,0:T(8,128)S(1)}, u32[]{:S(2)}, u32[]{:S(2)}) collective-permute-start(f32[48,128]{1,0:T(8,128)S(1)} %add.42), channel_id=1, source_target_pairs={{0,2},{2,0},{4,6},{6,4},{8,10},{10,8},{12,14},{14,12},{1,3},{3,1},... | collective-permute-start | bytes 73736 | tf_op jit(solution)/shard_map/ppermute | solution.py:27
  29.5 3.8 %collective-permute-start.3 = (f32[48,128]{1,0:T(8,128)S(1)}, f32[48,128]{1,0:T(8,128)S(1)}, u32[]{:S(2)}, u32[]{:S(2)}) collective-permute-start(f32[48,128]{1,0:T(8,128)S(1)} %add.43), channel_id=1, source_target_pairs={{0,4},{2,6},{4,0},{6,2},{8,12},{10,14},{12,8},{14,10},{1,5},{3,7},... | collective-permute-start | bytes 73736 | tf_op jit(solution)/shard_map/ppermute | solution.py:27
  33.3 4.7 %collective-permute-start.4 = (f32[48,128]{1,0:T(8,128)S(1)}, f32[48,128]{1,0:T(8,128)S(1)}, u32[]{:S(2)}, u32[]{:S(2)}) collective-permute-start(f32[48,128]{1,0:T(8,128)S(1)} %add.44), channel_id=1, source_target_pairs={{0,8},{2,10},{4,12},{6,14},{8,0},{10,2},{12,4},{14,6},{1,9},{3,11}... | collective-permute-start | bytes 73736 | tf_op jit(solution)/shard_map/ppermute | solution.py:27
  38.0 8.6 %copy-start.2 = (f32[256,48]{0,1:T(8,128)S(1)}, f32[256,48]{0,1:T(8,128)}, u32[]{:S(2)}) copy-start(f32[256,48]{0,1:T(8,128)} %param.6) | copy-start | bytes 147460
  38.1 0.9 copy-start.1
  43.0 19.1 %all-to-all-start.1 = ((f32[16,72,128]{2,1,0:T(8,128)}), f32[16,72,128]{2,1,0:T(8,128)S(1)}, u32[]{:S(2)}, u32[]{:S(2)}) async-start(f32[16,72,128]{2,1,0:T(8,128)} %bitcast.4), calls=%async_computation.1 | async-start | bytes 1179648 | tf_op jit(solution)/shard_map/all_to_all | solution.py:369
  62.8 1.3 %collective-permute-start.6 = (f32[48,256]{1,0:T(8,128)S(1)}, f32[48,256]{1,0:T(8,128)S(1)}, u32[]{:S(2)}, u32[]{:S(2)}) collective-permute-start(f32[48,256]{1,0:T(8,128)S(1)} %shard_map.78), channel_id=1, source_target_pairs={{0,1},{1,0},{2,3},{3,2},{4,5},{5,4},{6,7},{7,6},{8,9},{9,8},{10,11... | collective-permute-start | bytes 147464 | tf_op jit(solution)/shard_map/ppermute | solution.py:27
  64.1 4.2 %collective-permute-start.7 = (f32[48,256]{1,0:T(8,128)S(1)}, f32[48,256]{1,0:T(8,128)S(1)}, u32[]{:S(2)}, u32[]{:S(2)}) collective-permute-start(f32[48,256]{1,0:T(8,128)S(1)} %add.48), channel_id=1, source_target_pairs={{0,2},{2,0},{4,6},{6,4},{8,10},{10,8},{12,14},{14,12},{1,3},{3,1},... | collective-permute-start | bytes 147464 | tf_op jit(solution)/shard_map/ppermute | solution.py:27
  68.3 4.2 %collective-permute-start.8 = (f32[48,256]{1,0:T(8,128)S(1)}, f32[48,256]{1,0:T(8,128)S(1)}, u32[]{:S(2)}, u32[]{:S(2)}) collective-permute-start(f32[48,256]{1,0:T(8,128)S(1)} %add.49), channel_id=1, source_target_pairs={{0,4},{2,6},{4,0},{6,2},{8,12},{10,14},{12,8},{14,10},{1,5},{3,7},... | collective-permute-start | bytes 147464 | tf_op jit(solution)/shard_map/ppermute | solution.py:27
  72.4 5.1 %collective-permute-start.9 = (f32[48,256]{1,0:T(8,128)S(1)}, f32[48,256]{1,0:T(8,128)S(1)}, u32[]{:S(2)}, u32[]{:S(2)}) collective-permute-start(f32[48,256]{1,0:T(8,128)S(1)} %add.50), channel_id=1, source_target_pairs={{0,8},{2,10},{4,12},{6,14},{8,0},{10,2},{12,4},{14,6},{1,9},{3,11}... | collective-permute-start | bytes 147464 | tf_op jit(solution)/shard_map/ppermute | solution.py:27
  81.0 20.4 %all-to-all-start.2 = ((f32[16,24,128]{2,1,0:T(8,128)}), f32[16,24,128]{2,1,0:T(8,128)S(1)}, u32[]{:S(2)}, u32[]{:S(2)}) async-start(f32[16,24,128]{2,1,0:T(8,128)} %bitcast.7), calls=%async_computation.2 | async-start | bytes 393216 | tf_op jit(solution)/shard_map/all_to_all | solution.py:369
  85.9 1.4 %collective-permute-start.10 = (f32[48,192]{1,0:T(8,128)S(1)}, f32[48,192]{1,0:T(8,128)S(1)}, u32[]{:S(2)}, u32[]{:S(2)}) collective-permute-start(f32[48,192]{1,0:T(8,128)S(1)} %get-tuple-element.20), channel_id=1, source_target_pairs={{0,1},{1,0},{2,3},{3,2},{4,5},{5,4},{6,7},{7,6},{8,9},{9,8},{10,11... | collective-permute-start | bytes 110600 | tf_op jit(solution)/shard_map/ppermute | solution.py:27
  87.3 4.7 %collective-permute-start.11 = (f32[48,192]{1,0:T(8,128)S(1)}, f32[48,192]{1,0:T(8,128)S(1)}, u32[]{:S(2)}, u32[]{:S(2)}) collective-permute-start(f32[48,192]{1,0:T(8,128)S(1)} %add.52), channel_id=1, source_target_pairs={{0,2},{2,0},{4,6},{6,4},{8,10},{10,8},{12,14},{14,12},{1,3},{3,1},... | collective-permute-start | bytes 110600 | tf_op jit(solution)/shard_map/ppermute | solution.py:27
  92.0 4.2 %collective-permute-start.12 = (f32[48,192]{1,0:T(8,128)S(1)}, f32[48,192]{1,0:T(8,128)S(1)}, u32[]{:S(2)}, u32[]{:S(2)}) collective-permute-start(f32[48,192]{1,0:T(8,128)S(1)} %add.53), channel_id=1, source_target_pairs={{0,4},{2,6},{4,0},{6,2},{8,12},{10,14},{12,8},{14,10},{1,5},{3,7},... | collective-permute-start | bytes 110600 | tf_op jit(solution)/shard_map/ppermute | solution.py:27
  96.3 5.1 %collective-permute-start.13 = (f32[48,192]{1,0:T(8,128)S(1)}, f32[48,192]{1,0:T(8,128)S(1)}, u32[]{:S(2)}, u32[]{:S(2)}) collective-permute-start(f32[48,192]{1,0:T(8,128)S(1)} %add.54), channel_id=1, source_target_pairs={{0,8},{2,10},{4,12},{6,14},{8,0},{10,2},{12,4},{14,6},{1,9},{3,11}... | collective-permute-start | bytes 110600 | tf_op jit(solution)/shard_map/ppermute | solution.py:27

commit v4 on v3

--- a/solution.py
+++ b/solution.py
@@ -18,14 +18,29 @@
     return jnp.einsum(form, left, right, precision=precision)
 
 
-def total(part, axis):
-    size = lax.axis_size(axis)
-    if size & (size - 1):
-        return lax.psum(part, axis)
-    step = 1
-    while step < size:
-        part = part + lax.ppermute(part, axis, [(at, at ^ step) for at in range(size)])
-        step *= 2
+def total(part):
+    narrow = lax.axis_size("narrow")
+    count = lax.axis_size("wide") * narrow
+    if narrow != 2 or count & (count - 1):
+        return lax.psum(part, group)
+
+    def moved(mask):
+        return lax.ppermute(part, group, [(at, at ^ mask) for at in range(count)])
+
+    part = part + moved(1)
+    bits = []
+    while narrow < count:
+        bits.append(narrow)
+        narrow *= 2
+    single = len(bits) % 2
+    parts = [bits[:single]] if single else []
+    parts += [bits[at : at + 2] for at in range(single, len(bits), 2)]
+    for low, *high in parts:
+        if high:
+            near, far, both = moved(low + 1), moved(high[0] + 1), moved(low + high[0] + 1)
+            part = (part + near) + (far + both)
+        else:
+            part = part + moved(low + 1)
     return part
 
 
@@ -147,7 +162,7 @@
     unfold = contract("wnbki,wkc->bcni", got, three)
     weights = contract("bcni,nia->bca", unfold, one)
     product = contract("bcni,bca->ani", unfold, weights).reshape(rank, narrow * rows)
-    product = total(total(product, "narrow"), "wide")
+    product = total(product)
     one_t = call(orthonormal_body, [product.shape], product)[0]
 
     one_pad = jnp.pad(one_t, ((0, spare), (0, 0)))
@@ -161,13 +176,13 @@
     unfold = contract("dakj,dkc->acj", got, three)
     weights = contract("acj,jb->acb", unfold, factor_two)
     product = contract("acj,acb->bj", unfold, weights)
-    product = total(total(product, "narrow"), "wide")
+    product = total(product)
     two_t = call(orthonormal_body, [product.shape], product)[0]
 
     unfold = contract("dakj,bj->dakb", got, two_t)
     weights = contract("dakb,dkc->abc", unfold, three)
     product = contract("dakb,abc->cdk", unfold, weights).reshape(rank, count * half)
-    product = total(total(product, "narrow"), "wide")
+    product = total(product)
     three_t = call(orthonormal_body, [product.shape], product)[0]
     core = contract("dakb,cdk->abc", unfold, three_t.reshape(rank, count, half))
     core = core.reshape(share, count, rank * rank // count).transpose(1, 0, 2)
@@ -407,10 +422,11 @@
     got = exchange(packed, count)
     field, _ = lax.optimization_barrier((window_data, packed))
     other = swap(lax.dynamic_slice_in_dim(field, (1 - core_at) * half, half, 0))
+    got, other = lax.optimization_barrier((got, other))
     product, three = call(
         stage(work_one), [(rank, 2 * rows), (size, rank)], got, factor_one, swap(factor_one)
     )
-    product = total(total(product, "narrow"), "wide")
+    product = total(product)
 
     parts = cols // lanes
     one_t, packed = call(
@@ -427,7 +443,7 @@
     )
     got = exchange(packed, count)
     (product,) = call(stage(work_two), [(rank, cols)], got, factor_two, three)
-    product = total(total(product, "narrow"), "wide")
+    product = total(product)
 
     pitch = -(-share * share * -(-size // lanes) // 8) * 8
     two_t, product, sent = call(
@@ -439,7 +455,7 @@
         scratch_shapes=[pltpu.VMEM((parts * rank, lanes), jnp.float32)],
     )
     got = exchange(sent, count)
-    product = total(total(product, "narrow"), "wide")
+    product = total(product)
     basis_three, core = call(
         stage(finish),
         [(depth, rank), (rank, share * rank)],

time: 104 us -> 98.5 us (0.947)
  waiting for transfers between devices: 51.4 us -> 47.2 us
  starting transfers between devices: 33.4 us -> 32 us
    ppermute x12 -> x15, waiting for transfers between devices: 25.5 us -> 20.2 us  [moved(): return lax.ppermute(part, group, [(at, at ^ mask) for at in range(count)])]
    all_to_all x3, waiting for transfers between devices: 23.9 us -> 26.9 us  [exchange(): return lax.all_to_all(value, group, 0, 0, tiled=True).reshape(rows, lanes)]
    ppermute x2, waiting for transfers between devices: 1.95 us -> 0.01 us  [swap(): return lax.ppermute(value, 'narrow', [(0, 1), (1, 0)])]
    ppermute x12 -> x15, starting transfers between devices: 16.7 us -> 15.8 us  [moved(): return lax.ppermute(part, group, [(at, at ^ mask) for at in range(count)])]
  transfers between devices with their start and end apart: 17 -> 20, of which waited for: 15 -> 14; matrix products, arithmetic and copies ran while one was open for 2% -> 2% of each run, Pallas kernels for 1% -> 0%
where the time goes in v4:
time: 98.5 us; the launch traced here: 97.5 us
  waiting for transfers between devices  47.2 us (48%)
  starting transfers between devices  32 us (32%)
  Pallas kernels  15 us (15%)
  local copies, waits for them, and re-layouts  2.46 us (2%)
    all_to_all x3, waiting for transfers between devices, exchange(): return lax.all_to_all(value, group, 0, 0, tiled=True).reshape(rows, lanes)  26.9 us
    ppermute x15, waiting for transfers between devices, moved(): return lax.ppermute(part, group, [(at, at ^ mask) for at in range(count)])  20.2 us
    ppermute x15, starting transfers between devices, moved(): return lax.ppermute(part, group, [(at, at ^ mask) for at in range(count)])  15.8 us
    all_to_all x3, starting transfers between devices, exchange(): return lax.all_to_all(value, group, 0, 0, tiled=True).reshape(rows, lanes)  15.3 us
    pallas_call x6, Pallas kernels, call(): pl.pallas_call(body, in_specs=[away if at in far else near for at in rang...  15 us
  transfers between devices with their start and end apart: 20, of which 14 were waited for; matrix products, arithmetic and copies ran while one was open for 2% of the time, Pallas kernels for 0%

profile of v4, /device:TPU:0, one launch (start us, length us, event | category | flops | bytes accessed | tf_op | source)
XLA Modules:
  0.0 97.5 jit_solution(5749059372737848636)
XLA Ops:
  0.6 0.0 copy-start
  0.6 3.0 %shard_map.75 = f32[768,128]{1,0:T(8,128)} custom-call(f32[24,64,256]{2,1,0:T(8,128)} %refs_1_.3, f32[48,256]{1,0:T(8,128)} %bitcast.15, f32[24,48]{1,0:T(8,128)} %refs_2_.1), custom_call_target="tpu_custom_call" | custom-call | tf_op jit(solution)/shard_map/pallas_call | solution.py:123
  3.7 0.0 copy-start.3
  3.7 1.0 constant_dynamic-slice_fusion
  4.7 0.5 collective-permute-start
  5.2 7.0 %all-to-all-start = ((f32[16,48,128]{2,1,0:T(8,128)}), f32[16,48,128]{2,1,0:T(8,128)S(1)}, u32[]{:S(2)}, u32[]{:S(2)}) async-start(f32[16,48,128]{2,1,0:T(8,128)} %bitcast.1), calls=%async_computation | async-start | bytes 786432 | tf_op jit(solution)/shard_map/all_to_all | solution.py:384
  12.2 0.1 copy.9.refs_1_
  12.3 0.4 collective-permute-start.1
  12.8 11.6 %all-to-all-done = f32[16,48,128]{2,1,0:T(8,128)S(1)} async-done(((f32[16,48,128]{2,1,0:T(8,128)}), f32[16,48,128]{2,1,0:T(8,128)S(1)}, u32[]{:S(2)}, u32[]{:S(2)}) %all-to-all-start) | async-done | bytes 393248 | tf_op jit(solution)/shard_map/all_to_all | solution.py:384
  24.4 0.0 collective-permute-done.refs_2_
  24.4 1.1 %shard_map.76 = (f32[48,128]{1,0:T(8,128)S(1)}, f32[192,48]{1,0:T(8,128)S(1)}) custom-call(f32[768,128]{1,0:T(8,128)S(1)} %bitcast.13, f32[64,48]{1,0:T(8,128)S(1)} %copy.9.refs_1_, f32[64,48]{1,0:T(8,128)S(1)} %collective-permute-done.1.refs_2_), custom_call_target="tpu_custom_call" | custom-call | tf_op jit(solution)/shard_map/pallas_call | solution.py:123
  25.5 0.1 collective-permute-start.2
  25.6 1.1 %collective-permute-done.2 = f32[48,128]{1,0:T(8,128)S(1)} collective-permute-done((f32[48,128]{1,0:T(8,128)S(1)}, f32[48,128]{1,0:T(8,128)S(1)}, u32[]{:S(2)}, u32[]{:S(2)}) %collective-permute-start.2) | collective-permute-done | bytes 24608 | tf_op jit(solution)/shard_map/ppermute | solution.py:28
  26.7 0.6 collective-permute-start.3
  27.3 2.6 %collective-permute-done.3 = f32[48,128]{1,0:T(8,128)S(1)} collective-permute-done((f32[48,128]{1,0:T(8,128)S(1)}, f32[48,128]{1,0:T(8,128)S(1)}, u32[]{:S(2)}, u32[]{:S(2)}) %collective-permute-start.3) | collective-permute-done | bytes 24608 | tf_op jit(solution)/shard_map/ppermute | solution.py:28
  30.0 0.9 collective-permute-start.4
  30.9 0.8 collective-permute-start.5
  31.7 2.2 %collective-permute-start.6 = (f32[48,128]{1,0:T(8,128)S(1)}, f32[48,128]{1,0:T(8,128)S(1)}, u32[]{:S(2)}, u32[]{:S(2)}) collective-permute-start(f32[48,128]{1,0:T(8,128)S(1)} %add.53), channel_id=1, source_target_pairs={{0,13},{1,12},{2,15},{3,14},{4,9},{5,8},{6,11},{7,10},{8,5},{9,4},... | collective-permute-start | bytes 73736 | tf_op jit(solution)/shard_map/ppermute | solution.py:28
  33.9 1.2 %collective-permute-done.5 = f32[48,128]{1,0:T(8,128)S(1)} collective-permute-done((f32[48,128]{1,0:T(8,128)S(1)}, f32[48,128]{1,0:T(8,128)S(1)}, u32[]{:S(2)}, u32[]{:S(2)}) %collective-permute-start.5) | collective-permute-done | bytes 24608 | tf_op jit(solution)/shard_map/ppermute | solution.py:28
  35.0 1.7 %collective-permute-done.6 = f32[48,128]{1,0:T(8,128)S(1)} collective-permute-done((f32[48,128]{1,0:T(8,128)S(1)}, f32[48,128]{1,0:T(8,128)S(1)}, u32[]{:S(2)}, u32[]{:S(2)}) %collective-permute-start.6) | collective-permute-done | bytes 24608 | tf_op jit(solution)/shard_map/ppermute | solution.py:28
  36.8 0.0 copy-start.2
  36.8 4.0 %shard_map.77 = (f32[48,128]{1,0:T(8,128)S(1)}, f32[1152,128]{1,0:T(8,128)}) custom-call(f32[48,128]{1,0:T(8,128)S(1)} %add_add_fusion.2.refs_0_, f32[24,64,256]{2,1,0:T(8,128)} %refs_1_.3, f32[12,64,256]{2,1,0:T(8,128)} %copy-done.1), custom_call_target="tpu_custom_call" | custom-call | tf_op jit(solution)/shard_map/pallas_call | solution.py:123
  40.8 3.9 %all-to-all-start.1 = ((f32[16,72,128]{2,1,0:T(8,128)}), f32[16,72,128]{2,1,0:T(8,128)S(1)}, u32[]{:S(2)}, u32[]{:S(2)}) async-start(f32[16,72,128]{2,1,0:T(8,128)} %bitcast.4), calls=%async_computation.1 | async-start | bytes 1179648 | tf_op jit(solution)/shard_map/all_to_all | solution.py:384
  44.7 0.1 copy.10.refs_1_
  44.8 15.3 %all-to-all-done.1 = f32[16,72,128]{2,1,0:T(8,128)S(1)} async-done(((f32[16,72,128]{2,1,0:T(8,128)}), f32[16,72,128]{2,1,0:T(8,128)S(1)}, u32[]{:S(2)}, u32[]{:S(2)}) %all-to-all-start.1) | async-done | bytes 589856 | tf_op jit(solution)/shard_map/all_to_all | solution.py:384
  60.1 0.7 shard_map.78
  60.8 0.3 collective-permute-start.7
  61.1 1.0 %collective-permute-done.7 = f32[48,256]{1,0:T(8,128)S(1)} collective-permute-done((f32[48,256]{1,0:T(8,128)S(1)}, f32[48,256]{1,0:T(8,128)S(1)}, u32[]{:S(2)}, u32[]{:S(2)}) %collective-permute-start.7) | collective-permute-done | bytes 49184 | tf_op jit(solution)/shard_map/ppermute | solution.py:28
  62.1 1.3 %collective-permute-start.8 = (f32[48,256]{1,0:T(8,128)S(1)}, f32[48,256]{1,0:T(8,128)S(1)}, u32[]{:S(2)}, u32[]{:S(2)}) collective-permute-start(f32[48,256]{1,0:T(8,128)S(1)} %add.58), channel_id=1, source_target_pairs={{0,3},{1,2},{2,1},{3,0},{4,7},{5,6},{6,5},{7,4},{8,11},{9,10},{10,... | collective-permute-start | bytes 147464 | tf_op jit(solution)/shard_map/ppermute | solution.py:28
  63.4 2.4 %collective-permute-done.8 = f32[48,256]{1,0:T(8,128)S(1)} collective-permute-done((f32[48,256]{1,0:T(8,128)S(1)}, f32[48,256]{1,0:T(8,128)S(1)}, u32[]{:S(2)}, u32[]{:S(2)}) %collective-permute-start.8) | collective-permute-done | bytes 49184 | tf_op jit(solution)/shard_map/ppermute | solution.py:28
  65.8 2.6 %collective-permute-start.10 = (f32[48,256]{1,0:T(8,128)S(1)}, f32[48,256]{1,0:T(8,128)S(1)}, u32[]{:S(2)}, u32[]{:S(2)}) collective-permute-start(f32[48,256]{1,0:T(8,128)S(1)} %add.59), channel_id=1, source_target_pairs={{0,9},{1,8},{2,11},{3,10},{4,13},{5,12},{6,15},{7,14},{8,1},{9,0},... | collective-permute-start | bytes 147464 | tf_op jit(solution)/shard_map/ppermute | solution.py:28
  68.5 1.2 %collective-permute-start.11 = (f32[48,256]{1,0:T(8,128)S(1)}, f32[48,256]{1,0:T(8,128)S(1)}, u32[]{:S(2)}, u32[]{:S(2)}) collective-permute-start(f32[48,256]{1,0:T(8,128)S(1)} %add.59), channel_id=1, source_target_pairs={{0,13},{1,12},{2,15},{3,14},{4,9},{5,8},{6,11},{7,10},{8,5},{9,4},... | collective-permute-start | bytes 147464 | tf_op jit(solution)/shard_map/ppermute | solution.py:28
  69.7 0.7 collective-permute-done.10
  70.3 3.5 %collective-permute-done.11 = f32[48,256]{1,0:T(8,128)S(1)} collective-permute-done((f32[48,256]{1,0:T(8,128)S(1)}, f32[48,256]{1,0:T(8,128)S(1)}, u32[]{:S(2)}, u32[]{:S(2)}) %collective-permute-start.11) | collective-permute-done | bytes 49184 | tf_op jit(solution)/shard_map/ppermute | solution.py:28
  73.9 3.5 %shard_map.79 = (f32[48,256]{1,0:T(8,128)S(1)}, f32[48,192]{1,0:T(8,128)S(1)}, f32[384,128]{1,0:T(8,128)}) custom-call(f32[48,256]{1,0:T(8,128)S(1)} %add_add_fusion.1.refs_0_, f32[1152,128]{1,0:T(8,128)S(1)} %bitcast.12, f32[192,48]{1,0:T(8,128)S(1)} %get-tuple-element.22.refs_2_), custom_call_target="tpu_custom_call" | custom-call | tf_op jit(solution)/shard_map/pallas_call | solution.py:123
  77.4 0.8 collective-permute-start.12
  78.1 0.9 collective-permute-done.12
  79.0 0.8 collective-permute-start.13
  79.9 4.3 %all-to-all-start.2 = ((f32[16,24,128]{2,1,0:T(8,128)}), f32[16,24,128]{2,1,0:T(8,128)S(1)}, u32[]{:S(2)}, u32[]{:S(2)}) async-start(f32[16,24,128]{2,1,0:T(8,128)} %bitcast.7), calls=%async_computation.2 | async-start | bytes 393216 | tf_op jit(solution)/shard_map/all_to_all | solution.py:384
  84.2 1.7 %collective-permute-start.14 = (f32[48,192]{1,0:T(8,128)S(1)}, f32[48,192]{1,0:T(8,128)S(1)}, u32[]{:S(2)}, u32[]{:S(2)}) collective-permute-start(f32[48,192]{1,0:T(8,128)S(1)} %add.64), channel_id=1, source_target_pairs={{0,5},{1,4},{2,7},{3,6},{4,1},{5,0},{6,3},{7,2},{8,13},{9,12},{10,... | collective-permute-start | bytes 110600 | tf_op jit(solution)/shard_map/ppermute | solution.py:28
  85.9 2.4 %collective-permute-start.15 = (f32[48,192]{1,0:T(8,128)S(1)}, f32[48,192]{1,0:T(8,128)S(1)}, u32[]{:S(2)}, u32[]{:S(2)}) collective-permute-start(f32[48,192]{1,0:T(8,128)S(1)} %add.64), channel_id=1, source_target_pairs={{0,9},{1,8},{2,11},{3,10},{4,13},{5,12},{6,15},{7,14},{8,1},{9,0},... | collective-permute-start | bytes 110600 | tf_op jit(solution)/shard_map/ppermute | solution.py:28
  88.3 0.1 collective-permute-start.16
  88.4 0.7 dynamic-slice_bitcast_fusion
  89.1 0.6 copy.11
  89.7 0.4 collective-permute-done.14
  90.1 3.0 %collective-permute-done.15 = f32[48,192]{1,0:T(8,128)S(1)} collective-permute-done((f32[48,192]{1,0:T(8,128)S(1)}, f32[48,192]{1,0:T(8,128)S(1)}, u32[]{:S(2)}, u32[]{:S(2)}) %collective-permute-start.15) | collective-permute-done | bytes 36896 | tf_op jit(solution)/shard_map/ppermute | solution.py:28
  93.0 1.8 %collective-permute-done.16 = f32[48,192]{1,0:T(8,128)S(1)} collective-permute-done((f32[48,192]{1,0:T(8,128)S(1)}, f32[48,192]{1,0:T(8,128)S(1)}, u32[]{:S(2)}, u32[]{:S(2)}) %collective-permute-start.16) | collective-permute-done | bytes 36896 | tf_op jit(solution)/shard_map/ppermute | solution.py:28
  94.9 2.6 %shard_map.80 = (f32[24,48]{1,0:T(8,128)}, f32[48,144]{1,0:T(8,128)}) custom-call(f32[48,192]{1,0:T(8,128)S(1)} %add_add_fusion.refs_0_, f32[384,128]{1,0:T(8,128)S(1)} %bitcast.14), custom_call_target="tpu_custom_call" | custom-call | tf_op jit(solution)/shard_map/pallas_call | solution.py:123
  (20 shorter events, 0.1 us)
Async XLA Ops:
  0.6 3.1 %copy-start = (f32[24,64,256]{2,1,0:T(8,128)S(1)}, f32[24,64,256]{2,1,0:T(8,128)}, u32[]{:S(2)}) copy-start(f32[24,64,256]{2,1,0:T(8,128)} %refs_1_.3) | copy-start | bytes 4718596
  3.7 8.5 %copy-start.3 = (f32[64,48]{0,1:T(8,128)S(1)}, f32[64,48]{0,1:T(8,128)}, u32[]{:S(2)}) copy-start(f32[64,48]{0,1:T(8,128)} %param.5) | copy-start | bytes 36868
  4.7 19.7 %collective-permute-start = (f32[12,64,256]{2,1,0:T(8,128)}, f32[12,64,256]{2,1,0:T(8,128)S(1)}, u32[]{:S(2)}, u32[]{:S(2)}) collective-permute-start(f32[12,64,256]{2,1,0:T(8,128)} %constant_dynamic-slice_fusion), channel_id=1, source_target_pairs={{0,1},{1,0},{2,3},{3,2},{4,5},{5,4},{6,7},{7,6},{8,9},{9,8},{10,11... | collective-permute-start | bytes 2359304 | tf_op jit(solution)/shard_map/ppermute | solution.py:48
  5.2 19.2 %all-to-all-start = ((f32[16,48,128]{2,1,0:T(8,128)}), f32[16,48,128]{2,1,0:T(8,128)S(1)}, u32[]{:S(2)}, u32[]{:S(2)}) async-start(f32[16,48,128]{2,1,0:T(8,128)} %bitcast.1), calls=%async_computation | async-start | bytes 786432 | tf_op jit(solution)/shard_map/all_to_all | solution.py:384
  12.3 12.1 %collective-permute-start.1 = (f32[64,48]{1,0:T(8,128)S(1)}, f32[64,48]{1,0:T(8,128)S(1)}, u32[]{:S(2)}, u32[]{:S(2)}) collective-permute-start(f32[64,48]{1,0:T(8,128)S(1)} %copy.9.refs_1_), channel_id=1, source_target_pairs={{0,1},{1,0},{2,3},{3,2},{4,5},{5,4},{6,7},{7,6},{8,9},{9,8},{10,11... | collective-permute-start | bytes 36872 | tf_op jit(solution)/shard_map/ppermute | solution.py:48
  24.4 12.4 %copy-start.1 = (f32[12,64,256]{2,1,0:T(8,128)}, f32[12,64,256]{2,1,0:T(8,128)S(1)}, u32[]{:S(2)}) copy-start(f32[12,64,256]{2,1,0:T(8,128)S(1)} %collective-permute-done.refs_2_) | copy-start | bytes 2359300
  25.5 1.2 %collective-permute-start.2 = (f32[48,128]{1,0:T(8,128)S(1)}, f32[48,128]{1,0:T(8,128)S(1)}, u32[]{:S(2)}, u32[]{:S(2)}) collective-permute-start(f32[48,128]{1,0:T(8,128)S(1)} %get-tuple-element.18), channel_id=1, source_target_pairs={{0,1},{1,0},{2,3},{3,2},{4,5},{5,4},{6,7},{7,6},{8,9},{9,8},{10,11... | collective-permute-start | bytes 73736 | tf_op jit(solution)/shard_map/ppermute | solution.py:28
  26.7 3.3 %collective-permute-start.3 = (f32[48,128]{1,0:T(8,128)S(1)}, f32[48,128]{1,0:T(8,128)S(1)}, u32[]{:S(2)}, u32[]{:S(2)}) collective-permute-start(f32[48,128]{1,0:T(8,128)S(1)} %add.52), channel_id=1, source_target_pairs={{0,3},{1,2},{2,1},{3,0},{4,7},{5,6},{6,5},{7,4},{8,11},{9,10},{10,... | collective-permute-start | bytes 73736 | tf_op jit(solution)/shard_map/ppermute | solution.py:28
  30.0 3.9 %collective-permute-start.4 = (f32[48,128]{1,0:T(8,128)S(1)}, f32[48,128]{1,0:T(8,128)S(1)}, u32[]{:S(2)}, u32[]{:S(2)}) collective-permute-start(f32[48,128]{1,0:T(8,128)S(1)} %add.53), channel_id=1, source_target_pairs={{0,5},{1,4},{2,7},{3,6},{4,1},{5,0},{6,3},{7,2},{8,13},{9,12},{10,... | collective-permute-start | bytes 73736 | tf_op jit(solution)/shard_map/ppermute | solution.py:28
  30.9 4.2 %collective-permute-start.5 = (f32[48,128]{1,0:T(8,128)S(1)}, f32[48,128]{1,0:T(8,128)S(1)}, u32[]{:S(2)}, u32[]{:S(2)}) collective-permute-start(f32[48,128]{1,0:T(8,128)S(1)} %add.53), channel_id=1, source_target_pairs={{0,9},{1,8},{2,11},{3,10},{4,13},{5,12},{6,15},{7,14},{8,1},{9,0},... | collective-permute-start | bytes 73736 | tf_op jit(solution)/shard_map/ppermute | solution.py:28
  31.7 5.1 %collective-permute-start.6 = (f32[48,128]{1,0:T(8,128)S(1)}, f32[48,128]{1,0:T(8,128)S(1)}, u32[]{:S(2)}, u32[]{:S(2)}) collective-permute-start(f32[48,128]{1,0:T(8,128)S(1)} %add.53), channel_id=1, source_target_pairs={{0,13},{1,12},{2,15},{3,14},{4,9},{5,8},{6,11},{7,10},{8,5},{9,4},... | collective-permute-start | bytes 73736 | tf_op jit(solution)/shard_map/ppermute | solution.py:28
  36.8 7.9 %copy-start.2 = (f32[256,48]{0,1:T(8,128)S(1)}, f32[256,48]{0,1:T(8,128)}, u32[]{:S(2)}) copy-start(f32[256,48]{0,1:T(8,128)} %param.6) | copy-start | bytes 147460
  40.8 19.3 %all-to-all-start.1 = ((f32[16,72,128]{2,1,0:T(8,128)}), f32[16,72,128]{2,1,0:T(8,128)S(1)}, u32[]{:S(2)}, u32[]{:S(2)}) async-start(f32[16,72,128]{2,1,0:T(8,128)} %bitcast.4), calls=%async_computation.1 | async-start | bytes 1179648 | tf_op jit(solution)/shard_map/all_to_all | solution.py:384
  60.8 1.3 %collective-permute-start.7 = (f32[48,256]{1,0:T(8,128)S(1)}, f32[48,256]{1,0:T(8,128)S(1)}, u32[]{:S(2)}, u32[]{:S(2)}) collective-permute-start(f32[48,256]{1,0:T(8,128)S(1)} %shard_map.78), channel_id=1, source_target_pairs={{0,1},{1,0},{2,3},{3,2},{4,5},{5,4},{6,7},{7,6},{8,9},{9,8},{10,11... | collective-permute-start | bytes 147464 | tf_op jit(solution)/shard_map/ppermute | solution.py:28
  62.1 3.7 %collective-permute-start.8 = (f32[48,256]{1,0:T(8,128)S(1)}, f32[48,256]{1,0:T(8,128)S(1)}, u32[]{:S(2)}, u32[]{:S(2)}) collective-permute-start(f32[48,256]{1,0:T(8,128)S(1)} %add.58), channel_id=1, source_target_pairs={{0,3},{1,2},{2,1},{3,0},{4,7},{5,6},{6,5},{7,4},{8,11},{9,10},{10,... | collective-permute-start | bytes 147464 | tf_op jit(solution)/shard_map/ppermute | solution.py:28
  65.8 4.5 %collective-permute-start.10 = (f32[48,256]{1,0:T(8,128)S(1)}, f32[48,256]{1,0:T(8,128)S(1)}, u32[]{:S(2)}, u32[]{:S(2)}) collective-permute-start(f32[48,256]{1,0:T(8,128)S(1)} %add.59), channel_id=1, source_target_pairs={{0,9},{1,8},{2,11},{3,10},{4,13},{5,12},{6,15},{7,14},{8,1},{9,0},... | collective-permute-start | bytes 147464 | tf_op jit(solution)/shard_map/ppermute | solution.py:28
  68.5 5.4 %collective-permute-start.11 = (f32[48,256]{1,0:T(8,128)S(1)}, f32[48,256]{1,0:T(8,128)S(1)}, u32[]{:S(2)}, u32[]{:S(2)}) collective-permute-start(f32[48,256]{1,0:T(8,128)S(1)} %add.59), channel_id=1, source_target_pairs={{0,13},{1,12},{2,15},{3,14},{4,9},{5,8},{6,11},{7,10},{8,5},{9,4},... | collective-permute-start | bytes 147464 | tf_op jit(solution)/shard_map/ppermute | solution.py:28
  69.7 4.2 %collective-permute-start.9 = (f32[48,256]{1,0:T(8,128)S(1)}, f32[48,256]{1,0:T(8,128)S(1)}, u32[]{:S(2)}, u32[]{:S(2)}) collective-permute-start(f32[48,256]{1,0:T(8,128)S(1)} %add.59), channel_id=1, source_target_pairs={{0,5},{1,4},{2,7},{3,6},{4,1},{5,0},{6,3},{7,2},{8,13},{9,12},{10,... | collective-permute-start | bytes 147464 | tf_op jit(solution)/shard_map/ppermute | solution.py:28
  77.4 1.7 %collective-permute-start.12 = (f32[48,192]{1,0:T(8,128)S(1)}, f32[48,192]{1,0:T(8,128)S(1)}, u32[]{:S(2)}, u32[]{:S(2)}) collective-permute-start(f32[48,192]{1,0:T(8,128)S(1)} %get-tuple-element.24), channel_id=1, source_target_pairs={{0,1},{1,0},{2,3},{3,2},{4,5},{5,4},{6,7},{7,6},{8,9},{9,8},{10,11... | collective-permute-start | bytes 110600 | tf_op jit(solution)/shard_map/ppermute | solution.py:28
  79.0 5.2 %collective-permute-start.13 = (f32[48,192]{1,0:T(8,128)S(1)}, f32[48,192]{1,0:T(8,128)S(1)}, u32[]{:S(2)}, u32[]{:S(2)}) collective-permute-start(f32[48,192]{1,0:T(8,128)S(1)} %add.63), channel_id=1, source_target_pairs={{0,3},{1,2},{2,1},{3,0},{4,7},{5,6},{6,5},{7,4},{8,11},{9,10},{10,... | collective-permute-start | bytes 110600 | tf_op jit(solution)/shard_map/ppermute | solution.py:28
  79.9 15.0 %all-to-all-start.2 = ((f32[16,24,128]{2,1,0:T(8,128)}), f32[16,24,128]{2,1,0:T(8,128)S(1)}, u32[]{:S(2)}, u32[]{:S(2)}) async-start(f32[16,24,128]{2,1,0:T(8,128)} %bitcast.7), calls=%async_computation.2 | async-start | bytes 393216 | tf_op jit(solution)/shard_map/all_to_all | solution.py:384
  84.2 5.8 %collective-permute-start.14 = (f32[48,192]{1,0:T(8,128)S(1)}, f32[48,192]{1,0:T(8,128)S(1)}, u32[]{:S(2)}, u32[]{:S(2)}) collective-permute-start(f32[48,192]{1,0:T(8,128)S(1)} %add.64), channel_id=1, source_target_pairs={{0,5},{1,4},{2,7},{3,6},{4,1},{5,0},{6,3},{7,2},{8,13},{9,12},{10,... | collective-permute-start | bytes 110600 | tf_op jit(solution)/shard_map/ppermute | solution.py:28
  85.9 7.1 %collective-permute-start.15 = (f32[48,192]{1,0:T(8,128)S(1)}, f32[48,192]{1,0:T(8,128)S(1)}, u32[]{:S(2)}, u32[]{:S(2)}) collective-permute-start(f32[48,192]{1,0:T(8,128)S(1)} %add.64), channel_id=1, source_target_pairs={{0,9},{1,8},{2,11},{3,10},{4,13},{5,12},{6,15},{7,14},{8,1},{9,0},... | collective-permute-start | bytes 110600 | tf_op jit(solution)/shard_map/ppermute | solution.py:28
  88.3 6.5 %collective-permute-start.16 = (f32[48,192]{1,0:T(8,128)S(1)}, f32[48,192]{1,0:T(8,128)S(1)}, u32[]{:S(2)}, u32[]{:S(2)}) collective-permute-start(f32[48,192]{1,0:T(8,128)S(1)} %add.64), channel_id=1, source_target_pairs={{0,13},{1,12},{2,15},{3,14},{4,9},{5,8},{6,11},{7,10},{8,5},{9,4},... | collective-permute-start | bytes 110600 | tf_op jit(solution)/shard_map/ppermute | solution.py:28

commit v5 on v4

--- a/solution.py
+++ b/solution.py
@@ -112,19 +112,26 @@
     out[...] = orthonormal(part[...])
 
 
-def call(body, shapes, *operands, far=(), out_far=False, **settings):
-    near = pl.BlockSpec(memory_space=pltpu.VMEM)
-    away = pl.BlockSpec(memory_space=pl.ANY)
+def near(*shape, dtype=jnp.float32):
+    return pltpu.VMEM(shape, dtype)
+
+
+def far(*shape, dtype=jnp.float32):
+    return jax.ShapeDtypeStruct(shape, dtype)
+
+
+def call(body, shapes, *operands, away=(), away_out=(), **settings):
+    inside = pl.BlockSpec(memory_space=pltpu.VMEM)
+    outside = pl.BlockSpec(memory_space=pl.ANY)
     placed = [
-        x if at in far else pltpu.with_memory_space_constraint(x, pltpu.VMEM)
+        x if at in away else pltpu.with_memory_space_constraint(x, pltpu.VMEM)
         for at, x in enumerate(operands)
     ]
-    kind = jax.ShapeDtypeStruct if out_far else pltpu.VMEM
     return pl.pallas_call(
         body,
-        in_specs=[away if at in far else near for at in range(len(operands))],
-        out_specs=[near] * len(shapes),
-        out_shape=[kind(shape, jnp.float32) for shape in shapes],
+        in_specs=[outside if at in away else inside for at in range(len(operands))],
+        out_specs=[outside if at in away_out else inside for at in range(len(shapes))],
+        out_shape=shapes,
         **settings,
     )(*placed)
 
@@ -163,7 +170,7 @@
     weights = contract("bcni,nia->bca", unfold, one)
     product = contract("bcni,bca->ani", unfold, weights).reshape(rank, narrow * rows)
     product = total(product)
-    one_t = call(orthonormal_body, [product.shape], product)[0]
+    one_t = call(orthonormal_body, [near(*product.shape)], product)[0]
 
     one_pad = jnp.pad(one_t, ((0, spare), (0, 0)))
     one_own = lax.dynamic_slice_in_dim(one_pad, core_at * rows, rows, 1)
@@ -177,13 +184,13 @@
     weights = contract("acj,jb->acb", unfold, factor_two)
     product = contract("acj,acb->bj", unfold, weights)
     product = total(product)
-    two_t = call(orthonormal_body, [product.shape], product)[0]
+    two_t = call(orthonormal_body, [near(*product.shape)], product)[0]
 
     unfold = contract("dakj,bj->dakb", got, two_t)
     weights = contract("dakb,dkc->abc", unfold, three)
     product = contract("dakb,abc->cdk", unfold, weights).reshape(rank, count * half)
     product = total(product)
-    three_t = call(orthonormal_body, [product.shape], product)[0]
+    three_t = call(orthonormal_body, [near(*product.shape)], product)[0]
     core = contract("dakb,cdk->abc", unfold, three_t.reshape(rank, count, half))
     core = core.reshape(share, count, rank * rank // count).transpose(1, 0, 2)
     core = lax.all_to_all(core, group, 0, 0, tiled=True)
@@ -192,18 +199,30 @@
     return (one_own[:rank].T, two_t.T, basis_three, core)
 
 
-def pack_one(field, two_far, three_far, out, room, two, three, arrived, landed, *, share, half, count):
+def pack_one(field, two_far, three_far, out, sent, room, flat, two, three, sems, *, share, half, count):
     chunks, _, steps, rows, cols = room.shape
     rank = two.shape[0]
     slots = share + 1
+    at_core = lax.axis_index("narrow")
+    tall = steps * slots
 
     def fetch(at, h):
         source = field.at[pl.ds(h * half + at * steps, steps)]
-        return pltpu.make_async_copy(source, room.at[at, h], arrived.at[at, h])
+        return pltpu.make_async_copy(source, room.at[at, h], sems.at[2 * at + h])
+
+    def leave(at):
+        source = flat.reshape(count, half * slots, lanes).at[:, at * tall : (at + 1) * tall]
+        return pltpu.make_async_copy(
+            source, out.at[:, at * tall : (at + 1) * tall], sems.at[2 * chunks + at]
+        )
+
+    def hand(at):
+        target = sent.at[pl.ds(at * steps, steps)]
+        return pltpu.make_async_copy(room.at[at, 1 - at_core], target, sems.at[3 * chunks + at])
 
     copies = [
-        pltpu.make_async_copy(three_far, three, landed.at[0]),
-        pltpu.make_async_copy(two_far, two, landed.at[1]),
+        pltpu.make_async_copy(three_far, three, sems.at[4 * chunks]),
+        pltpu.make_async_copy(two_far, two, sems.at[4 * chunks + 1]),
     ]
     for copy in copies:
         copy.start()
@@ -216,13 +235,14 @@
     empty = jnp.zeros((half, lanes // 2 - rank), jnp.float32)
     both = jnp.concatenate([first, empty, second, empty], axis=1)
     for d in range(count):
-        out[pl.ds(d * half * slots + share, half, stride=slots), :] = both
+        flat[pl.ds(d * half * slots + share, half, stride=slots), :] = both
     copies[1].wait()
     two_high, two_low = split(two[...])
     both = jnp.concatenate([two_high, two_low])
     for at in range(chunks):
         for h in range(2):
             fetch(at, h).wait()
+        hand(at).start()
         for q in range(steps):
             high, low = split(room[at, :, q].reshape(2 * rows, cols))
             first = lax.dot_general(both, high, nt, preferred_element_type=jnp.float32)
@@ -230,9 +250,29 @@
             along = first[:rank] + (first[rank:] + second)
             for s in range(share):
                 start = (at * steps + q) * slots + s
-                out[pl.ds(start, count, stride=half * slots), :] = along[
+                flat[pl.ds(start, count, stride=half * slots), :] = along[
                     s * count : (s + 1) * count
                 ]
+        leave(at).start()
+    for at in range(chunks):
+        hand(at).wait()
+        leave(at).wait()
+
+
+def prepare(field, other, high, low, own, sem):
+    half, rows, cols = other.shape
+    at = lax.axis_index("narrow")
+    copy = pltpu.make_async_copy(field.at[pl.ds(at * half, half)], own, sem)
+    copy.start()
+
+    def put(value, core):
+        top, rest = split(value[...])
+        high[:, pl.ds(pl.multiple_of(core * rows, 16), rows), :] = top
+        low[:, pl.ds(pl.multiple_of(core * rows, 16), rows), :] = rest
+
+    put(other, 1 - at)
+    copy.wait()
+    put(own, at)
 
 
 def work_one(got, own, other, out, three, *, share, half, count):
@@ -264,38 +304,35 @@
     out[...] = dot3(dot3(unfold, one), unfold, tn)
 
 
-def pack_two(part, field, other, basis, out, room, arrived, *, share, half, count):
-    rows, cols = other.shape[1:]
-    at = lax.axis_index("narrow")
-    own = pltpu.make_async_copy(
-        field.at[pl.ds(at * half, half)],
-        room.at[:, pl.ds(pl.multiple_of(at * rows, 8), rows), :],
-        arrived.at[0],
-    )
-    rest = pltpu.make_async_copy(
-        other, room.at[:, pl.ds(pl.multiple_of((1 - at) * rows, 8), rows), :], arrived.at[1]
-    )
-    own.start()
-    rest.start()
+def pack_two(part, high, low, basis, out, flat, sems, *, share, half, count):
+    rank = part.shape[0]
+    parts = high.shape[2] // lanes
+    slots = share * parts
+    chunks = sems.shape[0]
+    tall = half // chunks * slots
+
+    def leave(at):
+        source = flat.reshape(count, half * slots, lanes).at[:, at * tall : (at + 1) * tall]
+        return pltpu.make_async_copy(source, out.at[:, at * tall : (at + 1) * tall], sems.at[at])
+
     value = orthonormal(part[...])
     basis[...] = value
-    slots = share * (cols // lanes)
     value = split(value)
     both = jnp.concatenate(value)
-    rank = part.shape[0]
-    own.wait()
-    rest.wait()
-    for k in range(half):
-        high, low = split(room[k])
-        first = lax.dot_general(both, high, nn, preferred_element_type=jnp.float32)
-        second = lax.dot_general(value[0], low, nn, preferred_element_type=jnp.float32)
-        along = first[:rank] + (first[rank:] + second)
-        for s in range(share):
-            for h in range(cols // lanes):
-                start = k * slots + s * (cols // lanes) + h
-                out[pl.ds(start, count, stride=half * slots), :] = along[
-                    s * count : (s + 1) * count, h * lanes : (h + 1) * lanes
-                ]
+    for at in range(chunks):
+        for k in range(at * half // chunks, (at + 1) * half // chunks):
+            first = lax.dot_general(both, high[k], nn, preferred_element_type=jnp.float32)
+            second = lax.dot_general(value[0], low[k], nn, preferred_element_type=jnp.float32)
+            along = first[:rank] + (first[rank:] + second)
+            for s in range(share):
+                for h in range(parts):
+                    start = k * slots + s * parts + h
+                    flat[pl.ds(start, count, stride=half * slots), :] = along[
+                        s * count : (s + 1) * count, h * lanes : (h + 1) * lanes
+                    ]
+        leave(at).start()
+    for at in range(chunks):
+        leave(at).wait()
 
 
 def taken(got, s, parts, slots, size):
@@ -304,22 +341,20 @@
     )
 
 
-def work_two(got, two, three, out, *, share, half, count):
+def work_two(got, two, three, out, high, low, *, share, half, count):
     parts = two.shape[0] // lanes
     size = count * half
     table = split(three[...])
-    unfold = split(
-        jnp.concatenate(
-            [
-                dot3(table, taken(got, s, parts, share * parts, size), tn)
-                for s in range(share)
-            ]
-        )
-    )
+    pieces = []
+    for s in range(share):
+        value = split(taken(got, s, parts, share * parts, size))
+        high[s], low[s] = value
+        pieces.append(dot3(table, value, tn))
+    unfold = split(jnp.concatenate(pieces))
     out[...] = dot3(dot3(unfold, two[...]), unfold, tn)
 
 
-def work_three(part, got, three, basis, out, sent, room, *, share, half, count):
+def work_three(part, high, low, three, basis, out, sent, room, *, share, half, count):
     rank, cols = part.shape
     parts = cols // lanes
     size = count * half
@@ -343,7 +378,7 @@
     table = split(three[...])
     result = None
     for s in range(share):
-        value = dot3(second, taken(got, s, parts, share * parts, size), nt)
+        value = dot3(second, (high[s], low[s]), nt)
         for b in range(share):
             for h in range(tall):
                 wide = min(lanes, size - h * lanes)
@@ -378,10 +413,9 @@
         core[:, b * rank : (b + 1) * rank] = dot3(jnp.concatenate(rows), value, nt)
 
 
-def exchange(value, count):
-    rows = value.shape[0]
-    value = value.reshape(count, rows // count, lanes)
-    return lax.all_to_all(value, group, 0, 0, tiled=True).reshape(rows, lanes)
+def exchange(value):
+    count, rows, _ = value.shape
+    return lax.all_to_all(value, group, 0, 0, tiled=True).reshape(count * rows, lanes)
 
 
 def special(window_data, factor_one, factor_two, factor_three):
@@ -402,67 +436,82 @@
         run.__name__ = body.__name__
         return run
 
-    chunks = 3 if half % 3 == 0 else 1
     slots = share + 1
-    (packed,) = call(
+    parts = cols // lanes
+    chunks = 3 if half % 3 == 0 and half // 3 * slots % 8 == 0 else 1
+    packed, sent = call(
         stage(pack_one),
-        [(size * slots, lanes)],
+        [far(count, half * slots, lanes), far(half, rows, cols)],
         window_data,
         factor_two.T,
         factor_three,
-        far=(0, 1, 2),
+        away=(0, 1, 2),
+        away_out=(0, 1),
         scratch_shapes=[
-            pltpu.VMEM((chunks, 2, half // chunks, rows, cols), jnp.float32),
-            pltpu.VMEM((rank, cols), jnp.float32),
-            pltpu.VMEM((depth, rank), jnp.float32),
-            pltpu.SemaphoreType.DMA((chunks, 2)),
-            pltpu.SemaphoreType.DMA((2,)),
+            near(chunks, 2, half // chunks, rows, cols),
+            near(size * slots, lanes),
+            near(rank, cols),
+            near(depth, rank),
+            pltpu.SemaphoreType.DMA((4 * chunks + 2,)),
         ],
     )
-    got = exchange(packed, count)
-    field, _ = lax.optimization_barrier((window_data, packed))
-    other = swap(lax.dynamic_slice_in_dim(field, (1 - core_at) * half, half, 0))
-    got, other = lax.optimization_barrier((got, other))
+    got = exchange(packed)
+    high, low = call(
+        prepare,
+        [near(half, 2 * rows, cols, dtype=jnp.bfloat16)] * 2,
+        window_data,
+        swap(sent),
+        away=(0,),
+        scratch_shapes=[near(half, rows, cols), pltpu.SemaphoreType.DMA],
+    )
+    one_other = swap(factor_one)
+    got, high, low = lax.optimization_barrier((got, high, low))
     product, three = call(
-        stage(work_one), [(rank, 2 * rows), (size, rank)], got, factor_one, swap(factor_one)
+        stage(work_one), [near(rank, 2 * rows), near(size, rank)], got, factor_one, one_other
     )
     product = total(product)
 
-    parts = cols // lanes
+    chunks = 3 if half % 3 == 0 and half // 3 * share * parts % 8 == 0 else 1
     one_t, packed = call(
         stage(pack_two),
-        [product.shape, (size * share * parts, lanes)],
+        [near(*product.shape), far(count, half * share * parts, lanes)],
         product,
-        window_data,
-        other,
-        far=(1, 2),
+        high,
+        low,
+        away_out=(1,),
         scratch_shapes=[
-            pltpu.VMEM((half, 2 * rows, cols), jnp.float32),
-            pltpu.SemaphoreType.DMA((2,)),
+            near(size * share * parts, lanes),
+            pltpu.SemaphoreType.DMA((chunks,)),
         ],
     )
-    got = exchange(packed, count)
-    (product,) = call(stage(work_two), [(rank, cols)], got, factor_two, three)
+    got = exchange(packed)
+    product, high, low = call(
+        stage(work_two),
+        [near(rank, cols)] + [near(share, size, cols, dtype=jnp.bfloat16)] * 2,
+        got,
+        factor_two,
+        three,
+    )
     product = total(product)
 
     pitch = -(-share * share * -(-size // lanes) // 8) * 8
     two_t, product, sent = call(
         stage(work_three),
-        [product.shape, (rank, size), (count * pitch, lanes)],
+        [near(*product.shape), near(rank, size), far(count * pitch, lanes)],
         product,
-        got,
+        high,
+        low,
         three,
-        scratch_shapes=[pltpu.VMEM((parts * rank, lanes), jnp.float32)],
-    )
-    got = exchange(sent, count)
+        scratch_shapes=[near(parts * rank, lanes)],
+    )
+    got = exchange(sent.reshape(count, pitch, lanes))
     product = total(product)
     basis_three, core = call(
         stage(finish),
-        [(depth, rank), (rank, share * rank)],
+        [far(depth, rank), far(rank, share * rank)],
         product,
         got,
-        out_far=True,
-        scratch_shapes=[pltpu.VMEM((size, rank), jnp.float32)],
+        scratch_shapes=[near(size, rank)],
     )
     basis_one = lax.dynamic_slice_in_dim(one_t, core_at * rows, rows, 1).T
     return (basis_one, two_t.T, basis_three, core)

time: 98.5 us -> 95.7 us (0.972)
  starting transfers between devices: 32 us -> 30.9 us
    all_to_all x3, waiting for transfers between devices: 26.9 us -> 25.7 us  [exchange(): lax.all_to_all(value, group, 0, 0, tiled=True).reshape(count * rows, lanes)]
    pallas_call x6 -> x7, Pallas kernels: 15 us -> 14.7 us  [call(): pl.pallas_call(body, in_specs=[outside if at in away else inside for at i...]
  transfers between devices with their start and end apart: 20 -> 20, of which waited for: 14 -> 12; matrix products, arithmetic and copies ran while one was open for 2% -> 2% of each run, Pallas kernels for 0% -> 1%
where the time goes in v5:
time: 95.7 us; the launch traced here: 94.8 us
  waiting for transfers between devices  46.8 us (49%)
  starting transfers between devices  30.9 us (32%)
  Pallas kernels  14.7 us (15%)
  local copies, waits for them, and re-layouts  1.48 us (2%)
    all_to_all x3, waiting for transfers between devices, exchange(): lax.all_to_all(value, group, 0, 0, tiled=True).reshape(count * rows, lanes)  25.7 us
    ppermute x15, waiting for transfers between devices, moved(): return lax.ppermute(part, group, [(at, at ^ mask) for at in range(count)])  21.1 us
    all_to_all x3, starting transfers between devices, exchange(): lax.all_to_all(value, group, 0, 0, tiled=True).reshape(count * rows, lanes)  15.1 us
    ppermute x15, starting transfers between devices, moved(): return lax.ppermute(part, group, [(at, at ^ mask) for at in range(count)])  14.8 us
    pallas_call x7, Pallas kernels, call(): pl.pallas_call(body, in_specs=[outside if at in away else inside for at i...  14.7 us
  transfers between devices with their start and end apart: 20, of which 12 were waited for; matrix products, arithmetic and copies ran while one was open for 2% of the time, Pallas kernels for 1%

profile of v5, /device:TPU:0, one launch (start us, length us, event | category | flops | bytes accessed | tf_op | source)
XLA Modules:
  0.0 94.8 jit_solution(1948781196094048999)
XLA Ops:
  0.6 2.8 %shard_map.75 = (f32[16,48,128]{2,1,0:T(8,128)}, f32[12,64,256]{2,1,0:T(8,128)}) custom-call(f32[24,64,256]{2,1,0:T(8,128)} %field.1, f32[48,256]{1,0:T(8,128)} %bitcast.12, f32[24,48]{1,0:T(8,128)} %refs_2_.1), custom_call_target="tpu_custom_call" | custom-call | tf_op jit(solution)/shard_map/pallas_call | solution.py:130
  3.4 0.6 collective-permute-start
  4.0 7.0 %all-to-all-start = ((f32[16,48,128]{2,1,0:T(8,128)}), f32[16,48,128]{2,1,0:T(8,128)S(1)}, u32[]{:S(2)}, u32[]{:S(2)}) async-start(f32[16,48,128]{2,1,0:T(8,128)} %get-tuple-element.23), calls=%async_computation | async-start | bytes 786432 | tf_op jit(solution)/shard_map/all_to_all | solution.py:418
  11.0 0.1 copy.9.refs_1_
  11.1 0.4 collective-permute-start.1
  11.5 0.0 collective-permute-done.other
  11.5 1.2 %shard_map.76 = (bf16[12,128,256]{2,1,0:T(8,128)(2,1)S(1)}, bf16[12,128,256]{2,1,0:T(8,128)(2,1)S(1)}) custom-call(f32[24,64,256]{2,1,0:T(8,128)} %field.1, f32[12,64,256]{2,1,0:T(8,128)S(1)} %collective-permute-done.other), custom_call_target="tpu_custom_call" | custom-call | tf_op jit(solution)/shard_map/pallas_call | solution.py:130
  12.8 10.4 %all-to-all-done = f32[16,48,128]{2,1,0:T(8,128)S(1)} async-done(((f32[16,48,128]{2,1,0:T(8,128)}), f32[16,48,128]{2,1,0:T(8,128)S(1)}, u32[]{:S(2)}, u32[]{:S(2)}) %all-to-all-start) | async-done | bytes 393248 | tf_op jit(solution)/shard_map/all_to_all | solution.py:418
  23.2 0.0 collective-permute-done.1.refs_2_
  23.2 1.1 %shard_map.77 = (f32[48,128]{1,0:T(8,128)S(1)}, f32[192,48]{1,0:T(8,128)S(1)}) custom-call(f32[768,128]{1,0:T(8,128)S(1)} %bitcast.10, f32[64,48]{1,0:T(8,128)S(1)} %copy.9.refs_1_, f32[64,48]{1,0:T(8,128)S(1)} %collective-permute-done.1.refs_2_), custom_call_target="tpu_custom_call" | custom-call | tf_op jit(solution)/shard_map/pallas_call | solution.py:130
  24.3 0.1 collective-permute-start.2
  24.4 1.1 %collective-permute-done.2 = f32[48,128]{1,0:T(8,128)S(1)} collective-permute-done((f32[48,128]{1,0:T(8,128)S(1)}, f32[48,128]{1,0:T(8,128)S(1)}, u32[]{:S(2)}, u32[]{:S(2)}) %collective-permute-start.2) | collective-permute-done | bytes 24608 | tf_op jit(solution)/shard_map/ppermute | solution.py:28
  25.5 0.6 collective-permute-start.3
  26.1 2.6 %collective-permute-done.3 = f32[48,128]{1,0:T(8,128)S(1)} collective-permute-done((f32[48,128]{1,0:T(8,128)S(1)}, f32[48,128]{1,0:T(8,128)S(1)}, u32[]{:S(2)}, u32[]{:S(2)}) %collective-permute-start.3) | collective-permute-done | bytes 24608 | tf_op jit(solution)/shard_map/ppermute | solution.py:28
  28.8 1.5 %collective-permute-start.5 = (f32[48,128]{1,0:T(8,128)S(1)}, f32[48,128]{1,0:T(8,128)S(1)}, u32[]{:S(2)}, u32[]{:S(2)}) collective-permute-start(f32[48,128]{1,0:T(8,128)S(1)} %add.49), channel_id=1, source_target_pairs={{0,9},{1,8},{2,11},{3,10},{4,13},{5,12},{6,15},{7,14},{8,1},{9,0},... | collective-permute-start | bytes 73736 | tf_op jit(solution)/shard_map/ppermute | solution.py:28
  30.2 1.5 %collective-permute-start.6 = (f32[48,128]{1,0:T(8,128)S(1)}, f32[48,128]{1,0:T(8,128)S(1)}, u32[]{:S(2)}, u32[]{:S(2)}) collective-permute-start(f32[48,128]{1,0:T(8,128)S(1)} %add.49), channel_id=1, source_target_pairs={{0,13},{1,12},{2,15},{3,14},{4,9},{5,8},{6,11},{7,10},{8,5},{9,4},... | collective-permute-start | bytes 73736 | tf_op jit(solution)/shard_map/ppermute | solution.py:28
  31.8 0.0 collective-permute-start.4
  31.8 1.1 %collective-permute-done.5 = f32[48,128]{1,0:T(8,128)S(1)} collective-permute-done((f32[48,128]{1,0:T(8,128)S(1)}, f32[48,128]{1,0:T(8,128)S(1)}, u32[]{:S(2)}, u32[]{:S(2)}) %collective-permute-start.5) | collective-permute-done | bytes 24608 | tf_op jit(solution)/shard_map/ppermute | solution.py:28
  32.9 2.4 %collective-permute-done.6 = f32[48,128]{1,0:T(8,128)S(1)} collective-permute-done((f32[48,128]{1,0:T(8,128)S(1)}, f32[48,128]{1,0:T(8,128)S(1)}, u32[]{:S(2)}, u32[]{:S(2)}) %collective-permute-start.6) | collective-permute-done | bytes 24608 | tf_op jit(solution)/shard_map/ppermute | solution.py:28
  35.3 0.0 collective-permute-done.4
  35.3 2.8 %shard_map.78 = (f32[48,128]{1,0:T(8,128)S(1)}, f32[16,72,128]{2,1,0:T(8,128)}) custom-call(f32[48,128]{1,0:T(8,128)S(1)} %add_add_fusion.2.refs_0_, bf16[12,128,256]{2,1,0:T(8,128)(2,1)S(1)} %get-tuple-element.29.refs_1_, bf16[12,128,256]{2,1,0:T(8,128)(2,1)S(1)} %get-tuple-element.30.refs_2_), custom_call_target="tpu_custom_call" | custom-call | tf_op jit(solution)/shard_map/pallas_call | solution.py:130
  38.1 3.7 %all-to-all-start.1 = ((f32[16,72,128]{2,1,0:T(8,128)}), f32[16,72,128]{2,1,0:T(8,128)S(1)}, u32[]{:S(2)}, u32[]{:S(2)}) async-start(f32[16,72,128]{2,1,0:T(8,128)} %get-tuple-element.32), calls=%async_computation.1 | async-start | bytes 1179648 | tf_op jit(solution)/shard_map/all_to_all | solution.py:418
  41.9 0.1 copy.10.refs_1_
  42.0 15.3 %all-to-all-done.1 = f32[16,72,128]{2,1,0:T(8,128)S(1)} async-done(((f32[16,72,128]{2,1,0:T(8,128)}), f32[16,72,128]{2,1,0:T(8,128)S(1)}, u32[]{:S(2)}, u32[]{:S(2)}) %all-to-all-start.1) | async-done | bytes 589856 | tf_op jit(solution)/shard_map/all_to_all | solution.py:418
  57.3 0.8 shard_map.79
  58.0 0.3 collective-permute-start.7
  58.3 1.0 %collective-permute-done.7 = f32[48,256]{1,0:T(8,128)S(1)} collective-permute-done((f32[48,256]{1,0:T(8,128)S(1)}, f32[48,256]{1,0:T(8,128)S(1)}, u32[]{:S(2)}, u32[]{:S(2)}) %collective-permute-start.7) | collective-permute-done | bytes 49184 | tf_op jit(solution)/shard_map/ppermute | solution.py:28
  59.3 1.3 %collective-permute-start.8 = (f32[48,256]{1,0:T(8,128)S(1)}, f32[48,256]{1,0:T(8,128)S(1)}, u32[]{:S(2)}, u32[]{:S(2)}) collective-permute-start(f32[48,256]{1,0:T(8,128)S(1)} %add.54), channel_id=1, source_target_pairs={{0,3},{1,2},{2,1},{3,0},{4,7},{5,6},{6,5},{7,4},{8,11},{9,10},{10,... | collective-permute-start | bytes 147464 | tf_op jit(solution)/shard_map/ppermute | solution.py:28
  60.6 2.4 %collective-permute-done.8 = f32[48,256]{1,0:T(8,128)S(1)} collective-permute-done((f32[48,256]{1,0:T(8,128)S(1)}, f32[48,256]{1,0:T(8,128)S(1)}, u32[]{:S(2)}, u32[]{:S(2)}) %collective-permute-start.8) | collective-permute-done | bytes 49184 | tf_op jit(solution)/shard_map/ppermute | solution.py:28
  63.0 2.6 %collective-permute-start.10 = (f32[48,256]{1,0:T(8,128)S(1)}, f32[48,256]{1,0:T(8,128)S(1)}, u32[]{:S(2)}, u32[]{:S(2)}) collective-permute-start(f32[48,256]{1,0:T(8,128)S(1)} %add.55), channel_id=1, source_target_pairs={{0,9},{1,8},{2,11},{3,10},{4,13},{5,12},{6,15},{7,14},{8,1},{9,0},... | collective-permute-start | bytes 147464 | tf_op jit(solution)/shard_map/ppermute | solution.py:28
  65.7 1.2 %collective-permute-start.11 = (f32[48,256]{1,0:T(8,128)S(1)}, f32[48,256]{1,0:T(8,128)S(1)}, u32[]{:S(2)}, u32[]{:S(2)}) collective-permute-start(f32[48,256]{1,0:T(8,128)S(1)} %add.55), channel_id=1, source_target_pairs={{0,13},{1,12},{2,15},{3,14},{4,9},{5,8},{6,11},{7,10},{8,5},{9,4},... | collective-permute-start | bytes 147464 | tf_op jit(solution)/shard_map/ppermute | solution.py:28
  66.9 0.0 collective-permute-start.9
  66.9 0.7 collective-permute-done.10
  67.6 3.5 %collective-permute-done.11 = f32[48,256]{1,0:T(8,128)S(1)} collective-permute-done((f32[48,256]{1,0:T(8,128)S(1)}, f32[48,256]{1,0:T(8,128)S(1)}, u32[]{:S(2)}, u32[]{:S(2)}) %collective-permute-start.11) | collective-permute-done | bytes 49184 | tf_op jit(solution)/shard_map/ppermute | solution.py:28
  71.1 0.0 collective-permute-done.9
  71.1 3.5 %shard_map.80 = (f32[48,256]{1,0:T(8,128)S(1)}, f32[48,192]{1,0:T(8,128)S(1)}, f32[384,128]{1,0:T(8,128)}) custom-call(f32[48,256]{1,0:T(8,128)S(1)} %add_add_fusion.1.refs_0_, bf16[3,192,256]{2,1,0:T(8,128)(2,1)S(1)} %get-tuple-element.35.refs_1_, bf16[3,192,256]{2,1,0:T(8,128)(2,1)S(1)} %get-tuple-element.36.refs_2_, ...), custom_call_target="tpu_custom_call" | custom-call | tf_op jit(solution)/shard_map/pallas_call | solution.py:130
  74.6 0.8 collective-permute-start.12
  75.3 0.9 collective-permute-done.12
  76.2 0.8 collective-permute-start.13
  77.1 4.3 %all-to-all-start.2 = ((f32[16,24,128]{2,1,0:T(8,128)}), f32[16,24,128]{2,1,0:T(8,128)S(1)}, u32[]{:S(2)}, u32[]{:S(2)}) async-start(f32[16,24,128]{2,1,0:T(8,128)} %bitcast.13), calls=%async_computation.2 | async-start | bytes 393216 | tf_op jit(solution)/shard_map/all_to_all | solution.py:418
  81.4 0.0 collective-permute-done.13
  81.4 2.6 %collective-permute-start.15 = (f32[48,192]{1,0:T(8,128)S(1)}, f32[48,192]{1,0:T(8,128)S(1)}, u32[]{:S(2)}, u32[]{:S(2)}) collective-permute-start(f32[48,192]{1,0:T(8,128)S(1)} %add.60), channel_id=1, source_target_pairs={{0,9},{1,8},{2,11},{3,10},{4,13},{5,12},{6,15},{7,14},{8,1},{9,0},... | collective-permute-start | bytes 110600 | tf_op jit(solution)/shard_map/ppermute | solution.py:28
  84.0 1.5 %collective-permute-start.16 = (f32[48,192]{1,0:T(8,128)S(1)}, f32[48,192]{1,0:T(8,128)S(1)}, u32[]{:S(2)}, u32[]{:S(2)}) collective-permute-start(f32[48,192]{1,0:T(8,128)S(1)} %add.60), channel_id=1, source_target_pairs={{0,13},{1,12},{2,15},{3,14},{4,9},{5,8},{6,11},{7,10},{8,5},{9,4},... | collective-permute-start | bytes 110600 | tf_op jit(solution)/shard_map/ppermute | solution.py:28
  85.5 0.0 collective-permute-start.14
  85.5 0.7 dynamic-slice_bitcast_fusion
  86.2 0.6 copy.11
  86.8 5.4 %collective-permute-done.15 = f32[48,192]{1,0:T(8,128)S(1)} collective-permute-done((f32[48,192]{1,0:T(8,128)S(1)}, f32[48,192]{1,0:T(8,128)S(1)}, u32[]{:S(2)}, u32[]{:S(2)}) %collective-permute-start.15) | collective-permute-done | bytes 36896 | tf_op jit(solution)/shard_map/ppermute | solution.py:28
  92.2 2.6 %shard_map.81 = (f32[24,48]{1,0:T(8,128)}, f32[48,144]{1,0:T(8,128)}) custom-call(f32[48,192]{1,0:T(8,128)S(1)} %add_add_fusion.refs_0_, f32[384,128]{1,0:T(8,128)S(1)} %bitcast.11), custom_call_target="tpu_custom_call" | custom-call | tf_op jit(solution)/shard_map/pallas_call | solution.py:130
  (16 shorter events, 0.1 us)
Async XLA Ops:
  0.6 10.4 %copy-start.1 = (f32[64,48]{0,1:T(8,128)S(1)}, f32[64,48]{0,1:T(8,128)}, u32[]{:S(2)}) copy-start(f32[64,48]{0,1:T(8,128)} %param.5) | copy-start | bytes 36868
  3.4 8.1 %collective-permute-start = (f32[12,64,256]{2,1,0:T(8,128)}, f32[12,64,256]{2,1,0:T(8,128)S(1)}, u32[]{:S(2)}, u32[]{:S(2)}) collective-permute-start(f32[12,64,256]{2,1,0:T(8,128)} %get-tuple-element.24), channel_id=1, source_target_pairs={{0,1},{1,0},{2,3},{3,2},{4,5},{5,4},{6,7},{7,6},{8,9},{9,8},{10,11... | collective-permute-start | bytes 2359304 | tf_op jit(solution)/shard_map/ppermute | solution.py:48
  4.0 19.2 %all-to-all-start = ((f32[16,48,128]{2,1,0:T(8,128)}), f32[16,48,128]{2,1,0:T(8,128)S(1)}, u32[]{:S(2)}, u32[]{:S(2)}) async-start(f32[16,48,128]{2,1,0:T(8,128)} %get-tuple-element.23), calls=%async_computation | async-start | bytes 786432 | tf_op jit(solution)/shard_map/all_to_all | solution.py:418
  11.1 12.1 %collective-permute-start.1 = (f32[64,48]{1,0:T(8,128)S(1)}, f32[64,48]{1,0:T(8,128)S(1)}, u32[]{:S(2)}, u32[]{:S(2)}) collective-permute-start(f32[64,48]{1,0:T(8,128)S(1)} %copy.9.refs_1_), channel_id=1, source_target_pairs={{0,1},{1,0},{2,3},{3,2},{4,5},{5,4},{6,7},{7,6},{8,9},{9,8},{10,11... | collective-permute-start | bytes 36872 | tf_op jit(solution)/shard_map/ppermute | solution.py:48
  24.3 17.6 %copy-start = (f32[256,48]{0,1:T(8,128)S(1)}, f32[256,48]{0,1:T(8,128)}, u32[]{:S(2)}) copy-start(f32[256,48]{0,1:T(8,128)} %param.6) | copy-start | bytes 147460
  24.3 1.2 %collective-permute-start.2 = (f32[48,128]{1,0:T(8,128)S(1)}, f32[48,128]{1,0:T(8,128)S(1)}, u32[]{:S(2)}, u32[]{:S(2)}) collective-permute-start(f32[48,128]{1,0:T(8,128)S(1)} %get-tuple-element.28), channel_id=1, source_target_pairs={{0,1},{1,0},{2,3},{3,2},{4,5},{5,4},{6,7},{7,6},{8,9},{9,8},{10,11... | collective-permute-start | bytes 73736 | tf_op jit(solution)/shard_map/ppermute | solution.py:28
  25.5 3.3 %collective-permute-start.3 = (f32[48,128]{1,0:T(8,128)S(1)}, f32[48,128]{1,0:T(8,128)S(1)}, u32[]{:S(2)}, u32[]{:S(2)}) collective-permute-start(f32[48,128]{1,0:T(8,128)S(1)} %add.48), channel_id=1, source_target_pairs={{0,3},{1,2},{2,1},{3,0},{4,7},{5,6},{6,5},{7,4},{8,11},{9,10},{10,... | collective-permute-start | bytes 73736 | tf_op jit(solution)/shard_map/ppermute | solution.py:28
  28.8 4.2 %collective-permute-start.5 = (f32[48,128]{1,0:T(8,128)S(1)}, f32[48,128]{1,0:T(8,128)S(1)}, u32[]{:S(2)}, u32[]{:S(2)}) collective-permute-start(f32[48,128]{1,0:T(8,128)S(1)} %add.49), channel_id=1, source_target_pairs={{0,9},{1,8},{2,11},{3,10},{4,13},{5,12},{6,15},{7,14},{8,1},{9,0},... | collective-permute-start | bytes 73736 | tf_op jit(solution)/shard_map/ppermute | solution.py:28
  30.2 5.0 %collective-permute-start.6 = (f32[48,128]{1,0:T(8,128)S(1)}, f32[48,128]{1,0:T(8,128)S(1)}, u32[]{:S(2)}, u32[]{:S(2)}) collective-permute-start(f32[48,128]{1,0:T(8,128)S(1)} %add.49), channel_id=1, source_target_pairs={{0,13},{1,12},{2,15},{3,14},{4,9},{5,8},{6,11},{7,10},{8,5},{9,4},... | collective-permute-start | bytes 73736 | tf_op jit(solution)/shard_map/ppermute | solution.py:28
  31.8 3.5 %collective-permute-start.4 = (f32[48,128]{1,0:T(8,128)S(1)}, f32[48,128]{1,0:T(8,128)S(1)}, u32[]{:S(2)}, u32[]{:S(2)}) collective-permute-start(f32[48,128]{1,0:T(8,128)S(1)} %add.49), channel_id=1, source_target_pairs={{0,5},{1,4},{2,7},{3,6},{4,1},{5,0},{6,3},{7,2},{8,13},{9,12},{10,... | collective-permute-start | bytes 73736 | tf_op jit(solution)/shard_map/ppermute | solution.py:28
  38.1 19.1 %all-to-all-start.1 = ((f32[16,72,128]{2,1,0:T(8,128)}), f32[16,72,128]{2,1,0:T(8,128)S(1)}, u32[]{:S(2)}, u32[]{:S(2)}) async-start(f32[16,72,128]{2,1,0:T(8,128)} %get-tuple-element.32), calls=%async_computation.1 | async-start | bytes 1179648 | tf_op jit(solution)/shard_map/all_to_all | solution.py:418
  58.0 1.3 %collective-permute-start.7 = (f32[48,256]{1,0:T(8,128)S(1)}, f32[48,256]{1,0:T(8,128)S(1)}, u32[]{:S(2)}, u32[]{:S(2)}) collective-permute-start(f32[48,256]{1,0:T(8,128)S(1)} %get-tuple-element.34), channel_id=1, source_target_pairs={{0,1},{1,0},{2,3},{3,2},{4,5},{5,4},{6,7},{7,6},{8,9},{9,8},{10,11... | collective-permute-start | bytes 147464 | tf_op jit(solution)/shard_map/ppermute | solution.py:28
  59.3 3.7 %collective-permute-start.8 = (f32[48,256]{1,0:T(8,128)S(1)}, f32[48,256]{1,0:T(8,128)S(1)}, u32[]{:S(2)}, u32[]{:S(2)}) collective-permute-start(f32[48,256]{1,0:T(8,128)S(1)} %add.54), channel_id=1, source_target_pairs={{0,3},{1,2},{2,1},{3,0},{4,7},{5,6},{6,5},{7,4},{8,11},{9,10},{10,... | collective-permute-start | bytes 147464 | tf_op jit(solution)/shard_map/ppermute | solution.py:28
  63.0 4.5 %collective-permute-start.10 = (f32[48,256]{1,0:T(8,128)S(1)}, f32[48,256]{1,0:T(8,128)S(1)}, u32[]{:S(2)}, u32[]{:S(2)}) collective-permute-start(f32[48,256]{1,0:T(8,128)S(1)} %add.55), channel_id=1, source_target_pairs={{0,9},{1,8},{2,11},{3,10},{4,13},{5,12},{6,15},{7,14},{8,1},{9,0},... | collective-permute-start | bytes 147464 | tf_op jit(solution)/shard_map/ppermute | solution.py:28
  65.7 5.4 %collective-permute-start.11 = (f32[48,256]{1,0:T(8,128)S(1)}, f32[48,256]{1,0:T(8,128)S(1)}, u32[]{:S(2)}, u32[]{:S(2)}) collective-permute-start(f32[48,256]{1,0:T(8,128)S(1)} %add.55), channel_id=1, source_target_pairs={{0,13},{1,12},{2,15},{3,14},{4,9},{5,8},{6,11},{7,10},{8,5},{9,4},... | collective-permute-start | bytes 147464 | tf_op jit(solution)/shard_map/ppermute | solution.py:28
  66.9 4.2 %collective-permute-start.9 = (f32[48,256]{1,0:T(8,128)S(1)}, f32[48,256]{1,0:T(8,128)S(1)}, u32[]{:S(2)}, u32[]{:S(2)}) collective-permute-start(f32[48,256]{1,0:T(8,128)S(1)} %add.55), channel_id=1, source_target_pairs={{0,5},{1,4},{2,7},{3,6},{4,1},{5,0},{6,3},{7,2},{8,13},{9,12},{10,... | collective-permute-start | bytes 147464 | tf_op jit(solution)/shard_map/ppermute | solution.py:28
  74.6 1.7 %collective-permute-start.12 = (f32[48,192]{1,0:T(8,128)S(1)}, f32[48,192]{1,0:T(8,128)S(1)}, u32[]{:S(2)}, u32[]{:S(2)}) collective-permute-start(f32[48,192]{1,0:T(8,128)S(1)} %get-tuple-element.38), channel_id=1, source_target_pairs={{0,1},{1,0},{2,3},{3,2},{4,5},{5,4},{6,7},{7,6},{8,9},{9,8},{10,11... | collective-permute-start | bytes 110600 | tf_op jit(solution)/shard_map/ppermute | solution.py:28
  76.2 5.2 %collective-permute-start.13 = (f32[48,192]{1,0:T(8,128)S(1)}, f32[48,192]{1,0:T(8,128)S(1)}, u32[]{:S(2)}, u32[]{:S(2)}) collective-permute-start(f32[48,192]{1,0:T(8,128)S(1)} %add.59), channel_id=1, source_target_pairs={{0,3},{1,2},{2,1},{3,0},{4,7},{5,6},{6,5},{7,4},{8,11},{9,10},{10,... | collective-permute-start | bytes 110600 | tf_op jit(solution)/shard_map/ppermute | solution.py:28
  77.1 15.2 %all-to-all-start.2 = ((f32[16,24,128]{2,1,0:T(8,128)}), f32[16,24,128]{2,1,0:T(8,128)S(1)}, u32[]{:S(2)}, u32[]{:S(2)}) async-start(f32[16,24,128]{2,1,0:T(8,128)} %bitcast.13), calls=%async_computation.2 | async-start | bytes 393216 | tf_op jit(solution)/shard_map/all_to_all | solution.py:418
  81.4 10.8 %collective-permute-start.15 = (f32[48,192]{1,0:T(8,128)S(1)}, f32[48,192]{1,0:T(8,128)S(1)}, u32[]{:S(2)}, u32[]{:S(2)}) collective-permute-start(f32[48,192]{1,0:T(8,128)S(1)} %add.60), channel_id=1, source_target_pairs={{0,9},{1,8},{2,11},{3,10},{4,13},{5,12},{6,15},{7,14},{8,1},{9,0},... | collective-permute-start | bytes 110600 | tf_op jit(solution)/shard_map/ppermute | solution.py:28
  84.0 8.2 %collective-permute-start.16 = (f32[48,192]{1,0:T(8,128)S(1)}, f32[48,192]{1,0:T(8,128)S(1)}, u32[]{:S(2)}, u32[]{:S(2)}) collective-permute-start(f32[48,192]{1,0:T(8,128)S(1)} %add.60), channel_id=1, source_target_pairs={{0,13},{1,12},{2,15},{3,14},{4,9},{5,8},{6,11},{7,10},{8,5},{9,4},... | collective-permute-start | bytes 110600 | tf_op jit(solution)/shard_map/ppermute | solution.py:28
  85.5 6.7 %collective-permute-start.14 = (f32[48,192]{1,0:T(8,128)S(1)}, f32[48,192]{1,0:T(8,128)S(1)}, u32[]{:S(2)}, u32[]{:S(2)}) collective-permute-start(f32[48,192]{1,0:T(8,128)S(1)} %add.60), channel_id=1, source_target_pairs={{0,5},{1,4},{2,7},{3,6},{4,1},{5,0},{6,3},{7,2},{8,13},{9,12},{10,... | collective-permute-start | bytes 110600 | tf_op jit(solution)/shard_map/ppermute | solution.py:28

commit v6 on v5

--- a/solution.py
+++ b/solution.py
@@ -32,13 +32,12 @@
     while narrow < count:
         bits.append(narrow)
         narrow *= 2
-    single = len(bits) % 2
-    parts = [bits[:single]] if single else []
-    parts += [bits[at : at + 2] for at in range(single, len(bits), 2)]
+    parts = [bits[-1:]] if len(bits) % 2 else []
+    parts += [bits[at : at + 2] for at in range(0, len(bits) - 1, 2)]
     for low, *high in parts:
         if high:
-            near, far, both = moved(low + 1), moved(high[0] + 1), moved(low + high[0] + 1)
-            part = (part + near) + (far + both)
+            near_sum, far_sum = moved(low + 1), moved(high[0] + 1)
+            part = (part + near_sum) + (far_sum + moved(low + high[0] + 1))
         else:
             part = part + moved(low + 1)
     return part
@@ -354,12 +353,18 @@
     out[...] = dot3(dot3(unfold, two[...]), unfold, tn)
 
 
-def work_three(part, high, low, three, basis, out, sent, room, *, share, half, count):
+def laid(size):
+    return size // lanes, size % lanes != 0
+
+
+def work_three(
+    part, high, low, three, basis, out, sent, room, flat, sem, *, share, half, count
+):
     rank, cols = part.shape
     parts = cols // lanes
     size = count * half
-    tall = -(-size // lanes)
-    pitch = sent.shape[0] // count
+    whole, rest = laid(size)
+    pitch = flat.shape[0] // count
     value = orthonormal(part[...])
     basis[...] = value
     for h in range(parts):
@@ -375,28 +380,47 @@
             ]
         )
     )
+    pieces = [dot3(second, (high[s], low[s]), nt) for s in range(share)]
+    ends = []
+    for b in range(share):
+        for s in range(share):
+            value = pieces[s][b * count : (b + 1) * count]
+            for h in range(whole):
+                start = (b * share + s) * whole + h
+                flat[pl.ds(start, count, stride=pitch), :] = value[:, h * lanes : (h + 1) * lanes]
+            if rest:
+                ends.append(value[:, whole * lanes :])
+    if len(ends) % 2:
+        ends.append(ends[-1])
+    for at in range(0, len(ends), 2):
+        flat[pl.ds(share * share * whole + at // 2, count, stride=pitch), :] = jnp.concatenate(
+            ends[at : at + 2], axis=1
+        )
+    copy = pltpu.make_async_copy(flat, sent, sem)
+    copy.start()
     table = split(three[...])
     result = None
-    for s in range(share):
-        value = dot3(second, (high[s], low[s]), nt)
-        for b in range(share):
-            for h in range(tall):
-                wide = min(lanes, size - h * lanes)
-                start = (b * share + s) * tall + h
-                sent[pl.ds(start, count, stride=pitch), :wide] = value[
-                    b * count : (b + 1) * count, h * lanes : h * lanes + wide
-                ]
+    for value in pieces:
         value = split(value)
         term = dot3(dot3(value, table), value, tn)
         result = term if result is None else result + term
-    out[...] = result
+    for h in range(whole):
+        out[h * rank : (h + 1) * rank, :] = result[:, h * lanes : (h + 1) * lanes]
+    if rest:
+        end = result[:, whole * lanes :]
+        out[whole * rank :, :] = jnp.concatenate([end[: rank // 2], end[rank // 2 :]], axis=1)
+    copy.wait()
 
 
 def finish(part, got, basis, core, room, *, share, half, count):
-    rank, size = part.shape
-    tall = -(-size // lanes)
+    size, rank = room.shape
+    whole, rest = laid(size)
     pitch = got.shape[0] // count
-    value = orthonormal(part[...])
+    value = [part[h * rank : (h + 1) * rank, :] for h in range(whole)]
+    if rest:
+        end = part[whole * rank :, :]
+        value.append(jnp.concatenate([end[:, : lanes // 2], end[:, lanes // 2 :]]))
+    value = orthonormal(jnp.concatenate(value, axis=1))
     room[...] = value.T
     depth = basis.shape[0]
     basis[...] = room[pl.ds(pl.multiple_of(lax.axis_index("wide") * depth, 8), depth), :]
@@ -404,11 +428,13 @@
     for b in range(share):
         rows = []
         for s in range(share):
-            pieces = []
-            for h in range(tall):
-                wide = min(lanes, size - h * lanes)
-                start = (b * share + s) * tall + h
-                pieces.append(got[pl.ds(start, count, stride=pitch), :][:, :wide])
+            at = b * share + s
+            pieces = [
+                got[pl.ds(at * whole + h, count, stride=pitch), :] for h in range(whole)
+            ]
+            if rest:
+                end = got[pl.ds(share * share * whole + at // 2, count, stride=pitch), :]
+                pieces.append(end[:, lanes // 2 :] if at % 2 else end[:, : lanes // 2])
             rows.append(jnp.concatenate(pieces, axis=1))
         core[:, b * rank : (b + 1) * rank] = dot3(jnp.concatenate(rows), value, nt)
 
@@ -438,7 +464,7 @@
 
     slots = share + 1
     parts = cols // lanes
-    chunks = 3 if half % 3 == 0 and half // 3 * slots % 8 == 0 else 1
+    chunks = max(n for n in (1, 3) if half % n == 0 and half // n * slots % 8 == 0)
     packed, sent = call(
         stage(pack_one),
         [far(count, half * slots, lanes), far(half, rows, cols)],
@@ -494,15 +520,26 @@
     )
     product = total(product)
 
-    pitch = -(-share * share * -(-size // lanes) // 8) * 8
+    whole, rest = laid(size)
+    pitch = share * share * whole + rest * -(-share * share // 2)
+    pitch = -(-pitch // 8) * 8
     two_t, product, sent = call(
         stage(work_three),
-        [near(*product.shape), near(rank, size), far(count * pitch, lanes)],
+        [
+            near(*product.shape),
+            near(rank * whole + rest * rank // 2, lanes),
+            far(count * pitch, lanes),
+        ],
         product,
         high,
         low,
         three,
-        scratch_shapes=[near(parts * rank, lanes)],
+        away_out=(2,),
+        scratch_shapes=[
+            near(parts * rank, lanes),
+            near(count * pitch, lanes),
+            pltpu.SemaphoreType.DMA,
+        ],
     )
     got = exchange(sent.reshape(count, pitch, lanes))
     product = total(product)
@@ -526,6 +563,8 @@
         and rank % count == 0
         and count % 8 == 0
         and depth % 8 == 0
+        and count * depth // 2 % (lanes // 2) == 0
+        and rank % 16 == 0
         and (depth // 2) * (rank // count + 1) % 8 == 0
         and (depth // 2) * (rank // count) * (cols // lanes) % 8 == 0
         and 2 * rows == lanes

time: 95.7 us -> 92 us (0.961)
  waiting for transfers between devices: 46.8 us -> 43.9 us
    ppermute x15, waiting for transfers between devices: 21.1 us -> 16.8 us  [moved(): return lax.ppermute(part, group, [(at, at ^ mask) for at in range(count)])]
    all_to_all x3, waiting for transfers between devices: 25.7 us -> 27.1 us  [exchange(): lax.all_to_all(value, group, 0, 0, tiled=True).reshape(count * rows, lanes)]
  transfers between devices with their start and end apart: 20 -> 20, of which waited for: 12 -> 14; matrix products, arithmetic and copies ran while one was open for 2% -> 2% of each run, Pallas kernels for 1% -> 1%
where the time goes in v6:
time: 92 us; the launch traced here: 91.5 us
  waiting for transfers between devices  43.9 us (48%)
  starting transfers between devices  30.8 us (33%)
  Pallas kernels  14.5 us (16%)
  local copies, waits for them, and re-layouts  1.48 us (2%)
    all_to_all x3, waiting for transfers between devices, exchange(): lax.all_to_all(value, group, 0, 0, tiled=True).reshape(count * rows, lanes)  27.1 us
    ppermute x15, waiting for transfers between devices, moved(): return lax.ppermute(part, group, [(at, at ^ mask) for at in range(count)])  16.8 us
    ppermute x15, starting transfers between devices, moved(): return lax.ppermute(part, group, [(at, at ^ mask) for at in range(count)])  15.5 us
    pallas_call x7, Pallas kernels, call(): pl.pallas_call(body, in_specs=[outside if at in away else inside for at i...  14.5 us
    all_to_all x3, starting transfers between devices, exchange(): lax.all_to_all(value, group, 0, 0, tiled=True).reshape(count * rows, lanes)  14.3 us
  transfers between devices with their start and end apart: 20, of which 14 were waited for; matrix products, arithmetic and copies ran while one was open for 2% of the time, Pallas kernels for 1%

profile of v6, /device:TPU:0, one launch (start us, length us, event | category | flops | bytes accessed | tf_op | source)
XLA Modules:
  0.0 91.5 jit_solution(1410353992604155596)
XLA Ops:
  0.6 2.8 %shard_map.75 = (f32[16,48,128]{2,1,0:T(8,128)}, f32[12,64,256]{2,1,0:T(8,128)}) custom-call(f32[24,64,256]{2,1,0:T(8,128)} %field.1, f32[48,256]{1,0:T(8,128)} %bitcast.12, f32[24,48]{1,0:T(8,128)} %refs_2_.1), custom_call_target="tpu_custom_call" | custom-call | tf_op jit(solution)/shard_map/pallas_call | solution.py:129
  3.4 0.6 collective-permute-start
  4.0 7.0 %all-to-all-start = ((f32[16,48,128]{2,1,0:T(8,128)}), f32[16,48,128]{2,1,0:T(8,128)S(1)}, u32[]{:S(2)}, u32[]{:S(2)}) async-start(f32[16,48,128]{2,1,0:T(8,128)} %get-tuple-element.23), calls=%async_computation | async-start | bytes 786432 | tf_op jit(solution)/shard_map/all_to_all | solution.py:444
  11.0 0.1 copy.9.refs_1_
  11.1 0.4 collective-permute-start.1
  11.5 1.2 %shard_map.76 = (bf16[12,128,256]{2,1,0:T(8,128)(2,1)S(1)}, bf16[12,128,256]{2,1,0:T(8,128)(2,1)S(1)}) custom-call(f32[24,64,256]{2,1,0:T(8,128)} %field.1, f32[12,64,256]{2,1,0:T(8,128)S(1)} %collective-permute-done.other), custom_call_target="tpu_custom_call" | custom-call | tf_op jit(solution)/shard_map/pallas_call | solution.py:129
  12.8 10.4 %all-to-all-done = f32[16,48,128]{2,1,0:T(8,128)S(1)} async-done(((f32[16,48,128]{2,1,0:T(8,128)}), f32[16,48,128]{2,1,0:T(8,128)S(1)}, u32[]{:S(2)}, u32[]{:S(2)}) %all-to-all-start) | async-done | bytes 393248 | tf_op jit(solution)/shard_map/all_to_all | solution.py:444
  23.2 1.1 %shard_map.77 = (f32[48,128]{1,0:T(8,128)S(1)}, f32[192,48]{1,0:T(8,128)S(1)}) custom-call(f32[768,128]{1,0:T(8,128)S(1)} %bitcast.10, f32[64,48]{1,0:T(8,128)S(1)} %copy.9.refs_1_, f32[64,48]{1,0:T(8,128)S(1)} %collective-permute-done.1.refs_2_), custom_call_target="tpu_custom_call" | custom-call | tf_op jit(solution)/shard_map/pallas_call | solution.py:129
  24.3 0.1 collective-permute-start.2
  24.4 1.1 %collective-permute-done.2 = f32[48,128]{1,0:T(8,128)S(1)} collective-permute-done((f32[48,128]{1,0:T(8,128)S(1)}, f32[48,128]{1,0:T(8,128)S(1)}, u32[]{:S(2)}, u32[]{:S(2)}) %collective-permute-start.2) | collective-permute-done | bytes 24608 | tf_op jit(solution)/shard_map/ppermute | solution.py:28
  25.5 1.5 %collective-permute-start.3 = (f32[48,128]{1,0:T(8,128)S(1)}, f32[48,128]{1,0:T(8,128)S(1)}, u32[]{:S(2)}, u32[]{:S(2)}) collective-permute-start(f32[48,128]{1,0:T(8,128)S(1)} %add.48), channel_id=1, source_target_pairs={{0,9},{1,8},{2,11},{3,10},{4,13},{5,12},{6,15},{7,14},{8,1},{9,0},... | collective-permute-start | bytes 73736 | tf_op jit(solution)/shard_map/ppermute | solution.py:28
  27.0 2.7 %collective-permute-done.3 = f32[48,128]{1,0:T(8,128)S(1)} collective-permute-done((f32[48,128]{1,0:T(8,128)S(1)}, f32[48,128]{1,0:T(8,128)S(1)}, u32[]{:S(2)}, u32[]{:S(2)}) %collective-permute-start.3) | collective-permute-done | bytes 24608 | tf_op jit(solution)/shard_map/ppermute | solution.py:28
  29.7 0.9 collective-permute-start.5
  30.5 1.0 %collective-permute-start.6 = (f32[48,128]{1,0:T(8,128)S(1)}, f32[48,128]{1,0:T(8,128)S(1)}, u32[]{:S(2)}, u32[]{:S(2)}) collective-permute-start(f32[48,128]{1,0:T(8,128)S(1)} %add.49), channel_id=1, source_target_pairs={{0,7},{1,6},{2,5},{3,4},{4,3},{5,2},{6,1},{7,0},{8,15},{9,14},{10,... | collective-permute-start | bytes 73736 | tf_op jit(solution)/shard_map/ppermute | solution.py:28
  31.5 1.4 %collective-permute-start.4 = (f32[48,128]{1,0:T(8,128)S(1)}, f32[48,128]{1,0:T(8,128)S(1)}, u32[]{:S(2)}, u32[]{:S(2)}) collective-permute-start(f32[48,128]{1,0:T(8,128)S(1)} %add.49), channel_id=1, source_target_pairs={{0,3},{1,2},{2,1},{3,0},{4,7},{5,6},{6,5},{7,4},{8,11},{9,10},{10,... | collective-permute-start | bytes 73736 | tf_op jit(solution)/shard_map/ppermute | solution.py:28
  32.9 0.0 collective-permute-done.5
  32.9 1.8 %collective-permute-done.6 = f32[48,128]{1,0:T(8,128)S(1)} collective-permute-done((f32[48,128]{1,0:T(8,128)S(1)}, f32[48,128]{1,0:T(8,128)S(1)}, u32[]{:S(2)}, u32[]{:S(2)}) %collective-permute-start.6) | collective-permute-done | bytes 24608 | tf_op jit(solution)/shard_map/ppermute | solution.py:28
  34.7 0.5 collective-permute-done.4
  35.2 2.8 %shard_map.78 = (f32[48,128]{1,0:T(8,128)S(1)}, f32[16,72,128]{2,1,0:T(8,128)}) custom-call(f32[48,128]{1,0:T(8,128)S(1)} %add_add_fusion.2.refs_0_, bf16[12,128,256]{2,1,0:T(8,128)(2,1)S(1)} %get-tuple-element.29.refs_1_, bf16[12,128,256]{2,1,0:T(8,128)(2,1)S(1)} %get-tuple-element.30.refs_2_), custom_call_target="tpu_custom_call" | custom-call | tf_op jit(solution)/shard_map/pallas_call | solution.py:129
  38.1 3.6 %all-to-all-start.1 = ((f32[16,72,128]{2,1,0:T(8,128)}), f32[16,72,128]{2,1,0:T(8,128)S(1)}, u32[]{:S(2)}, u32[]{:S(2)}) async-start(f32[16,72,128]{2,1,0:T(8,128)} %get-tuple-element.32), calls=%async_computation.1 | async-start | bytes 1179648 | tf_op jit(solution)/shard_map/all_to_all | solution.py:444
  41.7 0.1 copy.10.refs_1_
  41.8 15.4 %all-to-all-done.1 = f32[16,72,128]{2,1,0:T(8,128)S(1)} async-done(((f32[16,72,128]{2,1,0:T(8,128)}), f32[16,72,128]{2,1,0:T(8,128)S(1)}, u32[]{:S(2)}, u32[]{:S(2)}) %all-to-all-start.1) | async-done | bytes 589856 | tf_op jit(solution)/shard_map/all_to_all | solution.py:444
  57.2 0.8 shard_map.79
  57.9 0.1 collective-permute-start.7
  58.1 1.2 %collective-permute-done.7 = f32[48,256]{1,0:T(8,128)S(1)} collective-permute-done((f32[48,256]{1,0:T(8,128)S(1)}, f32[48,256]{1,0:T(8,128)S(1)}, u32[]{:S(2)}, u32[]{:S(2)}) %collective-permute-start.7) | collective-permute-done | bytes 49184 | tf_op jit(solution)/shard_map/ppermute | solution.py:28
  59.2 2.3 %collective-permute-start.8 = (f32[48,256]{1,0:T(8,128)S(1)}, f32[48,256]{1,0:T(8,128)S(1)}, u32[]{:S(2)}, u32[]{:S(2)}) collective-permute-start(f32[48,256]{1,0:T(8,128)S(1)} %add.54), channel_id=1, source_target_pairs={{0,9},{1,8},{2,11},{3,10},{4,13},{5,12},{6,15},{7,14},{8,1},{9,0},... | collective-permute-start | bytes 147464 | tf_op jit(solution)/shard_map/ppermute | solution.py:28
  61.6 2.4 %collective-permute-done.8 = f32[48,256]{1,0:T(8,128)S(1)} collective-permute-done((f32[48,256]{1,0:T(8,128)S(1)}, f32[48,256]{1,0:T(8,128)S(1)}, u32[]{:S(2)}, u32[]{:S(2)}) %collective-permute-start.8) | collective-permute-done | bytes 49184 | tf_op jit(solution)/shard_map/ppermute | solution.py:28
  63.9 1.5 %collective-permute-start.10 = (f32[48,256]{1,0:T(8,128)S(1)}, f32[48,256]{1,0:T(8,128)S(1)}, u32[]{:S(2)}, u32[]{:S(2)}) collective-permute-start(f32[48,256]{1,0:T(8,128)S(1)} %add.55), channel_id=1, source_target_pairs={{0,5},{1,4},{2,7},{3,6},{4,1},{5,0},{6,3},{7,2},{8,13},{9,12},{10,... | collective-permute-start | bytes 147464 | tf_op jit(solution)/shard_map/ppermute | solution.py:28
  65.4 0.6 collective-permute-start.11
  66.0 1.0 %collective-permute-start.9 = (f32[48,256]{1,0:T(8,128)S(1)}, f32[48,256]{1,0:T(8,128)S(1)}, u32[]{:S(2)}, u32[]{:S(2)}) collective-permute-start(f32[48,256]{1,0:T(8,128)S(1)} %add.55), channel_id=1, source_target_pairs={{0,3},{1,2},{2,1},{3,0},{4,7},{5,6},{6,5},{7,4},{8,11},{9,10},{10,... | collective-permute-start | bytes 147464 | tf_op jit(solution)/shard_map/ppermute | solution.py:28
  67.0 0.8 collective-permute-done.10
  67.7 2.4 %collective-permute-done.11 = f32[48,256]{1,0:T(8,128)S(1)} collective-permute-done((f32[48,256]{1,0:T(8,128)S(1)}, f32[48,256]{1,0:T(8,128)S(1)}, u32[]{:S(2)}, u32[]{:S(2)}) %collective-permute-start.11) | collective-permute-done | bytes 49184 | tf_op jit(solution)/shard_map/ppermute | solution.py:28
  70.2 0.5 collective-permute-done.9
  70.7 3.2 %shard_map.80 = (f32[48,256]{1,0:T(8,128)S(1)}, f32[72,128]{1,0:T(8,128)S(1)}, f32[256,128]{1,0:T(8,128)}) custom-call(f32[48,256]{1,0:T(8,128)S(1)} %add_add_fusion.refs_0_, bf16[3,192,256]{2,1,0:T(8,128)(2,1)S(1)} %get-tuple-element.35.refs_1_, bf16[3,192,256]{2,1,0:T(8,128)(2,1)S(1)} %get-tuple-element.36.refs_2_, ...), custom_call_target="tpu_custom_call" | custom-call | tf_op jit(solution)/shard_map/pallas_call | solution.py:129
  73.9 0.3 collective-permute-start.12
  74.2 1.0 %collective-permute-done.12 = f32[72,128]{1,0:T(8,128)S(1)} collective-permute-done((f32[72,128]{1,0:T(8,128)S(1)}, f32[72,128]{1,0:T(8,128)S(1)}, u32[]{:S(2)}, u32[]{:S(2)}) %collective-permute-start.12) | collective-permute-done | bytes 36896 | tf_op jit(solution)/shard_map/ppermute | solution.py:28
  75.1 1.5 %collective-permute-start.13 = (f32[72,128]{1,0:T(8,128)S(1)}, f32[72,128]{1,0:T(8,128)S(1)}, u32[]{:S(2)}, u32[]{:S(2)}) collective-permute-start(f32[72,128]{1,0:T(8,128)S(1)} %add.59), channel_id=1, source_target_pairs={{0,9},{1,8},{2,11},{3,10},{4,13},{5,12},{6,15},{7,14},{8,1},{9,0},... | collective-permute-start | bytes 110600 | tf_op jit(solution)/shard_map/ppermute | solution.py:28
  76.7 3.7 %all-to-all-start.2 = ((f32[16,16,128]{2,1,0:T(8,128)}), f32[16,16,128]{2,1,0:T(8,128)S(1)}, u32[]{:S(2)}, u32[]{:S(2)}) async-start(f32[16,16,128]{2,1,0:T(8,128)} %bitcast.13), calls=%async_computation.2 | async-start | bytes 262144 | tf_op jit(solution)/shard_map/all_to_all | solution.py:444
  80.4 0.0 collective-permute-done.13
  80.4 1.9 %collective-permute-start.15 = (f32[72,128]{1,0:T(8,128)S(1)}, f32[72,128]{1,0:T(8,128)S(1)}, u32[]{:S(2)}, u32[]{:S(2)}) collective-permute-start(f32[72,128]{1,0:T(8,128)S(1)} %add.60), channel_id=1, source_target_pairs={{0,5},{1,4},{2,7},{3,6},{4,1},{5,0},{6,3},{7,2},{8,13},{9,12},{10,... | collective-permute-start | bytes 110600 | tf_op jit(solution)/shard_map/ppermute | solution.py:28
  82.3 1.4 %collective-permute-start.16 = (f32[72,128]{1,0:T(8,128)S(1)}, f32[72,128]{1,0:T(8,128)S(1)}, u32[]{:S(2)}, u32[]{:S(2)}) collective-permute-start(f32[72,128]{1,0:T(8,128)S(1)} %add.60), channel_id=1, source_target_pairs={{0,7},{1,6},{2,5},{3,4},{4,3},{5,2},{6,1},{7,0},{8,15},{9,14},{10,... | collective-permute-start | bytes 110600 | tf_op jit(solution)/shard_map/ppermute | solution.py:28
  83.7 0.0 collective-permute-start.14
  83.7 0.7 dynamic-slice_bitcast_fusion
  84.4 0.6 copy.11
  85.0 0.0 collective-permute-done.15
  85.0 2.5 %collective-permute-done.16 = f32[72,128]{1,0:T(8,128)S(1)} collective-permute-done((f32[72,128]{1,0:T(8,128)S(1)}, f32[72,128]{1,0:T(8,128)S(1)}, u32[]{:S(2)}, u32[]{:S(2)}) %collective-permute-start.16) | collective-permute-done | bytes 36896 | tf_op jit(solution)/shard_map/ppermute | solution.py:28
  87.5 1.3 %all-to-all-done.2 = f32[16,16,128]{2,1,0:T(8,128)S(1)} async-done(((f32[16,16,128]{2,1,0:T(8,128)}), f32[16,16,128]{2,1,0:T(8,128)S(1)}, u32[]{:S(2)}, u32[]{:S(2)}) %all-to-all-start.2) | async-done | bytes 131104 | tf_op jit(solution)/shard_map/all_to_all | solution.py:444
  88.8 2.7 %shard_map.81 = (f32[24,48]{1,0:T(8,128)}, f32[48,144]{1,0:T(8,128)}) custom-call(f32[72,128]{1,0:T(8,128)S(1)} %add_add_fusion.1.refs_0_, f32[256,128]{1,0:T(8,128)S(1)} %bitcast.11), custom_call_target="tpu_custom_call" | custom-call | tf_op jit(solution)/shard_map/pallas_call | solution.py:129
  (16 shorter events, 0.1 us)
Async XLA Ops:
  0.6 10.4 %copy-start.1 = (f32[64,48]{0,1:T(8,128)S(1)}, f32[64,48]{0,1:T(8,128)}, u32[]{:S(2)}) copy-start(f32[64,48]{0,1:T(8,128)} %param.5) | copy-start | bytes 36868
  3.4 8.1 %collective-permute-start = (f32[12,64,256]{2,1,0:T(8,128)}, f32[12,64,256]{2,1,0:T(8,128)S(1)}, u32[]{:S(2)}, u32[]{:S(2)}) collective-permute-start(f32[12,64,256]{2,1,0:T(8,128)} %get-tuple-element.24), channel_id=1, source_target_pairs={{0,1},{1,0},{2,3},{3,2},{4,5},{5,4},{6,7},{7,6},{8,9},{9,8},{10,11... | collective-permute-start | bytes 2359304 | tf_op jit(solution)/shard_map/ppermute | solution.py:47
  4.0 19.2 %all-to-all-start = ((f32[16,48,128]{2,1,0:T(8,128)}), f32[16,48,128]{2,1,0:T(8,128)S(1)}, u32[]{:S(2)}, u32[]{:S(2)}) async-start(f32[16,48,128]{2,1,0:T(8,128)} %get-tuple-element.23), calls=%async_computation | async-start | bytes 786432 | tf_op jit(solution)/shard_map/all_to_all | solution.py:444
  11.1 12.1 %collective-permute-start.1 = (f32[64,48]{1,0:T(8,128)S(1)}, f32[64,48]{1,0:T(8,128)S(1)}, u32[]{:S(2)}, u32[]{:S(2)}) collective-permute-start(f32[64,48]{1,0:T(8,128)S(1)} %copy.9.refs_1_), channel_id=1, source_target_pairs={{0,1},{1,0},{2,3},{3,2},{4,5},{5,4},{6,7},{7,6},{8,9},{9,8},{10,11... | collective-permute-start | bytes 36872 | tf_op jit(solution)/shard_map/ppermute | solution.py:47
  24.3 17.4 %copy-start = (f32[256,48]{0,1:T(8,128)S(1)}, f32[256,48]{0,1:T(8,128)}, u32[]{:S(2)}) copy-start(f32[256,48]{0,1:T(8,128)} %param.6) | copy-start | bytes 147460
  24.3 1.2 %collective-permute-start.2 = (f32[48,128]{1,0:T(8,128)S(1)}, f32[48,128]{1,0:T(8,128)S(1)}, u32[]{:S(2)}, u32[]{:S(2)}) collective-permute-start(f32[48,128]{1,0:T(8,128)S(1)} %get-tuple-element.28), channel_id=1, source_target_pairs={{0,1},{1,0},{2,3},{3,2},{4,5},{5,4},{6,7},{7,6},{8,9},{9,8},{10,11... | collective-permute-start | bytes 73736 | tf_op jit(solution)/shard_map/ppermute | solution.py:28
  25.5 4.2 %collective-permute-start.3 = (f32[48,128]{1,0:T(8,128)S(1)}, f32[48,128]{1,0:T(8,128)S(1)}, u32[]{:S(2)}, u32[]{:S(2)}) collective-permute-start(f32[48,128]{1,0:T(8,128)S(1)} %add.48), channel_id=1, source_target_pairs={{0,9},{1,8},{2,11},{3,10},{4,13},{5,12},{6,15},{7,14},{8,1},{9,0},... | collective-permute-start | bytes 73736 | tf_op jit(solution)/shard_map/ppermute | solution.py:28
  29.7 3.3 %collective-permute-start.5 = (f32[48,128]{1,0:T(8,128)S(1)}, f32[48,128]{1,0:T(8,128)S(1)}, u32[]{:S(2)}, u32[]{:S(2)}) collective-permute-start(f32[48,128]{1,0:T(8,128)S(1)} %add.49), channel_id=1, source_target_pairs={{0,5},{1,4},{2,7},{3,6},{4,1},{5,0},{6,3},{7,2},{8,13},{9,12},{10,... | collective-permute-start | bytes 73736 | tf_op jit(solution)/shard_map/ppermute | solution.py:28
  30.5 4.2 %collective-permute-start.6 = (f32[48,128]{1,0:T(8,128)S(1)}, f32[48,128]{1,0:T(8,128)S(1)}, u32[]{:S(2)}, u32[]{:S(2)}) collective-permute-start(f32[48,128]{1,0:T(8,128)S(1)} %add.49), channel_id=1, source_target_pairs={{0,7},{1,6},{2,5},{3,4},{4,3},{5,2},{6,1},{7,0},{8,15},{9,14},{10,... | collective-permute-start | bytes 73736 | tf_op jit(solution)/shard_map/ppermute | solution.py:28
  31.5 3.7 %collective-permute-start.4 = (f32[48,128]{1,0:T(8,128)S(1)}, f32[48,128]{1,0:T(8,128)S(1)}, u32[]{:S(2)}, u32[]{:S(2)}) collective-permute-start(f32[48,128]{1,0:T(8,128)S(1)} %add.49), channel_id=1, source_target_pairs={{0,3},{1,2},{2,1},{3,0},{4,7},{5,6},{6,5},{7,4},{8,11},{9,10},{10,... | collective-permute-start | bytes 73736 | tf_op jit(solution)/shard_map/ppermute | solution.py:28
  38.1 19.1 %all-to-all-start.1 = ((f32[16,72,128]{2,1,0:T(8,128)}), f32[16,72,128]{2,1,0:T(8,128)S(1)}, u32[]{:S(2)}, u32[]{:S(2)}) async-start(f32[16,72,128]{2,1,0:T(8,128)} %get-tuple-element.32), calls=%async_computation.1 | async-start | bytes 1179648 | tf_op jit(solution)/shard_map/all_to_all | solution.py:444
  57.9 1.3 %collective-permute-start.7 = (f32[48,256]{1,0:T(8,128)S(1)}, f32[48,256]{1,0:T(8,128)S(1)}, u32[]{:S(2)}, u32[]{:S(2)}) collective-permute-start(f32[48,256]{1,0:T(8,128)S(1)} %get-tuple-element.34), channel_id=1, source_target_pairs={{0,1},{1,0},{2,3},{3,2},{4,5},{5,4},{6,7},{7,6},{8,9},{9,8},{10,11... | collective-permute-start | bytes 147464 | tf_op jit(solution)/shard_map/ppermute | solution.py:28
  59.2 4.7 %collective-permute-start.8 = (f32[48,256]{1,0:T(8,128)S(1)}, f32[48,256]{1,0:T(8,128)S(1)}, u32[]{:S(2)}, u32[]{:S(2)}) collective-permute-start(f32[48,256]{1,0:T(8,128)S(1)} %add.54), channel_id=1, source_target_pairs={{0,9},{1,8},{2,11},{3,10},{4,13},{5,12},{6,15},{7,14},{8,1},{9,0},... | collective-permute-start | bytes 147464 | tf_op jit(solution)/shard_map/ppermute | solution.py:28
  63.9 3.8 %collective-permute-start.10 = (f32[48,256]{1,0:T(8,128)S(1)}, f32[48,256]{1,0:T(8,128)S(1)}, u32[]{:S(2)}, u32[]{:S(2)}) collective-permute-start(f32[48,256]{1,0:T(8,128)S(1)} %add.55), channel_id=1, source_target_pairs={{0,5},{1,4},{2,7},{3,6},{4,1},{5,0},{6,3},{7,2},{8,13},{9,12},{10,... | collective-permute-start | bytes 147464 | tf_op jit(solution)/shard_map/ppermute | solution.py:28
  65.4 4.7 %collective-permute-start.11 = (f32[48,256]{1,0:T(8,128)S(1)}, f32[48,256]{1,0:T(8,128)S(1)}, u32[]{:S(2)}, u32[]{:S(2)}) collective-permute-start(f32[48,256]{1,0:T(8,128)S(1)} %add.55), channel_id=1, source_target_pairs={{0,7},{1,6},{2,5},{3,4},{4,3},{5,2},{6,1},{7,0},{8,15},{9,14},{10,... | collective-permute-start | bytes 147464 | tf_op jit(solution)/shard_map/ppermute | solution.py:28
  66.0 4.7 %collective-permute-start.9 = (f32[48,256]{1,0:T(8,128)S(1)}, f32[48,256]{1,0:T(8,128)S(1)}, u32[]{:S(2)}, u32[]{:S(2)}) collective-permute-start(f32[48,256]{1,0:T(8,128)S(1)} %add.55), channel_id=1, source_target_pairs={{0,3},{1,2},{2,1},{3,0},{4,7},{5,6},{6,5},{7,4},{8,11},{9,10},{10,... | collective-permute-start | bytes 147464 | tf_op jit(solution)/shard_map/ppermute | solution.py:28
  73.9 1.3 %collective-permute-start.12 = (f32[72,128]{1,0:T(8,128)S(1)}, f32[72,128]{1,0:T(8,128)S(1)}, u32[]{:S(2)}, u32[]{:S(2)}) collective-permute-start(f32[72,128]{1,0:T(8,128)S(1)} %get-tuple-element.38), channel_id=1, source_target_pairs={{0,1},{1,0},{2,3},{3,2},{4,5},{5,4},{6,7},{7,6},{8,9},{9,8},{10,11... | collective-permute-start | bytes 110600 | tf_op jit(solution)/shard_map/ppermute | solution.py:28
  75.1 5.2 %collective-permute-start.13 = (f32[72,128]{1,0:T(8,128)S(1)}, f32[72,128]{1,0:T(8,128)S(1)}, u32[]{:S(2)}, u32[]{:S(2)}) collective-permute-start(f32[72,128]{1,0:T(8,128)S(1)} %add.59), channel_id=1, source_target_pairs={{0,9},{1,8},{2,11},{3,10},{4,13},{5,12},{6,15},{7,14},{8,1},{9,0},... | collective-permute-start | bytes 110600 | tf_op jit(solution)/shard_map/ppermute | solution.py:28
  76.7 12.2 %all-to-all-start.2 = ((f32[16,16,128]{2,1,0:T(8,128)}), f32[16,16,128]{2,1,0:T(8,128)S(1)}, u32[]{:S(2)}, u32[]{:S(2)}) async-start(f32[16,16,128]{2,1,0:T(8,128)} %bitcast.13), calls=%async_computation.2 | async-start | bytes 262144 | tf_op jit(solution)/shard_map/all_to_all | solution.py:444
  80.4 4.6 %collective-permute-start.15 = (f32[72,128]{1,0:T(8,128)S(1)}, f32[72,128]{1,0:T(8,128)S(1)}, u32[]{:S(2)}, u32[]{:S(2)}) collective-permute-start(f32[72,128]{1,0:T(8,128)S(1)} %add.60), channel_id=1, source_target_pairs={{0,5},{1,4},{2,7},{3,6},{4,1},{5,0},{6,3},{7,2},{8,13},{9,12},{10,... | collective-permute-start | bytes 110600 | tf_op jit(solution)/shard_map/ppermute | solution.py:28
  82.3 5.2 %collective-permute-start.16 = (f32[72,128]{1,0:T(8,128)S(1)}, f32[72,128]{1,0:T(8,128)S(1)}, u32[]{:S(2)}, u32[]{:S(2)}) collective-permute-start(f32[72,128]{1,0:T(8,128)S(1)} %add.60), channel_id=1, source_target_pairs={{0,7},{1,6},{2,5},{3,4},{4,3},{5,2},{6,1},{7,0},{8,15},{9,14},{10,... | collective-permute-start | bytes 110600 | tf_op jit(solution)/shard_map/ppermute | solution.py:28
  83.7 3.9 %collective-permute-start.14 = (f32[72,128]{1,0:T(8,128)S(1)}, f32[72,128]{1,0:T(8,128)S(1)}, u32[]{:S(2)}, u32[]{:S(2)}) collective-permute-start(f32[72,128]{1,0:T(8,128)S(1)} %add.60), channel_id=1, source_target_pairs={{0,3},{1,2},{2,1},{3,0},{4,7},{5,6},{6,5},{7,4},{8,11},{9,10},{10,... | collective-permute-start | bytes 110600 | tf_op jit(solution)/shard_map/ppermute | solution.py:28

commit v7 on v6

--- a/solution.py
+++ b/solution.py
@@ -201,40 +201,35 @@
 def pack_one(field, two_far, three_far, out, sent, room, flat, two, three, sems, *, share, half, count):
     chunks, _, steps, rows, cols = room.shape
     rank = two.shape[0]
-    slots = share + 1
+    pitch = flat.shape[0] // count
     at_core = lax.axis_index("narrow")
-    tall = steps * slots
 
     def fetch(at, h):
         source = field.at[pl.ds(h * half + at * steps, steps)]
         return pltpu.make_async_copy(source, room.at[at, h], sems.at[2 * at + h])
 
-    def leave(at):
-        source = flat.reshape(count, half * slots, lanes).at[:, at * tall : (at + 1) * tall]
-        return pltpu.make_async_copy(
-            source, out.at[:, at * tall : (at + 1) * tall], sems.at[2 * chunks + at]
-        )
-
     def hand(at):
         target = sent.at[pl.ds(at * steps, steps)]
-        return pltpu.make_async_copy(room.at[at, 1 - at_core], target, sems.at[3 * chunks + at])
+        return pltpu.make_async_copy(room.at[at, 1 - at_core], target, sems.at[2 * chunks + at])
 
     copies = [
-        pltpu.make_async_copy(three_far, three, sems.at[4 * chunks]),
-        pltpu.make_async_copy(two_far, two, sems.at[4 * chunks + 1]),
+        pltpu.make_async_copy(three_far, three, sems.at[3 * chunks]),
+        pltpu.make_async_copy(two_far, two, sems.at[3 * chunks + 1]),
     ]
+    leave = pltpu.make_async_copy(flat, out, sems.at[3 * chunks + 2])
     for copy in copies:
         copy.start()
     for at in range(chunks):
         for h in range(2):
             fetch(at, h).start()
     copies[0].wait()
-    first = three[:half]
-    second = three[half:]
-    empty = jnp.zeros((half, lanes // 2 - rank), jnp.float32)
-    both = jnp.concatenate([first, empty, second, empty], axis=1)
-    for d in range(count):
-        flat[pl.ds(d * half * slots + share, half, stride=slots), :] = both
+    own = jnp.where(at_core == 0, three[:half], three[half:])
+    empty = jnp.zeros((half // 2, lanes // 2 - rank), jnp.float32)
+    both = jnp.concatenate([own[: half // 2], empty, own[half // 2 :], empty], axis=1)
+    for r in range(half // 2):
+        flat[pl.ds(half * share + r, count, stride=pitch), :] = jnp.broadcast_to(
+            both[r : r + 1], (count, lanes)
+        )
     copies[1].wait()
     two_high, two_low = split(two[...])
     both = jnp.concatenate([two_high, two_low])
@@ -248,14 +243,13 @@
             second = lax.dot_general(two_high, low, nt, preferred_element_type=jnp.float32)
             along = first[:rank] + (first[rank:] + second)
             for s in range(share):
-                start = (at * steps + q) * slots + s
-                flat[pl.ds(start, count, stride=half * slots), :] = along[
+                flat[pl.ds((at * steps + q) * share + s, count, stride=pitch), :] = along[
                     s * count : (s + 1) * count
                 ]
-        leave(at).start()
+    leave.start()
     for at in range(chunks):
         hand(at).wait()
-        leave(at).wait()
+    leave.wait()
 
 
 def prepare(field, other, high, low, own, sem):
@@ -274,25 +268,45 @@
     put(own, at)
 
 
-def work_one(got, own, other, out, three, *, share, half, count):
+def work_one(got, own, other, out, three, table, *, share, half, count):
     rank = own.shape[1]
-    slots = share + 1
-    size = count * half
+    part = lanes // 2
+    pitch = got.shape[0] // count
+    each = pitch // share
+    size = count * each
+    wide = count // 2
     at = lax.axis_index("narrow")
     low = jnp.where(at == 0, own[...], other[...])
     high = jnp.where(at == 0, other[...], own[...])
     one = jnp.concatenate([low, high])
-    table = got[pl.ds(share, size, stride=slots), :]
+    left = lax.broadcasted_iota(jnp.int32, (wide, lanes), 1) < part
+    for r in range(half // 2):
+        first, second = [
+            got[pl.ds(half * share + r + h * pitch, wide, stride=2 * pitch), :] for h in range(2)
+        ]
+        first_turned, second_turned = pltpu.roll(first, part, 1), pltpu.roll(second, part, 1)
+        for n in range(2):
+            start = n * each + r
+            table[pl.ds(start, wide, stride=2 * each), :] = jnp.where(left, first, second_turned)
+            table[pl.ds(start + half // 2, wide, stride=2 * each), :] = jnp.where(
+                left, first_turned, second
+            )
+        for at, value in enumerate((first, first_turned, second, second_turned)):
+            three[pl.ds(at * half // 2 + r, wide, stride=2 * half), :] = value
+    for r in range(half, each):
+        for n in range(2):
+            table[pl.ds(n * each + r, wide, stride=2 * each), :] = jnp.zeros(
+                (wide, lanes), jnp.float32
+            )
+    value = table[...]
     row = lax.broadcasted_iota(jnp.int32, (size, lanes), 0)
-    odd = (row // half) % 2 == 1
-    part = lanes // 2
-    three[...] = jnp.where(odd, pltpu.roll(table, part, 1), table)[:, :rank]
-    table = jnp.concatenate([jnp.where(odd, 0.0, table), jnp.where(odd, table, 0.0)], axis=1)
-    table = split(table)
+    odd = (row // each) % 2 == 1
+    value = jnp.concatenate([jnp.where(odd, 0.0, value), jnp.where(odd, value, 0.0)], axis=1)
+    mixed = split(value)
     lane = lax.broadcasted_iota(jnp.int32, (rank, lanes), 1)
     pieces = []
     for s in range(share):
-        value = dot3(table, got[pl.ds(s, size, stride=slots), :], tn)
+        value = dot3(mixed, got[pl.ds(s, size, stride=share), :], tn)
         first = value[:rank] + pltpu.roll(value[part : part + rank], part, 1)
         second = (
             pltpu.roll(value[2 * part : 2 * part + rank], part, 1)
@@ -343,7 +357,7 @@
 def work_two(got, two, three, out, high, low, *, share, half, count):
     parts = two.shape[0] // lanes
     size = count * half
-    table = split(three[...])
+    table = split(three[:, : two.shape[1]])
     pieces = []
     for s in range(share):
         value = split(taken(got, s, parts, share * parts, size))
@@ -398,7 +412,7 @@
         )
     copy = pltpu.make_async_copy(flat, sent, sem)
     copy.start()
-    table = split(three[...])
+    table = split(three[:, :rank])
     result = None
     for value in pieces:
         value = split(value)
@@ -439,9 +453,10 @@
         core[:, b * rank : (b + 1) * rank] = dot3(jnp.concatenate(rows), value, nt)
 
 
-def exchange(value):
-    count, rows, _ = value.shape
-    return lax.all_to_all(value, group, 0, 0, tiled=True).reshape(count * rows, lanes)
+def exchange(value, count):
+    rows = value.shape[0]
+    flat = value.reshape(count, 1, rows // count * lanes)
+    return lax.all_to_all(flat, group, 0, 0, tiled=True).reshape(rows, lanes)
 
 
 def special(window_data, factor_one, factor_two, factor_three):
@@ -462,12 +477,12 @@
         run.__name__ = body.__name__
         return run
 
-    slots = share + 1
     parts = cols // lanes
-    chunks = max(n for n in (1, 3) if half % n == 0 and half // n * slots % 8 == 0)
+    chunks = 3 if half % 3 == 0 else 1
+    pitch = half * share + half // 2
     packed, sent = call(
         stage(pack_one),
-        [far(count, half * slots, lanes), far(half, rows, cols)],
+        [far(count * pitch, lanes), far(half, rows, cols)],
         window_data,
         factor_two.T,
         factor_three,
@@ -475,13 +490,13 @@
         away_out=(0, 1),
         scratch_shapes=[
             near(chunks, 2, half // chunks, rows, cols),
-            near(size * slots, lanes),
+            near(count * pitch, lanes),
             near(rank, cols),
             near(depth, rank),
-            pltpu.SemaphoreType.DMA((4 * chunks + 2,)),
+            pltpu.SemaphoreType.DMA((3 * chunks + 3,)),
         ],
     )
-    got = exchange(packed)
+    got = exchange(packed, count)
     high, low = call(
         prepare,
         [near(half, 2 * rows, cols, dtype=jnp.bfloat16)] * 2,
@@ -493,7 +508,12 @@
     one_other = swap(factor_one)
     got, high, low = lax.optimization_barrier((got, high, low))
     product, three = call(
-        stage(work_one), [near(rank, 2 * rows), near(size, rank)], got, factor_one, one_other
+        stage(work_one),
+        [near(rank, 2 * rows), near(size, lanes)],
+        got,
+        factor_one,
+        one_other,
+        scratch_shapes=[near(count * pitch // share, lanes)],
     )
     product = total(product)
 
@@ -510,7 +530,7 @@
             pltpu.SemaphoreType.DMA((chunks,)),
         ],
     )
-    got = exchange(packed)
+    got = exchange(packed.reshape(size * share * parts, lanes), count)
     product, high, low = call(
         stage(work_two),
         [near(rank, cols)] + [near(share, size, cols, dtype=jnp.bfloat16)] * 2,
@@ -522,7 +542,6 @@
 
     whole, rest = laid(size)
     pitch = share * share * whole + rest * -(-share * share // 2)
-    pitch = -(-pitch // 8) * 8
     two_t, product, sent = call(
         stage(work_three),
         [
@@ -541,7 +560,7 @@
             pltpu.SemaphoreType.DMA,
         ],
     )
-    got = exchange(sent.reshape(count, pitch, lanes))
+    got = exchange(sent, count)
     product = total(product)
     basis_three, core = call(
         stage(finish),
@@ -565,7 +584,8 @@
         and depth % 8 == 0
         and count * depth // 2 % (lanes // 2) == 0
         and rank % 16 == 0
-        and (depth // 2) * (rank // count + 1) % 8 == 0
+        and depth // 4 % (rank // count) == 0
+        and count * depth * (2 * (rank // count) + 1) // 4 % 8 == 0
         and (depth // 2) * (rank // count) * (cols // lanes) % 8 == 0
         and 2 * rows == lanes
         and 2 * rank <= lanes

time: 92 us -> 98.5 us (1.071)
  waiting for transfers between devices: 43.9 us -> 49.4 us
    all_to_all x3, waiting for transfers between devices: 27.1 us -> 32.5 us  [exchange(): return lax.all_to_all(flat, group, 0, 0, tiled=True).reshape(rows, lanes)]
where the time goes in v7:
time: 98.5 us; the launch traced here: 98 us
  waiting for transfers between devices  49.4 us (50%)
  starting transfers between devices  31.7 us (32%)
  Pallas kernels  14.6 us (15%)
  local copies, waits for them, and re-layouts  1.48 us (2%)
    all_to_all x3, waiting for transfers between devices, exchange(): return lax.all_to_all(flat, group, 0, 0, tiled=True).reshape(rows, lanes)  32.5 us
    ppermute x15, waiting for transfers between devices, moved(): return lax.ppermute(part, group, [(at, at ^ mask) for at in range(count)])  16.9 us
    ppermute x15, starting transfers between devices, moved(): return lax.ppermute(part, group, [(at, at ^ mask) for at in range(count)])  16 us
    all_to_all x3, starting transfers between devices, exchange(): return lax.all_to_all(flat, group, 0, 0, tiled=True).reshape(rows, lanes)  14.7 us
    pallas_call x7, Pallas kernels, call(): pl.pallas_call(body, in_specs=[outside if at in away else inside for at i...  14.6 us
  transfers between devices with their start and end apart: 20, of which 14 were waited for; matrix products, arithmetic and copies ran while one was open for 2% of the time, Pallas kernels for 1%

profile of v7, /device:TPU:0, one launch (start us, length us, event | category | flops | bytes accessed | tf_op | source)
XLA Modules:
  0.0 98.0 jit_solution(12005591328321211358)
XLA Ops:
  0.6 2.8 %shard_map.75 = (f32[672,128]{1,0:T(8,128)}, f32[12,64,256]{2,1,0:T(8,128)}) custom-call(f32[24,64,256]{2,1,0:T(8,128)} %field.1, f32[48,256]{1,0:T(8,128)} %bitcast.16, f32[24,48]{1,0:T(8,128)} %refs_2_.1), custom_call_target="tpu_custom_call" | custom-call | tf_op jit(solution)/shard_map/pallas_call | solution.py:129
  3.5 0.6 collective-permute-start
  4.0 7.0 %all-to-all-start = ((f32[16,1,5376]{2,1,0:T(1,128)}), f32[16,1,5376]{2,1,0:T(1,128)S(1)}, u32[]{:S(2)}, u32[]{:S(2)}) async-start(f32[16,1,5376]{2,1,0:T(1,128)} %bitcast.15), calls=%async_computation | async-start | bytes 688128 | tf_op jit(solution)/shard_map/all_to_all | solution.py:459
  11.1 0.1 copy.13.refs_1_
  11.1 0.4 collective-permute-start.1
  11.6 1.2 %shard_map.76 = (bf16[12,128,256]{2,1,0:T(8,128)(2,1)S(1)}, bf16[12,128,256]{2,1,0:T(8,128)(2,1)S(1)}) custom-call(f32[24,64,256]{2,1,0:T(8,128)} %field.1, f32[12,64,256]{2,1,0:T(8,128)S(1)} %collective-permute-done.other), custom_call_target="tpu_custom_call" | custom-call | tf_op jit(solution)/shard_map/pallas_call | solution.py:129
  12.8 9.5 %all-to-all-done = f32[16,1,5376]{2,1,0:T(1,128)S(1)} async-done(((f32[16,1,5376]{2,1,0:T(1,128)}), f32[16,1,5376]{2,1,0:T(1,128)S(1)}, u32[]{:S(2)}, u32[]{:S(2)}) %all-to-all-start) | async-done | bytes 344096 | tf_op jit(solution)/shard_map/all_to_all | solution.py:459
  22.4 0.0 collective-permute-done.1.refs_2_
  22.4 1.1 %shard_map.77 = (f32[48,128]{1,0:T(8,128)S(1)}, f32[192,128]{1,0:T(8,128)S(1)}) custom-call(f32[672,128]{1,0:T(8,128)S(1)} %bitcast.12, f32[64,48]{1,0:T(8,128)S(1)} %copy.13.refs_1_, f32[64,48]{1,0:T(8,128)S(1)} %collective-permute-done.1.refs_2_), custom_call_target="tpu_custom_call" | custom-call | tf_op jit(solution)/shard_map/pallas_call | solution.py:129
  23.5 0.1 collective-permute-start.2
  23.7 1.1 %collective-permute-done.2 = f32[48,128]{1,0:T(8,128)S(1)} collective-permute-done((f32[48,128]{1,0:T(8,128)S(1)}, f32[48,128]{1,0:T(8,128)S(1)}, u32[]{:S(2)}, u32[]{:S(2)}) %collective-permute-start.2) | collective-permute-done | bytes 24608 | tf_op jit(solution)/shard_map/ppermute | solution.py:28
  24.8 1.3 %collective-permute-start.3 = (f32[48,128]{1,0:T(8,128)S(1)}, f32[48,128]{1,0:T(8,128)S(1)}, u32[]{:S(2)}, u32[]{:S(2)}) collective-permute-start(f32[48,128]{1,0:T(8,128)S(1)} %add.48), channel_id=1, source_target_pairs={{0,9},{1,8},{2,11},{3,10},{4,13},{5,12},{6,15},{7,14},{8,1},{9,0},... | collective-permute-start | bytes 73736 | tf_op jit(solution)/shard_map/ppermute | solution.py:28
  26.0 2.9 %collective-permute-done.3 = f32[48,128]{1,0:T(8,128)S(1)} collective-permute-done((f32[48,128]{1,0:T(8,128)S(1)}, f32[48,128]{1,0:T(8,128)S(1)}, u32[]{:S(2)}, u32[]{:S(2)}) %collective-permute-start.3) | collective-permute-done | bytes 24608 | tf_op jit(solution)/shard_map/ppermute | solution.py:28
  28.9 0.7 collective-permute-start.5
  29.6 1.0 %collective-permute-start.6 = (f32[48,128]{1,0:T(8,128)S(1)}, f32[48,128]{1,0:T(8,128)S(1)}, u32[]{:S(2)}, u32[]{:S(2)}) collective-permute-start(f32[48,128]{1,0:T(8,128)S(1)} %add.49), channel_id=1, source_target_pairs={{0,7},{1,6},{2,5},{3,4},{4,3},{5,2},{6,1},{7,0},{8,15},{9,14},{10,... | collective-permute-start | bytes 73736 | tf_op jit(solution)/shard_map/ppermute | solution.py:28
  30.6 1.7 %collective-permute-start.4 = (f32[48,128]{1,0:T(8,128)S(1)}, f32[48,128]{1,0:T(8,128)S(1)}, u32[]{:S(2)}, u32[]{:S(2)}) collective-permute-start(f32[48,128]{1,0:T(8,128)S(1)} %add.49), channel_id=1, source_target_pairs={{0,3},{1,2},{2,1},{3,0},{4,7},{5,6},{6,5},{7,4},{8,11},{9,10},{10,... | collective-permute-start | bytes 73736 | tf_op jit(solution)/shard_map/ppermute | solution.py:28
  32.3 0.0 collective-permute-done.5
  32.3 1.4 %collective-permute-done.6 = f32[48,128]{1,0:T(8,128)S(1)} collective-permute-done((f32[48,128]{1,0:T(8,128)S(1)}, f32[48,128]{1,0:T(8,128)S(1)}, u32[]{:S(2)}, u32[]{:S(2)}) %collective-permute-start.6) | collective-permute-done | bytes 24608 | tf_op jit(solution)/shard_map/ppermute | solution.py:28
  33.8 0.5 collective-permute-done.4
  34.3 2.8 %shard_map.78 = (f32[48,128]{1,0:T(8,128)S(1)}, f32[16,72,128]{2,1,0:T(8,128)}) custom-call(f32[48,128]{1,0:T(8,128)S(1)} %add_add_fusion.2.refs_0_, bf16[12,128,256]{2,1,0:T(8,128)(2,1)S(1)} %get-tuple-element.29.refs_1_, bf16[12,128,256]{2,1,0:T(8,128)(2,1)S(1)} %get-tuple-element.30.refs_2_), custom_call_target="tpu_custom_call" | custom-call | tf_op jit(solution)/shard_map/pallas_call | solution.py:129
  37.1 3.6 %all-to-all-start.1 = ((f32[16,1,9216]{2,1,0:T(1,128)}), f32[16,1,9216]{2,1,0:T(1,128)S(1)}, u32[]{:S(2)}, u32[]{:S(2)}) async-start(f32[16,1,9216]{2,1,0:T(1,128)} %bitcast.14), calls=%async_computation.1 | async-start | bytes 1179648 | tf_op jit(solution)/shard_map/all_to_all | solution.py:459
  40.8 0.1 copy.15.refs_1_
  40.8 15.4 %all-to-all-done.1 = f32[16,1,9216]{2,1,0:T(1,128)S(1)} async-done(((f32[16,1,9216]{2,1,0:T(1,128)}), f32[16,1,9216]{2,1,0:T(1,128)S(1)}, u32[]{:S(2)}, u32[]{:S(2)}) %all-to-all-start.1) | async-done | bytes 589856 | tf_op jit(solution)/shard_map/all_to_all | solution.py:459
  56.2 0.8 shard_map.79
  57.0 0.1 collective-permute-start.7
  57.1 1.2 %collective-permute-done.7 = f32[48,256]{1,0:T(8,128)S(1)} collective-permute-done((f32[48,256]{1,0:T(8,128)S(1)}, f32[48,256]{1,0:T(8,128)S(1)}, u32[]{:S(2)}, u32[]{:S(2)}) %collective-permute-start.7) | collective-permute-done | bytes 49184 | tf_op jit(solution)/shard_map/ppermute | solution.py:28
  58.3 2.3 %collective-permute-start.8 = (f32[48,256]{1,0:T(8,128)S(1)}, f32[48,256]{1,0:T(8,128)S(1)}, u32[]{:S(2)}, u32[]{:S(2)}) collective-permute-start(f32[48,256]{1,0:T(8,128)S(1)} %add.54), channel_id=1, source_target_pairs={{0,9},{1,8},{2,11},{3,10},{4,13},{5,12},{6,15},{7,14},{8,1},{9,0},... | collective-permute-start | bytes 147464 | tf_op jit(solution)/shard_map/ppermute | solution.py:28
  60.6 2.4 %collective-permute-done.8 = f32[48,256]{1,0:T(8,128)S(1)} collective-permute-done((f32[48,256]{1,0:T(8,128)S(1)}, f32[48,256]{1,0:T(8,128)S(1)}, u32[]{:S(2)}, u32[]{:S(2)}) %collective-permute-start.8) | collective-permute-done | bytes 49184 | tf_op jit(solution)/shard_map/ppermute | solution.py:28
  63.0 1.5 %collective-permute-start.10 = (f32[48,256]{1,0:T(8,128)S(1)}, f32[48,256]{1,0:T(8,128)S(1)}, u32[]{:S(2)}, u32[]{:S(2)}) collective-permute-start(f32[48,256]{1,0:T(8,128)S(1)} %add.55), channel_id=1, source_target_pairs={{0,5},{1,4},{2,7},{3,6},{4,1},{5,0},{6,3},{7,2},{8,13},{9,12},{10,... | collective-permute-start | bytes 147464 | tf_op jit(solution)/shard_map/ppermute | solution.py:28
  64.5 0.6 collective-permute-start.11
  65.1 1.0 collective-permute-start.9
  66.0 0.8 collective-permute-done.10
  66.8 2.4 %collective-permute-done.11 = f32[48,256]{1,0:T(8,128)S(1)} collective-permute-done((f32[48,256]{1,0:T(8,128)S(1)}, f32[48,256]{1,0:T(8,128)S(1)}, u32[]{:S(2)}, u32[]{:S(2)}) %collective-permute-start.11) | collective-permute-done | bytes 49184 | tf_op jit(solution)/shard_map/ppermute | solution.py:28
  69.2 0.5 collective-permute-done.9
  69.7 3.2 %shard_map.80 = (f32[48,256]{1,0:T(8,128)S(1)}, f32[72,128]{1,0:T(8,128)S(1)}, f32[224,128]{1,0:T(8,128)}) custom-call(f32[48,256]{1,0:T(8,128)S(1)} %add_add_fusion.refs_0_, bf16[3,192,256]{2,1,0:T(8,128)(2,1)S(1)} %get-tuple-element.35.refs_1_, bf16[3,192,256]{2,1,0:T(8,128)(2,1)S(1)} %get-tuple-element.36.refs_2_, ...), custom_call_target="tpu_custom_call" | custom-call | tf_op jit(solution)/shard_map/pallas_call | solution.py:129
  72.9 0.3 collective-permute-start.12
  73.2 1.0 collective-permute-done.12
  74.2 1.5 %collective-permute-start.13 = (f32[72,128]{1,0:T(8,128)S(1)}, f32[72,128]{1,0:T(8,128)S(1)}, u32[]{:S(2)}, u32[]{:S(2)}) collective-permute-start(f32[72,128]{1,0:T(8,128)S(1)} %add.59), channel_id=1, source_target_pairs={{0,9},{1,8},{2,11},{3,10},{4,13},{5,12},{6,15},{7,14},{8,1},{9,0},... | collective-permute-start | bytes 110600 | tf_op jit(solution)/shard_map/ppermute | solution.py:28
  75.7 2.8 %collective-permute-done.13 = f32[72,128]{1,0:T(8,128)S(1)} collective-permute-done((f32[72,128]{1,0:T(8,128)S(1)}, f32[72,128]{1,0:T(8,128)S(1)}, u32[]{:S(2)}, u32[]{:S(2)}) %collective-permute-start.13) | collective-permute-done | bytes 36896 | tf_op jit(solution)/shard_map/ppermute | solution.py:28
  78.5 1.2 %collective-permute-start.15 = (f32[72,128]{1,0:T(8,128)S(1)}, f32[72,128]{1,0:T(8,128)S(1)}, u32[]{:S(2)}, u32[]{:S(2)}) collective-permute-start(f32[72,128]{1,0:T(8,128)S(1)} %add.60), channel_id=1, source_target_pairs={{0,5},{1,4},{2,7},{3,6},{4,1},{5,0},{6,3},{7,2},{8,13},{9,12},{10,... | collective-permute-start | bytes 110600 | tf_op jit(solution)/shard_map/ppermute | solution.py:28
  79.6 2.3 %collective-permute-start.16 = (f32[72,128]{1,0:T(8,128)S(1)}, f32[72,128]{1,0:T(8,128)S(1)}, u32[]{:S(2)}, u32[]{:S(2)}) collective-permute-start(f32[72,128]{1,0:T(8,128)S(1)} %add.60), channel_id=1, source_target_pairs={{0,7},{1,6},{2,5},{3,4},{4,3},{5,2},{6,1},{7,0},{8,15},{9,14},{10,... | collective-permute-start | bytes 110600 | tf_op jit(solution)/shard_map/ppermute | solution.py:28
  82.0 0.4 collective-permute-start.14
  82.3 0.7 dynamic-slice_bitcast_fusion
  83.0 0.6 copy.17
  83.6 4.1 %all-to-all-start.2 = ((f32[16,1,1792]{2,1,0:T(1,128)}), f32[16,1,1792]{2,1,0:T(1,128)S(1)}, u32[]{:S(2)}, u32[]{:S(2)}) async-start(f32[16,1,1792]{2,1,0:T(1,128)} %bitcast.17), calls=%async_computation.2 | async-start | bytes 229376 | tf_op jit(solution)/shard_map/all_to_all | solution.py:459
  87.7 0.0 collective-permute-done.15
  87.8 7.6 %all-to-all-done.2 = f32[16,1,1792]{2,1,0:T(1,128)S(1)} async-done(((f32[16,1,1792]{2,1,0:T(1,128)}), f32[16,1,1792]{2,1,0:T(1,128)S(1)}, u32[]{:S(2)}, u32[]{:S(2)}) %all-to-all-start.2) | async-done | bytes 114720 | tf_op jit(solution)/shard_map/all_to_all | solution.py:459
  95.4 2.7 %shard_map.81 = (f32[24,48]{1,0:T(8,128)}, f32[48,144]{1,0:T(8,128)}) custom-call(f32[72,128]{1,0:T(8,128)S(1)} %add_add_fusion.1.refs_0_, f32[224,128]{1,0:T(8,128)S(1)} %bitcast.13), custom_call_target="tpu_custom_call" | custom-call | tf_op jit(solution)/shard_map/pallas_call | solution.py:129
  (16 shorter events, 0.1 us)
Async XLA Ops:
  0.6 10.4 %copy-start.1 = (f32[64,48]{0,1:T(8,128)S(1)}, f32[64,48]{0,1:T(8,128)}, u32[]{:S(2)}) copy-start(f32[64,48]{0,1:T(8,128)} %param.5) | copy-start | bytes 36868
  3.5 8.1 %collective-permute-start = (f32[12,64,256]{2,1,0:T(8,128)}, f32[12,64,256]{2,1,0:T(8,128)S(1)}, u32[]{:S(2)}, u32[]{:S(2)}) collective-permute-start(f32[12,64,256]{2,1,0:T(8,128)} %get-tuple-element.24), channel_id=1, source_target_pairs={{0,1},{1,0},{2,3},{3,2},{4,5},{5,4},{6,7},{7,6},{8,9},{9,8},{10,11... | collective-permute-start | bytes 2359304 | tf_op jit(solution)/shard_map/ppermute | solution.py:47
  4.0 18.4 %all-to-all-start = ((f32[16,1,5376]{2,1,0:T(1,128)}), f32[16,1,5376]{2,1,0:T(1,128)S(1)}, u32[]{:S(2)}, u32[]{:S(2)}) async-start(f32[16,1,5376]{2,1,0:T(1,128)} %bitcast.15), calls=%async_computation | async-start | bytes 688128 | tf_op jit(solution)/shard_map/all_to_all | solution.py:459
  11.1 11.2 %collective-permute-start.1 = (f32[64,48]{1,0:T(8,128)S(1)}, f32[64,48]{1,0:T(8,128)S(1)}, u32[]{:S(2)}, u32[]{:S(2)}) collective-permute-start(f32[64,48]{1,0:T(8,128)S(1)} %copy.13.refs_1_), channel_id=1, source_target_pairs={{0,1},{1,0},{2,3},{3,2},{4,5},{5,4},{6,7},{7,6},{8,9},{9,8},{10,11... | collective-permute-start | bytes 36872 | tf_op jit(solution)/shard_map/ppermute | solution.py:47
  23.5 17.2 %copy-start = (f32[256,48]{0,1:T(8,128)S(1)}, f32[256,48]{0,1:T(8,128)}, u32[]{:S(2)}) copy-start(f32[256,48]{0,1:T(8,128)} %param.6) | copy-start | bytes 147460
  23.5 1.2 %collective-permute-start.2 = (f32[48,128]{1,0:T(8,128)S(1)}, f32[48,128]{1,0:T(8,128)S(1)}, u32[]{:S(2)}, u32[]{:S(2)}) collective-permute-start(f32[48,128]{1,0:T(8,128)S(1)} %get-tuple-element.28), channel_id=1, source_target_pairs={{0,1},{1,0},{2,3},{3,2},{4,5},{5,4},{6,7},{7,6},{8,9},{9,8},{10,11... | collective-permute-start | bytes 73736 | tf_op jit(solution)/shard_map/ppermute | solution.py:28
  24.8 4.2 %collective-permute-start.3 = (f32[48,128]{1,0:T(8,128)S(1)}, f32[48,128]{1,0:T(8,128)S(1)}, u32[]{:S(2)}, u32[]{:S(2)}) collective-permute-start(f32[48,128]{1,0:T(8,128)S(1)} %add.48), channel_id=1, source_target_pairs={{0,9},{1,8},{2,11},{3,10},{4,13},{5,12},{6,15},{7,14},{8,1},{9,0},... | collective-permute-start | bytes 73736 | tf_op jit(solution)/shard_map/ppermute | solution.py:28
  28.9 3.4 %collective-permute-start.5 = (f32[48,128]{1,0:T(8,128)S(1)}, f32[48,128]{1,0:T(8,128)S(1)}, u32[]{:S(2)}, u32[]{:S(2)}) collective-permute-start(f32[48,128]{1,0:T(8,128)S(1)} %add.49), channel_id=1, source_target_pairs={{0,5},{1,4},{2,7},{3,6},{4,1},{5,0},{6,3},{7,2},{8,13},{9,12},{10,... | collective-permute-start | bytes 73736 | tf_op jit(solution)/shard_map/ppermute | solution.py:28
  29.6 4.2 %collective-permute-start.6 = (f32[48,128]{1,0:T(8,128)S(1)}, f32[48,128]{1,0:T(8,128)S(1)}, u32[]{:S(2)}, u32[]{:S(2)}) collective-permute-start(f32[48,128]{1,0:T(8,128)S(1)} %add.49), channel_id=1, source_target_pairs={{0,7},{1,6},{2,5},{3,4},{4,3},{5,2},{6,1},{7,0},{8,15},{9,14},{10,... | collective-permute-start | bytes 73736 | tf_op jit(solution)/shard_map/ppermute | solution.py:28
  30.6 3.7 %collective-permute-start.4 = (f32[48,128]{1,0:T(8,128)S(1)}, f32[48,128]{1,0:T(8,128)S(1)}, u32[]{:S(2)}, u32[]{:S(2)}) collective-permute-start(f32[48,128]{1,0:T(8,128)S(1)} %add.49), channel_id=1, source_target_pairs={{0,3},{1,2},{2,1},{3,0},{4,7},{5,6},{6,5},{7,4},{8,11},{9,10},{10,... | collective-permute-start | bytes 73736 | tf_op jit(solution)/shard_map/ppermute | solution.py:28
  37.1 19.1 %all-to-all-start.1 = ((f32[16,1,9216]{2,1,0:T(1,128)}), f32[16,1,9216]{2,1,0:T(1,128)S(1)}, u32[]{:S(2)}, u32[]{:S(2)}) async-start(f32[16,1,9216]{2,1,0:T(1,128)} %bitcast.14), calls=%async_computation.1 | async-start | bytes 1179648 | tf_op jit(solution)/shard_map/all_to_all | solution.py:459
  57.0 1.3 %collective-permute-start.7 = (f32[48,256]{1,0:T(8,128)S(1)}, f32[48,256]{1,0:T(8,128)S(1)}, u32[]{:S(2)}, u32[]{:S(2)}) collective-permute-start(f32[48,256]{1,0:T(8,128)S(1)} %get-tuple-element.34), channel_id=1, source_target_pairs={{0,1},{1,0},{2,3},{3,2},{4,5},{5,4},{6,7},{7,6},{8,9},{9,8},{10,11... | collective-permute-start | bytes 147464 | tf_op jit(solution)/shard_map/ppermute | solution.py:28
  58.3 4.7 %collective-permute-start.8 = (f32[48,256]{1,0:T(8,128)S(1)}, f32[48,256]{1,0:T(8,128)S(1)}, u32[]{:S(2)}, u32[]{:S(2)}) collective-permute-start(f32[48,256]{1,0:T(8,128)S(1)} %add.54), channel_id=1, source_target_pairs={{0,9},{1,8},{2,11},{3,10},{4,13},{5,12},{6,15},{7,14},{8,1},{9,0},... | collective-permute-start | bytes 147464 | tf_op jit(solution)/shard_map/ppermute | solution.py:28
  63.0 3.8 %collective-permute-start.10 = (f32[48,256]{1,0:T(8,128)S(1)}, f32[48,256]{1,0:T(8,128)S(1)}, u32[]{:S(2)}, u32[]{:S(2)}) collective-permute-start(f32[48,256]{1,0:T(8,128)S(1)} %add.55), channel_id=1, source_target_pairs={{0,5},{1,4},{2,7},{3,6},{4,1},{5,0},{6,3},{7,2},{8,13},{9,12},{10,... | collective-permute-start | bytes 147464 | tf_op jit(solution)/shard_map/ppermute | solution.py:28
  64.5 4.7 %collective-permute-start.11 = (f32[48,256]{1,0:T(8,128)S(1)}, f32[48,256]{1,0:T(8,128)S(1)}, u32[]{:S(2)}, u32[]{:S(2)}) collective-permute-start(f32[48,256]{1,0:T(8,128)S(1)} %add.55), channel_id=1, source_target_pairs={{0,7},{1,6},{2,5},{3,4},{4,3},{5,2},{6,1},{7,0},{8,15},{9,14},{10,... | collective-permute-start | bytes 147464 | tf_op jit(solution)/shard_map/ppermute | solution.py:28
  65.1 4.7 %collective-permute-start.9 = (f32[48,256]{1,0:T(8,128)S(1)}, f32[48,256]{1,0:T(8,128)S(1)}, u32[]{:S(2)}, u32[]{:S(2)}) collective-permute-start(f32[48,256]{1,0:T(8,128)S(1)} %add.55), channel_id=1, source_target_pairs={{0,3},{1,2},{2,1},{3,0},{4,7},{5,6},{6,5},{7,4},{8,11},{9,10},{10,... | collective-permute-start | bytes 147464 | tf_op jit(solution)/shard_map/ppermute | solution.py:28
  72.9 1.3 %collective-permute-start.12 = (f32[72,128]{1,0:T(8,128)S(1)}, f32[72,128]{1,0:T(8,128)S(1)}, u32[]{:S(2)}, u32[]{:S(2)}) collective-permute-start(f32[72,128]{1,0:T(8,128)S(1)} %get-tuple-element.38), channel_id=1, source_target_pairs={{0,1},{1,0},{2,3},{3,2},{4,5},{5,4},{6,7},{7,6},{8,9},{9,8},{10,11... | collective-permute-start | bytes 110600 | tf_op jit(solution)/shard_map/ppermute | solution.py:28
  74.2 4.3 %collective-permute-start.13 = (f32[72,128]{1,0:T(8,128)S(1)}, f32[72,128]{1,0:T(8,128)S(1)}, u32[]{:S(2)}, u32[]{:S(2)}) collective-permute-start(f32[72,128]{1,0:T(8,128)S(1)} %add.59), channel_id=1, source_target_pairs={{0,9},{1,8},{2,11},{3,10},{4,13},{5,12},{6,15},{7,14},{8,1},{9,0},... | collective-permute-start | bytes 110600 | tf_op jit(solution)/shard_map/ppermute | solution.py:28
  78.5 9.2 %collective-permute-start.15 = (f32[72,128]{1,0:T(8,128)S(1)}, f32[72,128]{1,0:T(8,128)S(1)}, u32[]{:S(2)}, u32[]{:S(2)}) collective-permute-start(f32[72,128]{1,0:T(8,128)S(1)} %add.60), channel_id=1, source_target_pairs={{0,5},{1,4},{2,7},{3,6},{4,1},{5,0},{6,3},{7,2},{8,13},{9,12},{10,... | collective-permute-start | bytes 110600 | tf_op jit(solution)/shard_map/ppermute | solution.py:28
  79.6 8.1 %collective-permute-start.16 = (f32[72,128]{1,0:T(8,128)S(1)}, f32[72,128]{1,0:T(8,128)S(1)}, u32[]{:S(2)}, u32[]{:S(2)}) collective-permute-start(f32[72,128]{1,0:T(8,128)S(1)} %add.60), channel_id=1, source_target_pairs={{0,7},{1,6},{2,5},{3,4},{4,3},{5,2},{6,1},{7,0},{8,15},{9,14},{10,... | collective-permute-start | bytes 110600 | tf_op jit(solution)/shard_map/ppermute | solution.py:28
  82.0 5.8 %collective-permute-start.14 = (f32[72,128]{1,0:T(8,128)S(1)}, f32[72,128]{1,0:T(8,128)S(1)}, u32[]{:S(2)}, u32[]{:S(2)}) collective-permute-start(f32[72,128]{1,0:T(8,128)S(1)} %add.60), channel_id=1, source_target_pairs={{0,3},{1,2},{2,1},{3,0},{4,7},{5,6},{6,5},{7,4},{8,11},{9,10},{10,... | collective-permute-start | bytes 110600 | tf_op jit(solution)/shard_map/ppermute | solution.py:28
  83.6 11.7 %all-to-all-start.2 = ((f32[16,1,1792]{2,1,0:T(1,128)}), f32[16,1,1792]{2,1,0:T(1,128)S(1)}, u32[]{:S(2)}, u32[]{:S(2)}) async-start(f32[16,1,1792]{2,1,0:T(1,128)} %bitcast.17), calls=%async_computation.2 | async-start | bytes 229376 | tf_op jit(solution)/shard_map/all_to_all | solution.py:459

commit v8 on v7

--- a/solution.py
+++ b/solution.py
@@ -78,9 +78,11 @@
             [jnp.broadcast_to(x[:, 8 * at + k : 8 * at + k + 1], (8, width)) for x in live]
             for k in range(8)
         ]
+        root = None
         for j in range(8):
             heads = [jnp.broadcast_to(columns[k][0][j : j + 1], (8, width)) for k in range(j, 8)]
             inverse = 1.0 / heads[0]
+            root = jnp.where(row == j, lax.rsqrt(heads[0]), 0.0 if root is None else root)
             scale = [x * inverse for x in columns[j]]
             scale[0] = jnp.where(row > j, scale[0], 0.0)
             for k in range(j + 1, 8):
@@ -88,6 +90,7 @@
             lead = jnp.broadcast_to(live[0][j : j + 1], (8, width))
             live = [x - y * lead for x, y in zip(live, scale)]
         tiles[at:] = live
+        tiles[at] = live[0] * root
     return jnp.concatenate(tiles, axis=0)
 
 
@@ -99,8 +102,7 @@
     row = lax.broadcasted_iota(jnp.int32, (rank, width), 0)
     lane = lax.broadcasted_iota(jnp.int32, (rank, width), 1)
     table = eliminate(jnp.where(lane == row + rank, 1.0, gram), rank)
-    pivots = jnp.sum(jnp.where(lane == row, table, 0.0), axis=1, keepdims=True)
-    table = jnp.where(lane < rank, 0.0, table * lax.rsqrt(pivots))
+    table = jnp.where(lane < rank, 0.0, table)
     padded = [jnp.zeros((rank, size), part.dtype), part]
     if width > 2 * rank:
         padded.append(jnp.zeros((width - 2 * rank, size), part.dtype))
@@ -542,6 +544,7 @@
 
     whole, rest = laid(size)
     pitch = share * share * whole + rest * -(-share * share // 2)
+    pitch = -(-pitch // 8) * 8
     two_t, product, sent = call(
         stage(work_three),
         [

time: 98.5 us -> 90.8 us (0.922)
  waiting for transfers between devices: 49.4 us -> 42.9 us
  starting transfers between devices: 31.7 us -> 30.7 us
    all_to_all x3, waiting for transfers between devices: 32.5 us -> 26.2 us  [exchange(): return lax.all_to_all(flat, group, 0, 0, tiled=True).reshape(rows, lanes)]
where the time goes in v8:
time: 90.8 us; the launch traced here: 90.3 us
  waiting for transfers between devices  42.9 us (47%)
  starting transfers between devices  30.7 us (34%)
  Pallas kernels  14.4 us (16%)
  local copies, waits for them, and re-layouts  1.48 us (2%)
    all_to_all x3, waiting for transfers between devices, exchange(): return lax.all_to_all(flat, group, 0, 0, tiled=True).reshape(rows, lanes)  26.2 us
    ppermute x15, waiting for transfers between devices, moved(): return lax.ppermute(part, group, [(at, at ^ mask) for at in range(count)])  16.7 us
    ppermute x15, starting transfers between devices, moved(): return lax.ppermute(part, group, [(at, at ^ mask) for at in range(count)])  15.4 us
    pallas_call x7, Pallas kernels, call(): pl.pallas_call(body, in_specs=[outside if at in away else inside for at i...  14.4 us
    all_to_all x3, starting transfers between devices, exchange(): return lax.all_to_all(flat, group, 0, 0, tiled=True).reshape(rows, lanes)  14.3 us
  transfers between devices with their start and end apart: 20, of which 14 were waited for; matrix products, arithmetic and copies ran while one was open for 2% of the time, Pallas kernels for 1%

profile of v8, /device:TPU:0, one launch (start us, length us, event | category | flops | bytes accessed | tf_op | source)
XLA Modules:
  0.0 90.3 jit_solution(6284334540575816630)
XLA Ops:
  0.6 2.8 %shard_map.75 = (f32[672,128]{1,0:T(8,128)}, f32[12,64,256]{2,1,0:T(8,128)}) custom-call(f32[24,64,256]{2,1,0:T(8,128)} %field.1, f32[48,256]{1,0:T(8,128)} %bitcast.16, f32[24,48]{1,0:T(8,128)} %refs_2_.1), custom_call_target="tpu_custom_call" | custom-call | tf_op jit(solution)/shard_map/pallas_call | solution.py:131
  3.5 0.6 collective-permute-start
  4.0 7.0 %all-to-all-start = ((f32[16,1,5376]{2,1,0:T(1,128)}), f32[16,1,5376]{2,1,0:T(1,128)S(1)}, u32[]{:S(2)}, u32[]{:S(2)}) async-start(f32[16,1,5376]{2,1,0:T(1,128)} %bitcast.15), calls=%async_computation | async-start | bytes 688128 | tf_op jit(solution)/shard_map/all_to_all | solution.py:461
  11.1 0.1 copy.13.refs_1_
  11.1 0.4 collective-permute-start.1
  11.6 0.0 collective-permute-done.other
  11.6 1.2 %shard_map.76 = (bf16[12,128,256]{2,1,0:T(8,128)(2,1)S(1)}, bf16[12,128,256]{2,1,0:T(8,128)(2,1)S(1)}) custom-call(f32[24,64,256]{2,1,0:T(8,128)} %field.1, f32[12,64,256]{2,1,0:T(8,128)S(1)} %collective-permute-done.other), custom_call_target="tpu_custom_call" | custom-call | tf_op jit(solution)/shard_map/pallas_call | solution.py:131
  12.8 9.5 %all-to-all-done = f32[16,1,5376]{2,1,0:T(1,128)S(1)} async-done(((f32[16,1,5376]{2,1,0:T(1,128)}), f32[16,1,5376]{2,1,0:T(1,128)S(1)}, u32[]{:S(2)}, u32[]{:S(2)}) %all-to-all-start) | async-done | bytes 344096 | tf_op jit(solution)/shard_map/all_to_all | solution.py:461
  22.4 1.1 %shard_map.77 = (f32[48,128]{1,0:T(8,128)S(1)}, f32[192,128]{1,0:T(8,128)S(1)}) custom-call(f32[672,128]{1,0:T(8,128)S(1)} %bitcast.12, f32[64,48]{1,0:T(8,128)S(1)} %copy.13.refs_1_, f32[64,48]{1,0:T(8,128)S(1)} %collective-permute-done.1.refs_2_), custom_call_target="tpu_custom_call" | custom-call | tf_op jit(solution)/shard_map/pallas_call | solution.py:131
  23.5 0.1 collective-permute-start.2
  23.7 1.1 %collective-permute-done.2 = f32[48,128]{1,0:T(8,128)S(1)} collective-permute-done((f32[48,128]{1,0:T(8,128)S(1)}, f32[48,128]{1,0:T(8,128)S(1)}, u32[]{:S(2)}, u32[]{:S(2)}) %collective-permute-start.2) | collective-permute-done | bytes 24608 | tf_op jit(solution)/shard_map/ppermute | solution.py:28
  24.8 1.3 %collective-permute-start.3 = (f32[48,128]{1,0:T(8,128)S(1)}, f32[48,128]{1,0:T(8,128)S(1)}, u32[]{:S(2)}, u32[]{:S(2)}) collective-permute-start(f32[48,128]{1,0:T(8,128)S(1)} %add.48), channel_id=1, source_target_pairs={{0,9},{1,8},{2,11},{3,10},{4,13},{5,12},{6,15},{7,14},{8,1},{9,0},... | collective-permute-start | bytes 73736 | tf_op jit(solution)/shard_map/ppermute | solution.py:28
  26.0 2.9 %collective-permute-done.3 = f32[48,128]{1,0:T(8,128)S(1)} collective-permute-done((f32[48,128]{1,0:T(8,128)S(1)}, f32[48,128]{1,0:T(8,128)S(1)}, u32[]{:S(2)}, u32[]{:S(2)}) %collective-permute-start.3) | collective-permute-done | bytes 24608 | tf_op jit(solution)/shard_map/ppermute | solution.py:28
  28.9 0.7 collective-permute-start.5
  29.6 1.0 %collective-permute-start.6 = (f32[48,128]{1,0:T(8,128)S(1)}, f32[48,128]{1,0:T(8,128)S(1)}, u32[]{:S(2)}, u32[]{:S(2)}) collective-permute-start(f32[48,128]{1,0:T(8,128)S(1)} %add.49), channel_id=1, source_target_pairs={{0,7},{1,6},{2,5},{3,4},{4,3},{5,2},{6,1},{7,0},{8,15},{9,14},{10,... | collective-permute-start | bytes 73736 | tf_op jit(solution)/shard_map/ppermute | solution.py:28
  30.6 1.7 %collective-permute-start.4 = (f32[48,128]{1,0:T(8,128)S(1)}, f32[48,128]{1,0:T(8,128)S(1)}, u32[]{:S(2)}, u32[]{:S(2)}) collective-permute-start(f32[48,128]{1,0:T(8,128)S(1)} %add.49), channel_id=1, source_target_pairs={{0,3},{1,2},{2,1},{3,0},{4,7},{5,6},{6,5},{7,4},{8,11},{9,10},{10,... | collective-permute-start | bytes 73736 | tf_op jit(solution)/shard_map/ppermute | solution.py:28
  32.3 0.0 collective-permute-done.5
  32.3 1.4 %collective-permute-done.6 = f32[48,128]{1,0:T(8,128)S(1)} collective-permute-done((f32[48,128]{1,0:T(8,128)S(1)}, f32[48,128]{1,0:T(8,128)S(1)}, u32[]{:S(2)}, u32[]{:S(2)}) %collective-permute-start.6) | collective-permute-done | bytes 24608 | tf_op jit(solution)/shard_map/ppermute | solution.py:28
  33.8 0.5 collective-permute-done.4
  34.3 2.7 %shard_map.78 = (f32[48,128]{1,0:T(8,128)S(1)}, f32[16,72,128]{2,1,0:T(8,128)}) custom-call(f32[48,128]{1,0:T(8,128)S(1)} %add_add_fusion.2.refs_0_, bf16[12,128,256]{2,1,0:T(8,128)(2,1)S(1)} %get-tuple-element.29.refs_1_, bf16[12,128,256]{2,1,0:T(8,128)(2,1)S(1)} %get-tuple-element.30.refs_2_), custom_call_target="tpu_custom_call" | custom-call | tf_op jit(solution)/shard_map/pallas_call | solution.py:131
  37.1 3.6 %all-to-all-start.1 = ((f32[16,1,9216]{2,1,0:T(1,128)}), f32[16,1,9216]{2,1,0:T(1,128)S(1)}, u32[]{:S(2)}, u32[]{:S(2)}) async-start(f32[16,1,9216]{2,1,0:T(1,128)} %bitcast.14), calls=%async_computation.1 | async-start | bytes 1179648 | tf_op jit(solution)/shard_map/all_to_all | solution.py:461
  40.7 0.1 copy.15.refs_1_
  40.8 15.4 %all-to-all-done.1 = f32[16,1,9216]{2,1,0:T(1,128)S(1)} async-done(((f32[16,1,9216]{2,1,0:T(1,128)}), f32[16,1,9216]{2,1,0:T(1,128)S(1)}, u32[]{:S(2)}, u32[]{:S(2)}) %all-to-all-start.1) | async-done | bytes 589856 | tf_op jit(solution)/shard_map/all_to_all | solution.py:461
  56.1 0.8 shard_map.79
  56.9 0.1 collective-permute-start.7
  57.0 1.2 %collective-permute-done.7 = f32[48,256]{1,0:T(8,128)S(1)} collective-permute-done((f32[48,256]{1,0:T(8,128)S(1)}, f32[48,256]{1,0:T(8,128)S(1)}, u32[]{:S(2)}, u32[]{:S(2)}) %collective-permute-start.7) | collective-permute-done | bytes 49184 | tf_op jit(solution)/shard_map/ppermute | solution.py:28
  58.2 2.3 %collective-permute-start.8 = (f32[48,256]{1,0:T(8,128)S(1)}, f32[48,256]{1,0:T(8,128)S(1)}, u32[]{:S(2)}, u32[]{:S(2)}) collective-permute-start(f32[48,256]{1,0:T(8,128)S(1)} %add.54), channel_id=1, source_target_pairs={{0,9},{1,8},{2,11},{3,10},{4,13},{5,12},{6,15},{7,14},{8,1},{9,0},... | collective-permute-start | bytes 147464 | tf_op jit(solution)/shard_map/ppermute | solution.py:28
  60.5 2.4 %collective-permute-done.8 = f32[48,256]{1,0:T(8,128)S(1)} collective-permute-done((f32[48,256]{1,0:T(8,128)S(1)}, f32[48,256]{1,0:T(8,128)S(1)}, u32[]{:S(2)}, u32[]{:S(2)}) %collective-permute-start.8) | collective-permute-done | bytes 49184 | tf_op jit(solution)/shard_map/ppermute | solution.py:28
  62.9 1.5 %collective-permute-start.10 = (f32[48,256]{1,0:T(8,128)S(1)}, f32[48,256]{1,0:T(8,128)S(1)}, u32[]{:S(2)}, u32[]{:S(2)}) collective-permute-start(f32[48,256]{1,0:T(8,128)S(1)} %add.55), channel_id=1, source_target_pairs={{0,5},{1,4},{2,7},{3,6},{4,1},{5,0},{6,3},{7,2},{8,13},{9,12},{10,... | collective-permute-start | bytes 147464 | tf_op jit(solution)/shard_map/ppermute | solution.py:28
  64.4 0.6 collective-permute-start.11
  65.0 1.0 %collective-permute-start.9 = (f32[48,256]{1,0:T(8,128)S(1)}, f32[48,256]{1,0:T(8,128)S(1)}, u32[]{:S(2)}, u32[]{:S(2)}) collective-permute-start(f32[48,256]{1,0:T(8,128)S(1)} %add.55), channel_id=1, source_target_pairs={{0,3},{1,2},{2,1},{3,0},{4,7},{5,6},{6,5},{7,4},{8,11},{9,10},{10,... | collective-permute-start | bytes 147464 | tf_op jit(solution)/shard_map/ppermute | solution.py:28
  65.9 0.8 collective-permute-done.10
  66.7 2.4 %collective-permute-done.11 = f32[48,256]{1,0:T(8,128)S(1)} collective-permute-done((f32[48,256]{1,0:T(8,128)S(1)}, f32[48,256]{1,0:T(8,128)S(1)}, u32[]{:S(2)}, u32[]{:S(2)}) %collective-permute-start.11) | collective-permute-done | bytes 49184 | tf_op jit(solution)/shard_map/ppermute | solution.py:28
  69.2 0.5 collective-permute-done.9
  69.7 3.1 %shard_map.80 = (f32[48,256]{1,0:T(8,128)S(1)}, f32[72,128]{1,0:T(8,128)S(1)}, f32[256,128]{1,0:T(8,128)}) custom-call(f32[48,256]{1,0:T(8,128)S(1)} %add_add_fusion.refs_0_, bf16[3,192,256]{2,1,0:T(8,128)(2,1)S(1)} %get-tuple-element.35.refs_1_, bf16[3,192,256]{2,1,0:T(8,128)(2,1)S(1)} %get-tuple-element.36.refs_2_, ...), custom_call_target="tpu_custom_call" | custom-call | tf_op jit(solution)/shard_map/pallas_call | solution.py:131
  72.8 0.3 collective-permute-start.12
  73.1 1.0 %collective-permute-done.12 = f32[72,128]{1,0:T(8,128)S(1)} collective-permute-done((f32[72,128]{1,0:T(8,128)S(1)}, f32[72,128]{1,0:T(8,128)S(1)}, u32[]{:S(2)}, u32[]{:S(2)}) %collective-permute-start.12) | collective-permute-done | bytes 36896 | tf_op jit(solution)/shard_map/ppermute | solution.py:28
  74.0 1.5 %collective-permute-start.13 = (f32[72,128]{1,0:T(8,128)S(1)}, f32[72,128]{1,0:T(8,128)S(1)}, u32[]{:S(2)}, u32[]{:S(2)}) collective-permute-start(f32[72,128]{1,0:T(8,128)S(1)} %add.59), channel_id=1, source_target_pairs={{0,9},{1,8},{2,11},{3,10},{4,13},{5,12},{6,15},{7,14},{8,1},{9,0},... | collective-permute-start | bytes 110600 | tf_op jit(solution)/shard_map/ppermute | solution.py:28
  75.6 3.7 %all-to-all-start.2 = ((f32[16,1,2048]{2,1,0:T(1,128)}), f32[16,1,2048]{2,1,0:T(1,128)S(1)}, u32[]{:S(2)}, u32[]{:S(2)}) async-start(f32[16,1,2048]{2,1,0:T(1,128)} %bitcast.17), calls=%async_computation.2 | async-start | bytes 262144 | tf_op jit(solution)/shard_map/all_to_all | solution.py:461
  79.3 1.9 %collective-permute-start.15 = (f32[72,128]{1,0:T(8,128)S(1)}, f32[72,128]{1,0:T(8,128)S(1)}, u32[]{:S(2)}, u32[]{:S(2)}) collective-permute-start(f32[72,128]{1,0:T(8,128)S(1)} %add.60), channel_id=1, source_target_pairs={{0,5},{1,4},{2,7},{3,6},{4,1},{5,0},{6,3},{7,2},{8,13},{9,12},{10,... | collective-permute-start | bytes 110600 | tf_op jit(solution)/shard_map/ppermute | solution.py:28
  81.2 1.4 %collective-permute-start.16 = (f32[72,128]{1,0:T(8,128)S(1)}, f32[72,128]{1,0:T(8,128)S(1)}, u32[]{:S(2)}, u32[]{:S(2)}) collective-permute-start(f32[72,128]{1,0:T(8,128)S(1)} %add.60), channel_id=1, source_target_pairs={{0,7},{1,6},{2,5},{3,4},{4,3},{5,2},{6,1},{7,0},{8,15},{9,14},{10,... | collective-permute-start | bytes 110600 | tf_op jit(solution)/shard_map/ppermute | solution.py:28
  82.6 0.0 collective-permute-start.14
  82.6 0.7 dynamic-slice_bitcast_fusion
  83.3 0.6 copy.17
  83.9 0.0 collective-permute-done.15
  83.9 2.5 %collective-permute-done.16 = f32[72,128]{1,0:T(8,128)S(1)} collective-permute-done((f32[72,128]{1,0:T(8,128)S(1)}, f32[72,128]{1,0:T(8,128)S(1)}, u32[]{:S(2)}, u32[]{:S(2)}) %collective-permute-start.16) | collective-permute-done | bytes 36896 | tf_op jit(solution)/shard_map/ppermute | solution.py:28
  86.4 1.3 %all-to-all-done.2 = f32[16,1,2048]{2,1,0:T(1,128)S(1)} async-done(((f32[16,1,2048]{2,1,0:T(1,128)}), f32[16,1,2048]{2,1,0:T(1,128)S(1)}, u32[]{:S(2)}, u32[]{:S(2)}) %all-to-all-start.2) | async-done | bytes 131104 | tf_op jit(solution)/shard_map/all_to_all | solution.py:461
  87.7 2.6 %shard_map.81 = (f32[24,48]{1,0:T(8,128)}, f32[48,144]{1,0:T(8,128)}) custom-call(f32[72,128]{1,0:T(8,128)S(1)} %add_add_fusion.1.refs_0_, f32[256,128]{1,0:T(8,128)S(1)} %bitcast.13), custom_call_target="tpu_custom_call" | custom-call | tf_op jit(solution)/shard_map/pallas_call | solution.py:131
  (16 shorter events, 0.1 us)
Async XLA Ops:
  0.6 10.4 %copy-start.1 = (f32[64,48]{0,1:T(8,128)S(1)}, f32[64,48]{0,1:T(8,128)}, u32[]{:S(2)}) copy-start(f32[64,48]{0,1:T(8,128)} %param.5) | copy-start | bytes 36868
  3.5 8.1 %collective-permute-start = (f32[12,64,256]{2,1,0:T(8,128)}, f32[12,64,256]{2,1,0:T(8,128)S(1)}, u32[]{:S(2)}, u32[]{:S(2)}) collective-permute-start(f32[12,64,256]{2,1,0:T(8,128)} %get-tuple-element.24), channel_id=1, source_target_pairs={{0,1},{1,0},{2,3},{3,2},{4,5},{5,4},{6,7},{7,6},{8,9},{9,8},{10,11... | collective-permute-start | bytes 2359304 | tf_op jit(solution)/shard_map/ppermute | solution.py:47
  4.0 18.4 %all-to-all-start = ((f32[16,1,5376]{2,1,0:T(1,128)}), f32[16,1,5376]{2,1,0:T(1,128)S(1)}, u32[]{:S(2)}, u32[]{:S(2)}) async-start(f32[16,1,5376]{2,1,0:T(1,128)} %bitcast.15), calls=%async_computation | async-start | bytes 688128 | tf_op jit(solution)/shard_map/all_to_all | solution.py:461
  11.1 11.2 %collective-permute-start.1 = (f32[64,48]{1,0:T(8,128)S(1)}, f32[64,48]{1,0:T(8,128)S(1)}, u32[]{:S(2)}, u32[]{:S(2)}) collective-permute-start(f32[64,48]{1,0:T(8,128)S(1)} %copy.13.refs_1_), channel_id=1, source_target_pairs={{0,1},{1,0},{2,3},{3,2},{4,5},{5,4},{6,7},{7,6},{8,9},{9,8},{10,11... | collective-permute-start | bytes 36872 | tf_op jit(solution)/shard_map/ppermute | solution.py:47
  23.5 17.1 %copy-start = (f32[256,48]{0,1:T(8,128)S(1)}, f32[256,48]{0,1:T(8,128)}, u32[]{:S(2)}) copy-start(f32[256,48]{0,1:T(8,128)} %param.6) | copy-start | bytes 147460
  23.5 1.2 %collective-permute-start.2 = (f32[48,128]{1,0:T(8,128)S(1)}, f32[48,128]{1,0:T(8,128)S(1)}, u32[]{:S(2)}, u32[]{:S(2)}) collective-permute-start(f32[48,128]{1,0:T(8,128)S(1)} %get-tuple-element.28), channel_id=1, source_target_pairs={{0,1},{1,0},{2,3},{3,2},{4,5},{5,4},{6,7},{7,6},{8,9},{9,8},{10,11... | collective-permute-start | bytes 73736 | tf_op jit(solution)/shard_map/ppermute | solution.py:28
  24.8 4.2 %collective-permute-start.3 = (f32[48,128]{1,0:T(8,128)S(1)}, f32[48,128]{1,0:T(8,128)S(1)}, u32[]{:S(2)}, u32[]{:S(2)}) collective-permute-start(f32[48,128]{1,0:T(8,128)S(1)} %add.48), channel_id=1, source_target_pairs={{0,9},{1,8},{2,11},{3,10},{4,13},{5,12},{6,15},{7,14},{8,1},{9,0},... | collective-permute-start | bytes 73736 | tf_op jit(solution)/shard_map/ppermute | solution.py:28
  28.9 3.4 %collective-permute-start.5 = (f32[48,128]{1,0:T(8,128)S(1)}, f32[48,128]{1,0:T(8,128)S(1)}, u32[]{:S(2)}, u32[]{:S(2)}) collective-permute-start(f32[48,128]{1,0:T(8,128)S(1)} %add.49), channel_id=1, source_target_pairs={{0,5},{1,4},{2,7},{3,6},{4,1},{5,0},{6,3},{7,2},{8,13},{9,12},{10,... | collective-permute-start | bytes 73736 | tf_op jit(solution)/shard_map/ppermute | solution.py:28
  29.6 4.2 %collective-permute-start.6 = (f32[48,128]{1,0:T(8,128)S(1)}, f32[48,128]{1,0:T(8,128)S(1)}, u32[]{:S(2)}, u32[]{:S(2)}) collective-permute-start(f32[48,128]{1,0:T(8,128)S(1)} %add.49), channel_id=1, source_target_pairs={{0,7},{1,6},{2,5},{3,4},{4,3},{5,2},{6,1},{7,0},{8,15},{9,14},{10,... | collective-permute-start | bytes 73736 | tf_op jit(solution)/shard_map/ppermute | solution.py:28
  30.6 3.7 %collective-permute-start.4 = (f32[48,128]{1,0:T(8,128)S(1)}, f32[48,128]{1,0:T(8,128)S(1)}, u32[]{:S(2)}, u32[]{:S(2)}) collective-permute-start(f32[48,128]{1,0:T(8,128)S(1)} %add.49), channel_id=1, source_target_pairs={{0,3},{1,2},{2,1},{3,0},{4,7},{5,6},{6,5},{7,4},{8,11},{9,10},{10,... | collective-permute-start | bytes 73736 | tf_op jit(solution)/shard_map/ppermute | solution.py:28
  37.1 19.1 %all-to-all-start.1 = ((f32[16,1,9216]{2,1,0:T(1,128)}), f32[16,1,9216]{2,1,0:T(1,128)S(1)}, u32[]{:S(2)}, u32[]{:S(2)}) async-start(f32[16,1,9216]{2,1,0:T(1,128)} %bitcast.14), calls=%async_computation.1 | async-start | bytes 1179648 | tf_op jit(solution)/shard_map/all_to_all | solution.py:461
  56.9 1.3 %collective-permute-start.7 = (f32[48,256]{1,0:T(8,128)S(1)}, f32[48,256]{1,0:T(8,128)S(1)}, u32[]{:S(2)}, u32[]{:S(2)}) collective-permute-start(f32[48,256]{1,0:T(8,128)S(1)} %get-tuple-element.34), channel_id=1, source_target_pairs={{0,1},{1,0},{2,3},{3,2},{4,5},{5,4},{6,7},{7,6},{8,9},{9,8},{10,11... | collective-permute-start | bytes 147464 | tf_op jit(solution)/shard_map/ppermute | solution.py:28
  58.2 4.7 %collective-permute-start.8 = (f32[48,256]{1,0:T(8,128)S(1)}, f32[48,256]{1,0:T(8,128)S(1)}, u32[]{:S(2)}, u32[]{:S(2)}) collective-permute-start(f32[48,256]{1,0:T(8,128)S(1)} %add.54), channel_id=1, source_target_pairs={{0,9},{1,8},{2,11},{3,10},{4,13},{5,12},{6,15},{7,14},{8,1},{9,0},... | collective-permute-start | bytes 147464 | tf_op jit(solution)/shard_map/ppermute | solution.py:28
  62.9 3.8 %collective-permute-start.10 = (f32[48,256]{1,0:T(8,128)S(1)}, f32[48,256]{1,0:T(8,128)S(1)}, u32[]{:S(2)}, u32[]{:S(2)}) collective-permute-start(f32[48,256]{1,0:T(8,128)S(1)} %add.55), channel_id=1, source_target_pairs={{0,5},{1,4},{2,7},{3,6},{4,1},{5,0},{6,3},{7,2},{8,13},{9,12},{10,... | collective-permute-start | bytes 147464 | tf_op jit(solution)/shard_map/ppermute | solution.py:28
  64.4 4.7 %collective-permute-start.11 = (f32[48,256]{1,0:T(8,128)S(1)}, f32[48,256]{1,0:T(8,128)S(1)}, u32[]{:S(2)}, u32[]{:S(2)}) collective-permute-start(f32[48,256]{1,0:T(8,128)S(1)} %add.55), channel_id=1, source_target_pairs={{0,7},{1,6},{2,5},{3,4},{4,3},{5,2},{6,1},{7,0},{8,15},{9,14},{10,... | collective-permute-start | bytes 147464 | tf_op jit(solution)/shard_map/ppermute | solution.py:28
  65.0 4.7 %collective-permute-start.9 = (f32[48,256]{1,0:T(8,128)S(1)}, f32[48,256]{1,0:T(8,128)S(1)}, u32[]{:S(2)}, u32[]{:S(2)}) collective-permute-start(f32[48,256]{1,0:T(8,128)S(1)} %add.55), channel_id=1, source_target_pairs={{0,3},{1,2},{2,1},{3,0},{4,7},{5,6},{6,5},{7,4},{8,11},{9,10},{10,... | collective-permute-start | bytes 147464 | tf_op jit(solution)/shard_map/ppermute | solution.py:28
  72.8 1.3 %collective-permute-start.12 = (f32[72,128]{1,0:T(8,128)S(1)}, f32[72,128]{1,0:T(8,128)S(1)}, u32[]{:S(2)}, u32[]{:S(2)}) collective-permute-start(f32[72,128]{1,0:T(8,128)S(1)} %get-tuple-element.38), channel_id=1, source_target_pairs={{0,1},{1,0},{2,3},{3,2},{4,5},{5,4},{6,7},{7,6},{8,9},{9,8},{10,11... | collective-permute-start | bytes 110600 | tf_op jit(solution)/shard_map/ppermute | solution.py:28
  74.0 5.2 %collective-permute-start.13 = (f32[72,128]{1,0:T(8,128)S(1)}, f32[72,128]{1,0:T(8,128)S(1)}, u32[]{:S(2)}, u32[]{:S(2)}) collective-permute-start(f32[72,128]{1,0:T(8,128)S(1)} %add.59), channel_id=1, source_target_pairs={{0,9},{1,8},{2,11},{3,10},{4,13},{5,12},{6,15},{7,14},{8,1},{9,0},... | collective-permute-start | bytes 110600 | tf_op jit(solution)/shard_map/ppermute | solution.py:28
  75.6 12.2 %all-to-all-start.2 = ((f32[16,1,2048]{2,1,0:T(1,128)}), f32[16,1,2048]{2,1,0:T(1,128)S(1)}, u32[]{:S(2)}, u32[]{:S(2)}) async-start(f32[16,1,2048]{2,1,0:T(1,128)} %bitcast.17), calls=%async_computation.2 | async-start | bytes 262144 | tf_op jit(solution)/shard_map/all_to_all | solution.py:461
  79.3 4.6 %collective-permute-start.15 = (f32[72,128]{1,0:T(8,128)S(1)}, f32[72,128]{1,0:T(8,128)S(1)}, u32[]{:S(2)}, u32[]{:S(2)}) collective-permute-start(f32[72,128]{1,0:T(8,128)S(1)} %add.60), channel_id=1, source_target_pairs={{0,5},{1,4},{2,7},{3,6},{4,1},{5,0},{6,3},{7,2},{8,13},{9,12},{10,... | collective-permute-start | bytes 110600 | tf_op jit(solution)/shard_map/ppermute | solution.py:28
  81.2 5.2 %collective-permute-start.16 = (f32[72,128]{1,0:T(8,128)S(1)}, f32[72,128]{1,0:T(8,128)S(1)}, u32[]{:S(2)}, u32[]{:S(2)}) collective-permute-start(f32[72,128]{1,0:T(8,128)S(1)} %add.60), channel_id=1, source_target_pairs={{0,7},{1,6},{2,5},{3,4},{4,3},{5,2},{6,1},{7,0},{8,15},{9,14},{10,... | collective-permute-start | bytes 110600 | tf_op jit(solution)/shard_map/ppermute | solution.py:28
  82.6 3.9 %collective-permute-start.14 = (f32[72,128]{1,0:T(8,128)S(1)}, f32[72,128]{1,0:T(8,128)S(1)}, u32[]{:S(2)}, u32[]{:S(2)}) collective-permute-start(f32[72,128]{1,0:T(8,128)S(1)} %add.60), channel_id=1, source_target_pairs={{0,3},{1,2},{2,1},{3,0},{4,7},{5,6},{6,5},{7,4},{8,11},{9,10},{10,... | collective-permute-start | bytes 110600 | tf_op jit(solution)/shard_map/ppermute | solution.py:28

commit v9 on v8

--- a/solution.py
+++ b/solution.py
@@ -239,14 +239,15 @@
         for h in range(2):
             fetch(at, h).wait()
         hand(at).start()
+        value = [room[at, h, q] for q in range(steps) for h in range(2)]
+        high, low = split(jnp.concatenate(value))
+        first = lax.dot_general(both, high, nt, preferred_element_type=jnp.float32)
+        second = lax.dot_general(two_high, low, nt, preferred_element_type=jnp.float32)
+        along = first[:rank] + (first[rank:] + second)
         for q in range(steps):
-            high, low = split(room[at, :, q].reshape(2 * rows, cols))
-            first = lax.dot_general(both, high, nt, preferred_element_type=jnp.float32)
-            second = lax.dot_general(two_high, low, nt, preferred_element_type=jnp.float32)
-            along = first[:rank] + (first[rank:] + second)
             for s in range(share):
                 flat[pl.ds((at * steps + q) * share + s, count, stride=pitch), :] = along[
-                    s * count : (s + 1) * count
+                    s * count : (s + 1) * count, q * lanes : (q + 1) * lanes
                 ]
     leave.start()
     for at in range(chunks):
@@ -307,8 +308,10 @@
     mixed = split(value)
     lane = lax.broadcasted_iota(jnp.int32, (rank, lanes), 1)
     pieces = []
+    field = jnp.concatenate([got[pl.ds(s, size, stride=share), :] for s in range(share)], axis=1)
+    field = dot3(mixed, field, tn)
     for s in range(share):
-        value = dot3(mixed, got[pl.ds(s, size, stride=share), :], tn)
+        value = field[:, s * lanes : (s + 1) * lanes]
         first = value[:rank] + pltpu.roll(value[part : part + rank], part, 1)
         second = (
             pltpu.roll(value[2 * part : 2 * part + rank], part, 1)
@@ -360,12 +363,15 @@
     parts = two.shape[0] // lanes
     size = count * half
     table = split(three[:, : two.shape[1]])
-    pieces = []
+    field = []
     for s in range(share):
         value = split(taken(got, s, parts, share * parts, size))
         high[s], low[s] = value
-        pieces.append(dot3(table, value, tn))
-    unfold = split(jnp.concatenate(pieces))
+        field.append(value)
+    field = [jnp.concatenate(value, axis=1) for value in zip(*field)]
+    field = dot3(table, tuple(field), tn)
+    cols = parts * lanes
+    unfold = split(jnp.concatenate([field[:, s * cols : (s + 1) * cols] for s in range(share)]))
     out[...] = dot3(dot3(unfold, two[...]), unfold, tn)
 
 
@@ -414,12 +420,8 @@
         )
     copy = pltpu.make_async_copy(flat, sent, sem)
     copy.start()
-    table = split(three[:, :rank])
-    result = None
-    for value in pieces:
-        value = split(value)
-        term = dot3(dot3(value, table), value, tn)
-        result = term if result is None else result + term
+    value = split(jnp.concatenate(pieces))
+    result = dot3(dot3(value, three[:, :rank]), value, tn)
     for h in range(whole):
         out[h * rank : (h + 1) * rank, :] = result[:, h * lanes : (h + 1) * lanes]
     if rest:
@@ -440,9 +442,8 @@
     room[...] = value.T
     depth = basis.shape[0]
     basis[...] = room[pl.ds(pl.multiple_of(lax.axis_index("wide") * depth, 8), depth), :]
-    value = split(value)
+    rows = []
     for b in range(share):
-        rows = []
         for s in range(share):
             at = b * share + s
             pieces = [
@@ -452,7 +453,9 @@
                 end = got[pl.ds(share * share * whole + at // 2, count, stride=pitch), :]
                 pieces.append(end[:, lanes // 2 :] if at % 2 else end[:, : lanes // 2])
             rows.append(jnp.concatenate(pieces, axis=1))
-        core[:, b * rank : (b + 1) * rank] = dot3(jnp.concatenate(rows), value, nt)
+    value = dot3(jnp.concatenate(rows), value, nt)
+    for b in range(share):
+        core[:, b * rank : (b + 1) * rank] = value[b * rank : (b + 1) * rank]
 
 
 def exchange(value, count):

time: 90.8 us -> 90.5 us (level)
  no operation moved by 1% of the time
where the time goes in v9:
time: 90.5 us; the launch traced here: 90 us
  waiting for transfers between devices  42.9 us (47%)
  starting transfers between devices  30.7 us (34%)
  Pallas kernels  14.1 us (16%)
  local copies, waits for them, and re-layouts  1.48 us (2%)
    all_to_all x3, waiting for transfers between devices, exchange(): return lax.all_to_all(flat, group, 0, 0, tiled=True).reshape(rows, lanes)  26.2 us
    ppermute x15, waiting for transfers between devices, moved(): return lax.ppermute(part, group, [(at, at ^ mask) for at in range(count)])  16.7 us
    ppermute x15, starting transfers between devices, moved(): return lax.ppermute(part, group, [(at, at ^ mask) for at in range(count)])  15.4 us
    all_to_all x3, starting transfers between devices, exchange(): return lax.all_to_all(flat, group, 0, 0, tiled=True).reshape(rows, lanes)  14.3 us
    pallas_call x7, Pallas kernels, call(): pl.pallas_call(body, in_specs=[outside if at in away else inside for at i...  14.1 us
  transfers between devices with their start and end apart: 20, of which 14 were waited for; matrix products, arithmetic and copies ran while one was open for 2% of the time, Pallas kernels for 1%

profile of v9, /device:TPU:0, one launch (start us, length us, event | category | flops | bytes accessed | tf_op | source)
XLA Modules:
  0.0 90.0 jit_solution(2355362377877995611)
XLA Ops:
  0.6 2.8 %shard_map.75 = (f32[672,128]{1,0:T(8,128)}, f32[12,64,256]{2,1,0:T(8,128)}) custom-call(f32[24,64,256]{2,1,0:T(8,128)} %field.1, f32[48,256]{1,0:T(8,128)} %bitcast.16, f32[24,48]{1,0:T(8,128)} %refs_2_.1), custom_call_target="tpu_custom_call" | custom-call | tf_op jit(solution)/shard_map/pallas_call | solution.py:131
  3.4 0.6 collective-permute-start
  4.0 7.0 %all-to-all-start = ((f32[16,1,5376]{2,1,0:T(1,128)}), f32[16,1,5376]{2,1,0:T(1,128)S(1)}, u32[]{:S(2)}, u32[]{:S(2)}) async-start(f32[16,1,5376]{2,1,0:T(1,128)} %bitcast.15), calls=%async_computation | async-start | bytes 688128 | tf_op jit(solution)/shard_map/all_to_all | solution.py:464
  11.0 0.1 copy.13.refs_1_
  11.1 0.4 collective-permute-start.1
  11.5 0.0 collective-permute-done.other
  11.5 1.2 %shard_map.76 = (bf16[12,128,256]{2,1,0:T(8,128)(2,1)S(1)}, bf16[12,128,256]{2,1,0:T(8,128)(2,1)S(1)}) custom-call(f32[24,64,256]{2,1,0:T(8,128)} %field.1, f32[12,64,256]{2,1,0:T(8,128)S(1)} %collective-permute-done.other), custom_call_target="tpu_custom_call" | custom-call | tf_op jit(solution)/shard_map/pallas_call | solution.py:131
  12.8 9.5 %all-to-all-done = f32[16,1,5376]{2,1,0:T(1,128)S(1)} async-done(((f32[16,1,5376]{2,1,0:T(1,128)}), f32[16,1,5376]{2,1,0:T(1,128)S(1)}, u32[]{:S(2)}, u32[]{:S(2)}) %all-to-all-start) | async-done | bytes 344096 | tf_op jit(solution)/shard_map/all_to_all | solution.py:464
  22.3 0.0 collective-permute-done.1.refs_2_
  22.3 1.0 %shard_map.77 = (f32[48,128]{1,0:T(8,128)S(1)}, f32[192,128]{1,0:T(8,128)S(1)}) custom-call(f32[672,128]{1,0:T(8,128)S(1)} %bitcast.12, f32[64,48]{1,0:T(8,128)S(1)} %copy.13.refs_1_, f32[64,48]{1,0:T(8,128)S(1)} %collective-permute-done.1.refs_2_), custom_call_target="tpu_custom_call" | custom-call | tf_op jit(solution)/shard_map/pallas_call | solution.py:131
  23.3 0.1 collective-permute-start.2
  23.4 1.1 %collective-permute-done.2 = f32[48,128]{1,0:T(8,128)S(1)} collective-permute-done((f32[48,128]{1,0:T(8,128)S(1)}, f32[48,128]{1,0:T(8,128)S(1)}, u32[]{:S(2)}, u32[]{:S(2)}) %collective-permute-start.2) | collective-permute-done | bytes 24608 | tf_op jit(solution)/shard_map/ppermute | solution.py:28
  24.5 1.3 %collective-permute-start.3 = (f32[48,128]{1,0:T(8,128)S(1)}, f32[48,128]{1,0:T(8,128)S(1)}, u32[]{:S(2)}, u32[]{:S(2)}) collective-permute-start(f32[48,128]{1,0:T(8,128)S(1)} %add.48), channel_id=1, source_target_pairs={{0,9},{1,8},{2,11},{3,10},{4,13},{5,12},{6,15},{7,14},{8,1},{9,0},... | collective-permute-start | bytes 73736 | tf_op jit(solution)/shard_map/ppermute | solution.py:28
  25.8 2.9 %collective-permute-done.3 = f32[48,128]{1,0:T(8,128)S(1)} collective-permute-done((f32[48,128]{1,0:T(8,128)S(1)}, f32[48,128]{1,0:T(8,128)S(1)}, u32[]{:S(2)}, u32[]{:S(2)}) %collective-permute-start.3) | collective-permute-done | bytes 24608 | tf_op jit(solution)/shard_map/ppermute | solution.py:28
  28.7 0.7 collective-permute-start.5
  29.4 1.0 %collective-permute-start.6 = (f32[48,128]{1,0:T(8,128)S(1)}, f32[48,128]{1,0:T(8,128)S(1)}, u32[]{:S(2)}, u32[]{:S(2)}) collective-permute-start(f32[48,128]{1,0:T(8,128)S(1)} %add.49), channel_id=1, source_target_pairs={{0,7},{1,6},{2,5},{3,4},{4,3},{5,2},{6,1},{7,0},{8,15},{9,14},{10,... | collective-permute-start | bytes 73736 | tf_op jit(solution)/shard_map/ppermute | solution.py:28
  30.4 1.7 %collective-permute-start.4 = (f32[48,128]{1,0:T(8,128)S(1)}, f32[48,128]{1,0:T(8,128)S(1)}, u32[]{:S(2)}, u32[]{:S(2)}) collective-permute-start(f32[48,128]{1,0:T(8,128)S(1)} %add.49), channel_id=1, source_target_pairs={{0,3},{1,2},{2,1},{3,0},{4,7},{5,6},{6,5},{7,4},{8,11},{9,10},{10,... | collective-permute-start | bytes 73736 | tf_op jit(solution)/shard_map/ppermute | solution.py:28
  32.1 1.4 %collective-permute-done.6 = f32[48,128]{1,0:T(8,128)S(1)} collective-permute-done((f32[48,128]{1,0:T(8,128)S(1)}, f32[48,128]{1,0:T(8,128)S(1)}, u32[]{:S(2)}, u32[]{:S(2)}) %collective-permute-start.6) | collective-permute-done | bytes 24608 | tf_op jit(solution)/shard_map/ppermute | solution.py:28
  33.6 0.5 collective-permute-done.4
  34.1 2.7 %shard_map.78 = (f32[48,128]{1,0:T(8,128)S(1)}, f32[16,72,128]{2,1,0:T(8,128)}) custom-call(f32[48,128]{1,0:T(8,128)S(1)} %add_add_fusion.2.refs_0_, bf16[12,128,256]{2,1,0:T(8,128)(2,1)S(1)} %get-tuple-element.29.refs_1_, bf16[12,128,256]{2,1,0:T(8,128)(2,1)S(1)} %get-tuple-element.30.refs_2_), custom_call_target="tpu_custom_call" | custom-call | tf_op jit(solution)/shard_map/pallas_call | solution.py:131
  36.8 3.6 %all-to-all-start.1 = ((f32[16,1,9216]{2,1,0:T(1,128)}), f32[16,1,9216]{2,1,0:T(1,128)S(1)}, u32[]{:S(2)}, u32[]{:S(2)}) async-start(f32[16,1,9216]{2,1,0:T(1,128)} %bitcast.14), calls=%async_computation.1 | async-start | bytes 1179648 | tf_op jit(solution)/shard_map/all_to_all | solution.py:464
  40.4 0.1 copy.15.refs_1_
  40.5 15.4 %all-to-all-done.1 = f32[16,1,9216]{2,1,0:T(1,128)S(1)} async-done(((f32[16,1,9216]{2,1,0:T(1,128)}), f32[16,1,9216]{2,1,0:T(1,128)S(1)}, u32[]{:S(2)}, u32[]{:S(2)}) %all-to-all-start.1) | async-done | bytes 589856 | tf_op jit(solution)/shard_map/all_to_all | solution.py:464
  55.9 0.8 shard_map.79
  56.7 0.1 collective-permute-start.7
  56.8 1.2 %collective-permute-done.7 = f32[48,256]{1,0:T(8,128)S(1)} collective-permute-done((f32[48,256]{1,0:T(8,128)S(1)}, f32[48,256]{1,0:T(8,128)S(1)}, u32[]{:S(2)}, u32[]{:S(2)}) %collective-permute-start.7) | collective-permute-done | bytes 49184 | tf_op jit(solution)/shard_map/ppermute | solution.py:28
  58.0 2.3 %collective-permute-start.8 = (f32[48,256]{1,0:T(8,128)S(1)}, f32[48,256]{1,0:T(8,128)S(1)}, u32[]{:S(2)}, u32[]{:S(2)}) collective-permute-start(f32[48,256]{1,0:T(8,128)S(1)} %add.54), channel_id=1, source_target_pairs={{0,9},{1,8},{2,11},{3,10},{4,13},{5,12},{6,15},{7,14},{8,1},{9,0},... | collective-permute-start | bytes 147464 | tf_op jit(solution)/shard_map/ppermute | solution.py:28
  60.3 2.4 %collective-permute-done.8 = f32[48,256]{1,0:T(8,128)S(1)} collective-permute-done((f32[48,256]{1,0:T(8,128)S(1)}, f32[48,256]{1,0:T(8,128)S(1)}, u32[]{:S(2)}, u32[]{:S(2)}) %collective-permute-start.8) | collective-permute-done | bytes 49184 | tf_op jit(solution)/shard_map/ppermute | solution.py:28
  62.7 1.5 %collective-permute-start.10 = (f32[48,256]{1,0:T(8,128)S(1)}, f32[48,256]{1,0:T(8,128)S(1)}, u32[]{:S(2)}, u32[]{:S(2)}) collective-permute-start(f32[48,256]{1,0:T(8,128)S(1)} %add.55), channel_id=1, source_target_pairs={{0,5},{1,4},{2,7},{3,6},{4,1},{5,0},{6,3},{7,2},{8,13},{9,12},{10,... | collective-permute-start | bytes 147464 | tf_op jit(solution)/shard_map/ppermute | solution.py:28
  64.2 0.6 collective-permute-start.11
  64.8 1.0 %collective-permute-start.9 = (f32[48,256]{1,0:T(8,128)S(1)}, f32[48,256]{1,0:T(8,128)S(1)}, u32[]{:S(2)}, u32[]{:S(2)}) collective-permute-start(f32[48,256]{1,0:T(8,128)S(1)} %add.55), channel_id=1, source_target_pairs={{0,3},{1,2},{2,1},{3,0},{4,7},{5,6},{6,5},{7,4},{8,11},{9,10},{10,... | collective-permute-start | bytes 147464 | tf_op jit(solution)/shard_map/ppermute | solution.py:28
  65.7 0.8 collective-permute-done.10
  66.5 2.4 %collective-permute-done.11 = f32[48,256]{1,0:T(8,128)S(1)} collective-permute-done((f32[48,256]{1,0:T(8,128)S(1)}, f32[48,256]{1,0:T(8,128)S(1)}, u32[]{:S(2)}, u32[]{:S(2)}) %collective-permute-start.11) | collective-permute-done | bytes 49184 | tf_op jit(solution)/shard_map/ppermute | solution.py:28
  68.9 0.5 collective-permute-done.9
  69.4 3.0 %shard_map.80 = (f32[48,256]{1,0:T(8,128)S(1)}, f32[72,128]{1,0:T(8,128)S(1)}, f32[256,128]{1,0:T(8,128)}) custom-call(f32[48,256]{1,0:T(8,128)S(1)} %add_add_fusion.refs_0_, bf16[3,192,256]{2,1,0:T(8,128)(2,1)S(1)} %get-tuple-element.35.refs_1_, bf16[3,192,256]{2,1,0:T(8,128)(2,1)S(1)} %get-tuple-element.36.refs_2_, ...), custom_call_target="tpu_custom_call" | custom-call | tf_op jit(solution)/shard_map/pallas_call | solution.py:131
  72.4 0.3 collective-permute-start.12
  72.8 1.0 %collective-permute-done.12 = f32[72,128]{1,0:T(8,128)S(1)} collective-permute-done((f32[72,128]{1,0:T(8,128)S(1)}, f32[72,128]{1,0:T(8,128)S(1)}, u32[]{:S(2)}, u32[]{:S(2)}) %collective-permute-start.12) | collective-permute-done | bytes 36896 | tf_op jit(solution)/shard_map/ppermute | solution.py:28
  73.7 1.5 %collective-permute-start.13 = (f32[72,128]{1,0:T(8,128)S(1)}, f32[72,128]{1,0:T(8,128)S(1)}, u32[]{:S(2)}, u32[]{:S(2)}) collective-permute-start(f32[72,128]{1,0:T(8,128)S(1)} %add.59), channel_id=1, source_target_pairs={{0,9},{1,8},{2,11},{3,10},{4,13},{5,12},{6,15},{7,14},{8,1},{9,0},... | collective-permute-start | bytes 110600 | tf_op jit(solution)/shard_map/ppermute | solution.py:28
  75.3 3.7 %all-to-all-start.2 = ((f32[16,1,2048]{2,1,0:T(1,128)}), f32[16,1,2048]{2,1,0:T(1,128)S(1)}, u32[]{:S(2)}, u32[]{:S(2)}) async-start(f32[16,1,2048]{2,1,0:T(1,128)} %bitcast.17), calls=%async_computation.2 | async-start | bytes 262144 | tf_op jit(solution)/shard_map/all_to_all | solution.py:464
  79.0 1.9 %collective-permute-start.15 = (f32[72,128]{1,0:T(8,128)S(1)}, f32[72,128]{1,0:T(8,128)S(1)}, u32[]{:S(2)}, u32[]{:S(2)}) collective-permute-start(f32[72,128]{1,0:T(8,128)S(1)} %add.60), channel_id=1, source_target_pairs={{0,5},{1,4},{2,7},{3,6},{4,1},{5,0},{6,3},{7,2},{8,13},{9,12},{10,... | collective-permute-start | bytes 110600 | tf_op jit(solution)/shard_map/ppermute | solution.py:28
  80.9 1.4 %collective-permute-start.16 = (f32[72,128]{1,0:T(8,128)S(1)}, f32[72,128]{1,0:T(8,128)S(1)}, u32[]{:S(2)}, u32[]{:S(2)}) collective-permute-start(f32[72,128]{1,0:T(8,128)S(1)} %add.60), channel_id=1, source_target_pairs={{0,7},{1,6},{2,5},{3,4},{4,3},{5,2},{6,1},{7,0},{8,15},{9,14},{10,... | collective-permute-start | bytes 110600 | tf_op jit(solution)/shard_map/ppermute | solution.py:28
  82.3 0.0 collective-permute-start.14
  82.3 0.7 dynamic-slice_bitcast_fusion
  83.0 0.6 copy.17
  83.6 0.0 collective-permute-done.15
  83.6 2.5 %collective-permute-done.16 = f32[72,128]{1,0:T(8,128)S(1)} collective-permute-done((f32[72,128]{1,0:T(8,128)S(1)}, f32[72,128]{1,0:T(8,128)S(1)}, u32[]{:S(2)}, u32[]{:S(2)}) %collective-permute-start.16) | collective-permute-done | bytes 36896 | tf_op jit(solution)/shard_map/ppermute | solution.py:28
  86.1 1.3 %all-to-all-done.2 = f32[16,1,2048]{2,1,0:T(1,128)S(1)} async-done(((f32[16,1,2048]{2,1,0:T(1,128)}), f32[16,1,2048]{2,1,0:T(1,128)S(1)}, u32[]{:S(2)}, u32[]{:S(2)}) %all-to-all-start.2) | async-done | bytes 131104 | tf_op jit(solution)/shard_map/all_to_all | solution.py:464
  87.4 2.6 %shard_map.81 = (f32[24,48]{1,0:T(8,128)}, f32[48,144]{1,0:T(8,128)}) custom-call(f32[72,128]{1,0:T(8,128)S(1)} %add_add_fusion.1.refs_0_, f32[256,128]{1,0:T(8,128)S(1)} %bitcast.13), custom_call_target="tpu_custom_call" | custom-call | tf_op jit(solution)/shard_map/pallas_call | solution.py:131
  (16 shorter events, 0.1 us)
Async XLA Ops:
  0.6 10.4 %copy-start.1 = (f32[64,48]{0,1:T(8,128)S(1)}, f32[64,48]{0,1:T(8,128)}, u32[]{:S(2)}) copy-start(f32[64,48]{0,1:T(8,128)} %param.5) | copy-start | bytes 36868
  3.4 8.1 %collective-permute-start = (f32[12,64,256]{2,1,0:T(8,128)}, f32[12,64,256]{2,1,0:T(8,128)S(1)}, u32[]{:S(2)}, u32[]{:S(2)}) collective-permute-start(f32[12,64,256]{2,1,0:T(8,128)} %get-tuple-element.24), channel_id=1, source_target_pairs={{0,1},{1,0},{2,3},{3,2},{4,5},{5,4},{6,7},{7,6},{8,9},{9,8},{10,11... | collective-permute-start | bytes 2359304 | tf_op jit(solution)/shard_map/ppermute | solution.py:47
  4.0 18.4 %all-to-all-start = ((f32[16,1,5376]{2,1,0:T(1,128)}), f32[16,1,5376]{2,1,0:T(1,128)S(1)}, u32[]{:S(2)}, u32[]{:S(2)}) async-start(f32[16,1,5376]{2,1,0:T(1,128)} %bitcast.15), calls=%async_computation | async-start | bytes 688128 | tf_op jit(solution)/shard_map/all_to_all | solution.py:464
  11.1 11.2 %collective-permute-start.1 = (f32[64,48]{1,0:T(8,128)S(1)}, f32[64,48]{1,0:T(8,128)S(1)}, u32[]{:S(2)}, u32[]{:S(2)}) collective-permute-start(f32[64,48]{1,0:T(8,128)S(1)} %copy.13.refs_1_), channel_id=1, source_target_pairs={{0,1},{1,0},{2,3},{3,2},{4,5},{5,4},{6,7},{7,6},{8,9},{9,8},{10,11... | collective-permute-start | bytes 36872 | tf_op jit(solution)/shard_map/ppermute | solution.py:47
  23.3 17.1 %copy-start = (f32[256,48]{0,1:T(8,128)S(1)}, f32[256,48]{0,1:T(8,128)}, u32[]{:S(2)}) copy-start(f32[256,48]{0,1:T(8,128)} %param.6) | copy-start | bytes 147460
  23.3 1.2 %collective-permute-start.2 = (f32[48,128]{1,0:T(8,128)S(1)}, f32[48,128]{1,0:T(8,128)S(1)}, u32[]{:S(2)}, u32[]{:S(2)}) collective-permute-start(f32[48,128]{1,0:T(8,128)S(1)} %get-tuple-element.28), channel_id=1, source_target_pairs={{0,1},{1,0},{2,3},{3,2},{4,5},{5,4},{6,7},{7,6},{8,9},{9,8},{10,11... | collective-permute-start | bytes 73736 | tf_op jit(solution)/shard_map/ppermute | solution.py:28
  24.5 4.2 %collective-permute-start.3 = (f32[48,128]{1,0:T(8,128)S(1)}, f32[48,128]{1,0:T(8,128)S(1)}, u32[]{:S(2)}, u32[]{:S(2)}) collective-permute-start(f32[48,128]{1,0:T(8,128)S(1)} %add.48), channel_id=1, source_target_pairs={{0,9},{1,8},{2,11},{3,10},{4,13},{5,12},{6,15},{7,14},{8,1},{9,0},... | collective-permute-start | bytes 73736 | tf_op jit(solution)/shard_map/ppermute | solution.py:28
  28.7 3.4 %collective-permute-start.5 = (f32[48,128]{1,0:T(8,128)S(1)}, f32[48,128]{1,0:T(8,128)S(1)}, u32[]{:S(2)}, u32[]{:S(2)}) collective-permute-start(f32[48,128]{1,0:T(8,128)S(1)} %add.49), channel_id=1, source_target_pairs={{0,5},{1,4},{2,7},{3,6},{4,1},{5,0},{6,3},{7,2},{8,13},{9,12},{10,... | collective-permute-start | bytes 73736 | tf_op jit(solution)/shard_map/ppermute | solution.py:28
  29.4 4.2 %collective-permute-start.6 = (f32[48,128]{1,0:T(8,128)S(1)}, f32[48,128]{1,0:T(8,128)S(1)}, u32[]{:S(2)}, u32[]{:S(2)}) collective-permute-start(f32[48,128]{1,0:T(8,128)S(1)} %add.49), channel_id=1, source_target_pairs={{0,7},{1,6},{2,5},{3,4},{4,3},{5,2},{6,1},{7,0},{8,15},{9,14},{10,... | collective-permute-start | bytes 73736 | tf_op jit(solution)/shard_map/ppermute | solution.py:28
  30.4 3.7 %collective-permute-start.4 = (f32[48,128]{1,0:T(8,128)S(1)}, f32[48,128]{1,0:T(8,128)S(1)}, u32[]{:S(2)}, u32[]{:S(2)}) collective-permute-start(f32[48,128]{1,0:T(8,128)S(1)} %add.49), channel_id=1, source_target_pairs={{0,3},{1,2},{2,1},{3,0},{4,7},{5,6},{6,5},{7,4},{8,11},{9,10},{10,... | collective-permute-start | bytes 73736 | tf_op jit(solution)/shard_map/ppermute | solution.py:28
  36.8 19.1 %all-to-all-start.1 = ((f32[16,1,9216]{2,1,0:T(1,128)}), f32[16,1,9216]{2,1,0:T(1,128)S(1)}, u32[]{:S(2)}, u32[]{:S(2)}) async-start(f32[16,1,9216]{2,1,0:T(1,128)} %bitcast.14), calls=%async_computation.1 | async-start | bytes 1179648 | tf_op jit(solution)/shard_map/all_to_all | solution.py:464
  56.7 1.3 %collective-permute-start.7 = (f32[48,256]{1,0:T(8,128)S(1)}, f32[48,256]{1,0:T(8,128)S(1)}, u32[]{:S(2)}, u32[]{:S(2)}) collective-permute-start(f32[48,256]{1,0:T(8,128)S(1)} %get-tuple-element.34), channel_id=1, source_target_pairs={{0,1},{1,0},{2,3},{3,2},{4,5},{5,4},{6,7},{7,6},{8,9},{9,8},{10,11... | collective-permute-start | bytes 147464 | tf_op jit(solution)/shard_map/ppermute | solution.py:28
  58.0 4.7 %collective-permute-start.8 = (f32[48,256]{1,0:T(8,128)S(1)}, f32[48,256]{1,0:T(8,128)S(1)}, u32[]{:S(2)}, u32[]{:S(2)}) collective-permute-start(f32[48,256]{1,0:T(8,128)S(1)} %add.54), channel_id=1, source_target_pairs={{0,9},{1,8},{2,11},{3,10},{4,13},{5,12},{6,15},{7,14},{8,1},{9,0},... | collective-permute-start | bytes 147464 | tf_op jit(solution)/shard_map/ppermute | solution.py:28
  62.7 3.8 %collective-permute-start.10 = (f32[48,256]{1,0:T(8,128)S(1)}, f32[48,256]{1,0:T(8,128)S(1)}, u32[]{:S(2)}, u32[]{:S(2)}) collective-permute-start(f32[48,256]{1,0:T(8,128)S(1)} %add.55), channel_id=1, source_target_pairs={{0,5},{1,4},{2,7},{3,6},{4,1},{5,0},{6,3},{7,2},{8,13},{9,12},{10,... | collective-permute-start | bytes 147464 | tf_op jit(solution)/shard_map/ppermute | solution.py:28
  64.2 4.7 %collective-permute-start.11 = (f32[48,256]{1,0:T(8,128)S(1)}, f32[48,256]{1,0:T(8,128)S(1)}, u32[]{:S(2)}, u32[]{:S(2)}) collective-permute-start(f32[48,256]{1,0:T(8,128)S(1)} %add.55), channel_id=1, source_target_pairs={{0,7},{1,6},{2,5},{3,4},{4,3},{5,2},{6,1},{7,0},{8,15},{9,14},{10,... | collective-permute-start | bytes 147464 | tf_op jit(solution)/shard_map/ppermute | solution.py:28
  64.8 4.7 %collective-permute-start.9 = (f32[48,256]{1,0:T(8,128)S(1)}, f32[48,256]{1,0:T(8,128)S(1)}, u32[]{:S(2)}, u32[]{:S(2)}) collective-permute-start(f32[48,256]{1,0:T(8,128)S(1)} %add.55), channel_id=1, source_target_pairs={{0,3},{1,2},{2,1},{3,0},{4,7},{5,6},{6,5},{7,4},{8,11},{9,10},{10,... | collective-permute-start | bytes 147464 | tf_op jit(solution)/shard_map/ppermute | solution.py:28
  72.4 1.3 %collective-permute-start.12 = (f32[72,128]{1,0:T(8,128)S(1)}, f32[72,128]{1,0:T(8,128)S(1)}, u32[]{:S(2)}, u32[]{:S(2)}) collective-permute-start(f32[72,128]{1,0:T(8,128)S(1)} %get-tuple-element.38), channel_id=1, source_target_pairs={{0,1},{1,0},{2,3},{3,2},{4,5},{5,4},{6,7},{7,6},{8,9},{9,8},{10,11... | collective-permute-start | bytes 110600 | tf_op jit(solution)/shard_map/ppermute | solution.py:28
  73.7 5.2 %collective-permute-start.13 = (f32[72,128]{1,0:T(8,128)S(1)}, f32[72,128]{1,0:T(8,128)S(1)}, u32[]{:S(2)}, u32[]{:S(2)}) collective-permute-start(f32[72,128]{1,0:T(8,128)S(1)} %add.59), channel_id=1, source_target_pairs={{0,9},{1,8},{2,11},{3,10},{4,13},{5,12},{6,15},{7,14},{8,1},{9,0},... | collective-permute-start | bytes 110600 | tf_op jit(solution)/shard_map/ppermute | solution.py:28
  75.3 12.2 %all-to-all-start.2 = ((f32[16,1,2048]{2,1,0:T(1,128)}), f32[16,1,2048]{2,1,0:T(1,128)S(1)}, u32[]{:S(2)}, u32[]{:S(2)}) async-start(f32[16,1,2048]{2,1,0:T(1,128)} %bitcast.17), calls=%async_computation.2 | async-start | bytes 262144 | tf_op jit(solution)/shard_map/all_to_all | solution.py:464
  79.0 4.6 %collective-permute-start.15 = (f32[72,128]{1,0:T(8,128)S(1)}, f32[72,128]{1,0:T(8,128)S(1)}, u32[]{:S(2)}, u32[]{:S(2)}) collective-permute-start(f32[72,128]{1,0:T(8,128)S(1)} %add.60), channel_id=1, source_target_pairs={{0,5},{1,4},{2,7},{3,6},{4,1},{5,0},{6,3},{7,2},{8,13},{9,12},{10,... | collective-permute-start | bytes 110600 | tf_op jit(solution)/shard_map/ppermute | solution.py:28
  80.9 5.2 %collective-permute-start.16 = (f32[72,128]{1,0:T(8,128)S(1)}, f32[72,128]{1,0:T(8,128)S(1)}, u32[]{:S(2)}, u32[]{:S(2)}) collective-permute-start(f32[72,128]{1,0:T(8,128)S(1)} %add.60), channel_id=1, source_target_pairs={{0,7},{1,6},{2,5},{3,4},{4,3},{5,2},{6,1},{7,0},{8,15},{9,14},{10,... | collective-permute-start | bytes 110600 | tf_op jit(solution)/shard_map/ppermute | solution.py:28
  82.3 3.9 %collective-permute-start.14 = (f32[72,128]{1,0:T(8,128)S(1)}, f32[72,128]{1,0:T(8,128)S(1)}, u32[]{:S(2)}, u32[]{:S(2)}) collective-permute-start(f32[72,128]{1,0:T(8,128)S(1)} %add.60), channel_id=1, source_target_pairs={{0,3},{1,2},{2,1},{3,0},{4,7},{5,6},{6,5},{7,4},{8,11},{9,10},{10,... | collective-permute-start | bytes 110600 | tf_op jit(solution)/shard_map/ppermute | solution.py:28

commit v10 on v9

--- a/solution.py
+++ b/solution.py
@@ -18,7 +18,7 @@
     return jnp.einsum(form, left, right, precision=precision)
 
 
-def total(part):
+def total(part, far_first=True):
     narrow = lax.axis_size("narrow")
     count = lax.axis_size("wide") * narrow
     if narrow != 2 or count & (count - 1):
@@ -32,8 +32,11 @@
     while narrow < count:
         bits.append(narrow)
         narrow *= 2
-    parts = [bits[-1:]] if len(bits) % 2 else []
-    parts += [bits[at : at + 2] for at in range(0, len(bits) - 1, 2)]
+    parts = []
+    if len(bits) % 2:
+        parts = [bits[-1:]] if far_first else [bits[:1]]
+        bits = bits[:-1] if far_first else bits[1:]
+    parts += [bits[at : at + 2] for at in range(0, len(bits), 2)]
     for low, *high in parts:
         if high:
             near_sum, far_sum = moved(low + 1), moved(high[0] + 1)
@@ -219,9 +222,11 @@
         pltpu.make_async_copy(two_far, two, sems.at[3 * chunks + 1]),
     ]
     leave = pltpu.make_async_copy(flat, out, sems.at[3 * chunks + 2])
+    for h in range(2):
+        fetch(0, h).start()
     for copy in copies:
         copy.start()
-    for at in range(chunks):
+    for at in range(1, chunks):
         for h in range(2):
             fetch(at, h).start()
     copies[0].wait()
@@ -543,7 +548,7 @@
         factor_two,
         three,
     )
-    product = total(product)
+    product = total(product, far_first=False)
 
     whole, rest = laid(size)
     pitch = share * share * whole + rest * -(-share * share // 2)

time: 90.5 us -> 90.3 us (level)
  starting transfers between devices: 30.7 us -> 29.6 us
  waiting for transfers between devices: 42.9 us -> 43.9 us
    ppermute x15, waiting for transfers between devices: 16.7 us -> 18.3 us  [moved(): return lax.ppermute(part, group, [(at, at ^ mask) for at in range(count)])]
    ppermute x15, starting transfers between devices: 15.4 us -> 14.5 us  [moved(): return lax.ppermute(part, group, [(at, at ^ mask) for at in range(count)])]
  transfers between devices with their start and end apart: 20 -> 20, of which waited for: 14 -> 16; matrix products, arithmetic and copies ran while one was open for 2% -> 2% of each run, Pallas kernels for 1% -> 1%
where the time goes in v10:
time: 90.3 us; the launch traced here: 89.9 us
  waiting for transfers between devices  43.9 us (49%)
  starting transfers between devices  29.6 us (33%)
  Pallas kernels  14 us (16%)
  local copies, waits for them, and re-layouts  1.48 us (2%)
    all_to_all x3, waiting for transfers between devices, exchange(): return lax.all_to_all(flat, group, 0, 0, tiled=True).reshape(rows, lanes)  25.6 us
    ppermute x15, waiting for transfers between devices, moved(): return lax.ppermute(part, group, [(at, at ^ mask) for at in range(count)])  18.3 us
    ppermute x15, starting transfers between devices, moved(): return lax.ppermute(part, group, [(at, at ^ mask) for at in range(count)])  14.5 us
    all_to_all x3, starting transfers between devices, exchange(): return lax.all_to_all(flat, group, 0, 0, tiled=True).reshape(rows, lanes)  14.1 us
    pallas_call x7, Pallas kernels, call(): pl.pallas_call(body, in_specs=[outside if at in away else inside for at i...  14 us
  transfers between devices with their start and end apart: 20, of which 16 were waited for; matrix products, arithmetic and copies ran while one was open for 2% of the time, Pallas kernels for 1%

profile of v10, /device:TPU:0, one launch (start us, length us, event | category | flops | bytes accessed | tf_op | source)
XLA Modules:
  0.0 89.9 jit_solution(15651940119847944365)
XLA Ops:
  0.6 2.7 %shard_map.75 = (f32[672,128]{1,0:T(8,128)}, f32[12,64,256]{2,1,0:T(8,128)}) custom-call(f32[24,64,256]{2,1,0:T(8,128)} %field.1, f32[48,256]{1,0:T(8,128)} %bitcast.16, f32[24,48]{1,0:T(8,128)} %refs_2_.1), custom_call_target="tpu_custom_call" | custom-call | tf_op jit(solution)/shard_map/pallas_call | solution.py:134
  3.4 0.6 collective-permute-start
  3.9 7.0 %all-to-all-start = ((f32[16,1,5376]{2,1,0:T(1,128)}), f32[16,1,5376]{2,1,0:T(1,128)S(1)}, u32[]{:S(2)}, u32[]{:S(2)}) async-start(f32[16,1,5376]{2,1,0:T(1,128)} %bitcast.15), calls=%async_computation | async-start | bytes 688128 | tf_op jit(solution)/shard_map/all_to_all | solution.py:469
  11.0 0.1 copy.13.refs_1_
  11.0 0.4 collective-permute-start.1
  11.5 1.2 %shard_map.76 = (bf16[12,128,256]{2,1,0:T(8,128)(2,1)S(1)}, bf16[12,128,256]{2,1,0:T(8,128)(2,1)S(1)}) custom-call(f32[24,64,256]{2,1,0:T(8,128)} %field.1, f32[12,64,256]{2,1,0:T(8,128)S(1)} %collective-permute-done.other), custom_call_target="tpu_custom_call" | custom-call | tf_op jit(solution)/shard_map/pallas_call | solution.py:134
  12.7 9.5 %all-to-all-done = f32[16,1,5376]{2,1,0:T(1,128)S(1)} async-done(((f32[16,1,5376]{2,1,0:T(1,128)}), f32[16,1,5376]{2,1,0:T(1,128)S(1)}, u32[]{:S(2)}, u32[]{:S(2)}) %all-to-all-start) | async-done | bytes 344096 | tf_op jit(solution)/shard_map/all_to_all | solution.py:469
  22.3 0.0 collective-permute-done.1.refs_2_
  22.3 1.0 %shard_map.77 = (f32[48,128]{1,0:T(8,128)S(1)}, f32[192,128]{1,0:T(8,128)S(1)}) custom-call(f32[672,128]{1,0:T(8,128)S(1)} %bitcast.12, f32[64,48]{1,0:T(8,128)S(1)} %copy.13.refs_1_, f32[64,48]{1,0:T(8,128)S(1)} %collective-permute-done.1.refs_2_), custom_call_target="tpu_custom_call" | custom-call | tf_op jit(solution)/shard_map/pallas_call | solution.py:134
  23.3 0.1 collective-permute-start.2
  23.4 1.1 %collective-permute-done.2 = f32[48,128]{1,0:T(8,128)S(1)} collective-permute-done((f32[48,128]{1,0:T(8,128)S(1)}, f32[48,128]{1,0:T(8,128)S(1)}, u32[]{:S(2)}, u32[]{:S(2)}) %collective-permute-start.2) | collective-permute-done | bytes 24608 | tf_op jit(solution)/shard_map/ppermute | solution.py:28
  24.5 1.3 %collective-permute-start.3 = (f32[48,128]{1,0:T(8,128)S(1)}, f32[48,128]{1,0:T(8,128)S(1)}, u32[]{:S(2)}, u32[]{:S(2)}) collective-permute-start(f32[48,128]{1,0:T(8,128)S(1)} %add.48), channel_id=1, source_target_pairs={{0,9},{1,8},{2,11},{3,10},{4,13},{5,12},{6,15},{7,14},{8,1},{9,0},... | collective-permute-start | bytes 73736 | tf_op jit(solution)/shard_map/ppermute | solution.py:28
  25.8 2.9 %collective-permute-done.3 = f32[48,128]{1,0:T(8,128)S(1)} collective-permute-done((f32[48,128]{1,0:T(8,128)S(1)}, f32[48,128]{1,0:T(8,128)S(1)}, u32[]{:S(2)}, u32[]{:S(2)}) %collective-permute-start.3) | collective-permute-done | bytes 24608 | tf_op jit(solution)/shard_map/ppermute | solution.py:28
  28.7 0.7 collective-permute-start.5
  29.3 1.0 %collective-permute-start.6 = (f32[48,128]{1,0:T(8,128)S(1)}, f32[48,128]{1,0:T(8,128)S(1)}, u32[]{:S(2)}, u32[]{:S(2)}) collective-permute-start(f32[48,128]{1,0:T(8,128)S(1)} %add.49), channel_id=1, source_target_pairs={{0,7},{1,6},{2,5},{3,4},{4,3},{5,2},{6,1},{7,0},{8,15},{9,14},{10,... | collective-permute-start | bytes 73736 | tf_op jit(solution)/shard_map/ppermute | solution.py:28
  30.3 1.7 %collective-permute-start.4 = (f32[48,128]{1,0:T(8,128)S(1)}, f32[48,128]{1,0:T(8,128)S(1)}, u32[]{:S(2)}, u32[]{:S(2)}) collective-permute-start(f32[48,128]{1,0:T(8,128)S(1)} %add.49), channel_id=1, source_target_pairs={{0,3},{1,2},{2,1},{3,0},{4,7},{5,6},{6,5},{7,4},{8,11},{9,10},{10,... | collective-permute-start | bytes 73736 | tf_op jit(solution)/shard_map/ppermute | solution.py:28
  32.1 1.4 %collective-permute-done.6 = f32[48,128]{1,0:T(8,128)S(1)} collective-permute-done((f32[48,128]{1,0:T(8,128)S(1)}, f32[48,128]{1,0:T(8,128)S(1)}, u32[]{:S(2)}, u32[]{:S(2)}) %collective-permute-start.6) | collective-permute-done | bytes 24608 | tf_op jit(solution)/shard_map/ppermute | solution.py:28
  33.5 0.5 collective-permute-done.4
  34.0 2.7 %shard_map.78 = (f32[48,128]{1,0:T(8,128)S(1)}, f32[16,72,128]{2,1,0:T(8,128)}) custom-call(f32[48,128]{1,0:T(8,128)S(1)} %add_add_fusion.2.refs_0_, bf16[12,128,256]{2,1,0:T(8,128)(2,1)S(1)} %get-tuple-element.29.refs_1_, bf16[12,128,256]{2,1,0:T(8,128)(2,1)S(1)} %get-tuple-element.30.refs_2_), custom_call_target="tpu_custom_call" | custom-call | tf_op jit(solution)/shard_map/pallas_call | solution.py:134
  36.8 3.6 %all-to-all-start.1 = ((f32[16,1,9216]{2,1,0:T(1,128)}), f32[16,1,9216]{2,1,0:T(1,128)S(1)}, u32[]{:S(2)}, u32[]{:S(2)}) async-start(f32[16,1,9216]{2,1,0:T(1,128)} %bitcast.14), calls=%async_computation.1 | async-start | bytes 1179648 | tf_op jit(solution)/shard_map/all_to_all | solution.py:469
  40.4 0.1 copy.15.refs_1_
  40.5 15.4 %all-to-all-done.1 = f32[16,1,9216]{2,1,0:T(1,128)S(1)} async-done(((f32[16,1,9216]{2,1,0:T(1,128)}), f32[16,1,9216]{2,1,0:T(1,128)S(1)}, u32[]{:S(2)}, u32[]{:S(2)}) %all-to-all-start.1) | async-done | bytes 589856 | tf_op jit(solution)/shard_map/all_to_all | solution.py:469
  55.9 0.8 shard_map.79
  56.6 0.1 collective-permute-start.7
  56.8 1.2 %collective-permute-done.7 = f32[48,256]{1,0:T(8,128)S(1)} collective-permute-done((f32[48,256]{1,0:T(8,128)S(1)}, f32[48,256]{1,0:T(8,128)S(1)}, u32[]{:S(2)}, u32[]{:S(2)}) %collective-permute-start.7) | collective-permute-done | bytes 49184 | tf_op jit(solution)/shard_map/ppermute | solution.py:28
  58.0 1.1 %collective-permute-start.8 = (f32[48,256]{1,0:T(8,128)S(1)}, f32[48,256]{1,0:T(8,128)S(1)}, u32[]{:S(2)}, u32[]{:S(2)}) collective-permute-start(f32[48,256]{1,0:T(8,128)S(1)} %add.54), channel_id=1, source_target_pairs={{0,3},{1,2},{2,1},{3,0},{4,7},{5,6},{6,5},{7,4},{8,11},{9,10},{10,... | collective-permute-start | bytes 147464 | tf_op jit(solution)/shard_map/ppermute | solution.py:28
  59.0 2.7 %collective-permute-done.8 = f32[48,256]{1,0:T(8,128)S(1)} collective-permute-done((f32[48,256]{1,0:T(8,128)S(1)}, f32[48,256]{1,0:T(8,128)S(1)}, u32[]{:S(2)}, u32[]{:S(2)}) %collective-permute-start.8) | collective-permute-done | bytes 49184 | tf_op jit(solution)/shard_map/ppermute | solution.py:28
  61.8 2.3 %collective-permute-start.10 = (f32[48,256]{1,0:T(8,128)S(1)}, f32[48,256]{1,0:T(8,128)S(1)}, u32[]{:S(2)}, u32[]{:S(2)}) collective-permute-start(f32[48,256]{1,0:T(8,128)S(1)} %add.55), channel_id=1, source_target_pairs={{0,9},{1,8},{2,11},{3,10},{4,13},{5,12},{6,15},{7,14},{8,1},{9,0},... | collective-permute-start | bytes 147464 | tf_op jit(solution)/shard_map/ppermute | solution.py:28
  64.1 1.2 %collective-permute-start.11 = (f32[48,256]{1,0:T(8,128)S(1)}, f32[48,256]{1,0:T(8,128)S(1)}, u32[]{:S(2)}, u32[]{:S(2)}) collective-permute-start(f32[48,256]{1,0:T(8,128)S(1)} %add.55), channel_id=1, source_target_pairs={{0,13},{1,12},{2,15},{3,14},{4,9},{5,8},{6,11},{7,10},{8,5},{9,4},... | collective-permute-start | bytes 147464 | tf_op jit(solution)/shard_map/ppermute | solution.py:28
  65.3 0.0 collective-permute-start.9
  65.3 1.1 %collective-permute-done.10 = f32[48,256]{1,0:T(8,128)S(1)} collective-permute-done((f32[48,256]{1,0:T(8,128)S(1)}, f32[48,256]{1,0:T(8,128)S(1)}, u32[]{:S(2)}, u32[]{:S(2)}) %collective-permute-start.10) | collective-permute-done | bytes 49184 | tf_op jit(solution)/shard_map/ppermute | solution.py:28
  66.5 3.0 %collective-permute-done.11 = f32[48,256]{1,0:T(8,128)S(1)} collective-permute-done((f32[48,256]{1,0:T(8,128)S(1)}, f32[48,256]{1,0:T(8,128)S(1)}, u32[]{:S(2)}, u32[]{:S(2)}) %collective-permute-start.11) | collective-permute-done | bytes 49184 | tf_op jit(solution)/shard_map/ppermute | solution.py:28
  69.5 3.0 %shard_map.80 = (f32[48,256]{1,0:T(8,128)S(1)}, f32[72,128]{1,0:T(8,128)S(1)}, f32[256,128]{1,0:T(8,128)}) custom-call(f32[48,256]{1,0:T(8,128)S(1)} %add_add_fusion.refs_0_, bf16[3,192,256]{2,1,0:T(8,128)(2,1)S(1)} %get-tuple-element.35.refs_1_, bf16[3,192,256]{2,1,0:T(8,128)(2,1)S(1)} %get-tuple-element.36.refs_2_, ...), custom_call_target="tpu_custom_call" | custom-call | tf_op jit(solution)/shard_map/pallas_call | solution.py:134
  72.5 0.9 collective-permute-start.12
  73.4 0.9 collective-permute-done.12
  74.3 1.0 %collective-permute-start.13 = (f32[72,128]{1,0:T(8,128)S(1)}, f32[72,128]{1,0:T(8,128)S(1)}, u32[]{:S(2)}, u32[]{:S(2)}) collective-permute-start(f32[72,128]{1,0:T(8,128)S(1)} %add.59), channel_id=1, source_target_pairs={{0,9},{1,8},{2,11},{3,10},{4,13},{5,12},{6,15},{7,14},{8,1},{9,0},... | collective-permute-start | bytes 110600 | tf_op jit(solution)/shard_map/ppermute | solution.py:28
  75.3 3.5 %all-to-all-start.2 = ((f32[16,1,2048]{2,1,0:T(1,128)}), f32[16,1,2048]{2,1,0:T(1,128)S(1)}, u32[]{:S(2)}, u32[]{:S(2)}) async-start(f32[16,1,2048]{2,1,0:T(1,128)} %bitcast.17), calls=%async_computation.2 | async-start | bytes 262144 | tf_op jit(solution)/shard_map/all_to_all | solution.py:469
  78.8 0.8 collective-permute-done.13
  79.6 1.0 %collective-permute-start.15 = (f32[72,128]{1,0:T(8,128)S(1)}, f32[72,128]{1,0:T(8,128)S(1)}, u32[]{:S(2)}, u32[]{:S(2)}) collective-permute-start(f32[72,128]{1,0:T(8,128)S(1)} %add.60), channel_id=1, source_target_pairs={{0,5},{1,4},{2,7},{3,6},{4,1},{5,0},{6,3},{7,2},{8,13},{9,12},{10,... | collective-permute-start | bytes 110600 | tf_op jit(solution)/shard_map/ppermute | solution.py:28
  80.6 1.4 %collective-permute-start.16 = (f32[72,128]{1,0:T(8,128)S(1)}, f32[72,128]{1,0:T(8,128)S(1)}, u32[]{:S(2)}, u32[]{:S(2)}) collective-permute-start(f32[72,128]{1,0:T(8,128)S(1)} %add.60), channel_id=1, source_target_pairs={{0,7},{1,6},{2,5},{3,4},{4,3},{5,2},{6,1},{7,0},{8,15},{9,14},{10,... | collective-permute-start | bytes 110600 | tf_op jit(solution)/shard_map/ppermute | solution.py:28
  82.0 0.5 collective-permute-start.14
  82.5 0.7 dynamic-slice_bitcast_fusion
  83.2 0.6 copy.17
  83.8 0.2 collective-permute-done.15
  84.1 1.8 %collective-permute-done.16 = f32[72,128]{1,0:T(8,128)S(1)} collective-permute-done((f32[72,128]{1,0:T(8,128)S(1)}, f32[72,128]{1,0:T(8,128)S(1)}, u32[]{:S(2)}, u32[]{:S(2)}) %collective-permute-start.16) | collective-permute-done | bytes 36896 | tf_op jit(solution)/shard_map/ppermute | solution.py:28
  85.9 0.7 collective-permute-done.14
  86.6 0.7 all-to-all-done.2
  87.3 2.6 %shard_map.81 = (f32[24,48]{1,0:T(8,128)}, f32[48,144]{1,0:T(8,128)}) custom-call(f32[72,128]{1,0:T(8,128)S(1)} %add_add_fusion.1.refs_0_, f32[256,128]{1,0:T(8,128)S(1)} %bitcast.13), custom_call_target="tpu_custom_call" | custom-call | tf_op jit(solution)/shard_map/pallas_call | solution.py:134
  (16 shorter events, 0.1 us)
Async XLA Ops:
  0.6 10.3 %copy-start.1 = (f32[64,48]{0,1:T(8,128)S(1)}, f32[64,48]{0,1:T(8,128)}, u32[]{:S(2)}) copy-start(f32[64,48]{0,1:T(8,128)} %param.5) | copy-start | bytes 36868
  3.4 8.1 %collective-permute-start = (f32[12,64,256]{2,1,0:T(8,128)}, f32[12,64,256]{2,1,0:T(8,128)S(1)}, u32[]{:S(2)}, u32[]{:S(2)}) collective-permute-start(f32[12,64,256]{2,1,0:T(8,128)} %get-tuple-element.24), channel_id=1, source_target_pairs={{0,1},{1,0},{2,3},{3,2},{4,5},{5,4},{6,7},{7,6},{8,9},{9,8},{10,11... | collective-permute-start | bytes 2359304 | tf_op jit(solution)/shard_map/ppermute | solution.py:50
  3.9 18.4 %all-to-all-start = ((f32[16,1,5376]{2,1,0:T(1,128)}), f32[16,1,5376]{2,1,0:T(1,128)S(1)}, u32[]{:S(2)}, u32[]{:S(2)}) async-start(f32[16,1,5376]{2,1,0:T(1,128)} %bitcast.15), calls=%async_computation | async-start | bytes 688128 | tf_op jit(solution)/shard_map/all_to_all | solution.py:469
  11.0 11.2 %collective-permute-start.1 = (f32[64,48]{1,0:T(8,128)S(1)}, f32[64,48]{1,0:T(8,128)S(1)}, u32[]{:S(2)}, u32[]{:S(2)}) collective-permute-start(f32[64,48]{1,0:T(8,128)S(1)} %copy.13.refs_1_), channel_id=1, source_target_pairs={{0,1},{1,0},{2,3},{3,2},{4,5},{5,4},{6,7},{7,6},{8,9},{9,8},{10,11... | collective-permute-start | bytes 36872 | tf_op jit(solution)/shard_map/ppermute | solution.py:50
  23.3 17.1 %copy-start = (f32[256,48]{0,1:T(8,128)S(1)}, f32[256,48]{0,1:T(8,128)}, u32[]{:S(2)}) copy-start(f32[256,48]{0,1:T(8,128)} %param.6) | copy-start | bytes 147460
  23.3 1.2 %collective-permute-start.2 = (f32[48,128]{1,0:T(8,128)S(1)}, f32[48,128]{1,0:T(8,128)S(1)}, u32[]{:S(2)}, u32[]{:S(2)}) collective-permute-start(f32[48,128]{1,0:T(8,128)S(1)} %get-tuple-element.28), channel_id=1, source_target_pairs={{0,1},{1,0},{2,3},{3,2},{4,5},{5,4},{6,7},{7,6},{8,9},{9,8},{10,11... | collective-permute-start | bytes 73736 | tf_op jit(solution)/shard_map/ppermute | solution.py:28
  24.5 4.2 %collective-permute-start.3 = (f32[48,128]{1,0:T(8,128)S(1)}, f32[48,128]{1,0:T(8,128)S(1)}, u32[]{:S(2)}, u32[]{:S(2)}) collective-permute-start(f32[48,128]{1,0:T(8,128)S(1)} %add.48), channel_id=1, source_target_pairs={{0,9},{1,8},{2,11},{3,10},{4,13},{5,12},{6,15},{7,14},{8,1},{9,0},... | collective-permute-start | bytes 73736 | tf_op jit(solution)/shard_map/ppermute | solution.py:28
  28.7 3.4 %collective-permute-start.5 = (f32[48,128]{1,0:T(8,128)S(1)}, f32[48,128]{1,0:T(8,128)S(1)}, u32[]{:S(2)}, u32[]{:S(2)}) collective-permute-start(f32[48,128]{1,0:T(8,128)S(1)} %add.49), channel_id=1, source_target_pairs={{0,5},{1,4},{2,7},{3,6},{4,1},{5,0},{6,3},{7,2},{8,13},{9,12},{10,... | collective-permute-start | bytes 73736 | tf_op jit(solution)/shard_map/ppermute | solution.py:28
  29.3 4.2 %collective-permute-start.6 = (f32[48,128]{1,0:T(8,128)S(1)}, f32[48,128]{1,0:T(8,128)S(1)}, u32[]{:S(2)}, u32[]{:S(2)}) collective-permute-start(f32[48,128]{1,0:T(8,128)S(1)} %add.49), channel_id=1, source_target_pairs={{0,7},{1,6},{2,5},{3,4},{4,3},{5,2},{6,1},{7,0},{8,15},{9,14},{10,... | collective-permute-start | bytes 73736 | tf_op jit(solution)/shard_map/ppermute | solution.py:28
  30.3 3.7 %collective-permute-start.4 = (f32[48,128]{1,0:T(8,128)S(1)}, f32[48,128]{1,0:T(8,128)S(1)}, u32[]{:S(2)}, u32[]{:S(2)}) collective-permute-start(f32[48,128]{1,0:T(8,128)S(1)} %add.49), channel_id=1, source_target_pairs={{0,3},{1,2},{2,1},{3,0},{4,7},{5,6},{6,5},{7,4},{8,11},{9,10},{10,... | collective-permute-start | bytes 73736 | tf_op jit(solution)/shard_map/ppermute | solution.py:28
  36.8 19.1 %all-to-all-start.1 = ((f32[16,1,9216]{2,1,0:T(1,128)}), f32[16,1,9216]{2,1,0:T(1,128)S(1)}, u32[]{:S(2)}, u32[]{:S(2)}) async-start(f32[16,1,9216]{2,1,0:T(1,128)} %bitcast.14), calls=%async_computation.1 | async-start | bytes 1179648 | tf_op jit(solution)/shard_map/all_to_all | solution.py:469
  56.6 1.3 %collective-permute-start.7 = (f32[48,256]{1,0:T(8,128)S(1)}, f32[48,256]{1,0:T(8,128)S(1)}, u32[]{:S(2)}, u32[]{:S(2)}) collective-permute-start(f32[48,256]{1,0:T(8,128)S(1)} %get-tuple-element.34), channel_id=1, source_target_pairs={{0,1},{1,0},{2,3},{3,2},{4,5},{5,4},{6,7},{7,6},{8,9},{9,8},{10,11... | collective-permute-start | bytes 147464 | tf_op jit(solution)/shard_map/ppermute | solution.py:28
  58.0 3.8 %collective-permute-start.8 = (f32[48,256]{1,0:T(8,128)S(1)}, f32[48,256]{1,0:T(8,128)S(1)}, u32[]{:S(2)}, u32[]{:S(2)}) collective-permute-start(f32[48,256]{1,0:T(8,128)S(1)} %add.54), channel_id=1, source_target_pairs={{0,3},{1,2},{2,1},{3,0},{4,7},{5,6},{6,5},{7,4},{8,11},{9,10},{10,... | collective-permute-start | bytes 147464 | tf_op jit(solution)/shard_map/ppermute | solution.py:28
  61.8 4.7 %collective-permute-start.10 = (f32[48,256]{1,0:T(8,128)S(1)}, f32[48,256]{1,0:T(8,128)S(1)}, u32[]{:S(2)}, u32[]{:S(2)}) collective-permute-start(f32[48,256]{1,0:T(8,128)S(1)} %add.55), channel_id=1, source_target_pairs={{0,9},{1,8},{2,11},{3,10},{4,13},{5,12},{6,15},{7,14},{8,1},{9,0},... | collective-permute-start | bytes 147464 | tf_op jit(solution)/shard_map/ppermute | solution.py:28
  64.1 5.4 %collective-permute-start.11 = (f32[48,256]{1,0:T(8,128)S(1)}, f32[48,256]{1,0:T(8,128)S(1)}, u32[]{:S(2)}, u32[]{:S(2)}) collective-permute-start(f32[48,256]{1,0:T(8,128)S(1)} %add.55), channel_id=1, source_target_pairs={{0,13},{1,12},{2,15},{3,14},{4,9},{5,8},{6,11},{7,10},{8,5},{9,4},... | collective-permute-start | bytes 147464 | tf_op jit(solution)/shard_map/ppermute | solution.py:28
  65.3 4.1 %collective-permute-start.9 = (f32[48,256]{1,0:T(8,128)S(1)}, f32[48,256]{1,0:T(8,128)S(1)}, u32[]{:S(2)}, u32[]{:S(2)}) collective-permute-start(f32[48,256]{1,0:T(8,128)S(1)} %add.55), channel_id=1, source_target_pairs={{0,5},{1,4},{2,7},{3,6},{4,1},{5,0},{6,3},{7,2},{8,13},{9,12},{10,... | collective-permute-start | bytes 147464 | tf_op jit(solution)/shard_map/ppermute | solution.py:28
  72.5 1.7 %collective-permute-start.12 = (f32[72,128]{1,0:T(8,128)S(1)}, f32[72,128]{1,0:T(8,128)S(1)}, u32[]{:S(2)}, u32[]{:S(2)}) collective-permute-start(f32[72,128]{1,0:T(8,128)S(1)} %get-tuple-element.38), channel_id=1, source_target_pairs={{0,1},{1,0},{2,3},{3,2},{4,5},{5,4},{6,7},{7,6},{8,9},{9,8},{10,11... | collective-permute-start | bytes 110600 | tf_op jit(solution)/shard_map/ppermute | solution.py:28
  74.3 5.3 %collective-permute-start.13 = (f32[72,128]{1,0:T(8,128)S(1)}, f32[72,128]{1,0:T(8,128)S(1)}, u32[]{:S(2)}, u32[]{:S(2)}) collective-permute-start(f32[72,128]{1,0:T(8,128)S(1)} %add.59), channel_id=1, source_target_pairs={{0,9},{1,8},{2,11},{3,10},{4,13},{5,12},{6,15},{7,14},{8,1},{9,0},... | collective-permute-start | bytes 110600 | tf_op jit(solution)/shard_map/ppermute | solution.py:28
  75.3 12.0 %all-to-all-start.2 = ((f32[16,1,2048]{2,1,0:T(1,128)}), f32[16,1,2048]{2,1,0:T(1,128)S(1)}, u32[]{:S(2)}, u32[]{:S(2)}) async-start(f32[16,1,2048]{2,1,0:T(1,128)} %bitcast.17), calls=%async_computation.2 | async-start | bytes 262144 | tf_op jit(solution)/shard_map/all_to_all | solution.py:469
  79.6 4.5 %collective-permute-start.15 = (f32[72,128]{1,0:T(8,128)S(1)}, f32[72,128]{1,0:T(8,128)S(1)}, u32[]{:S(2)}, u32[]{:S(2)}) collective-permute-start(f32[72,128]{1,0:T(8,128)S(1)} %add.60), channel_id=1, source_target_pairs={{0,5},{1,4},{2,7},{3,6},{4,1},{5,0},{6,3},{7,2},{8,13},{9,12},{10,... | collective-permute-start | bytes 110600 | tf_op jit(solution)/shard_map/ppermute | solution.py:28
  80.6 5.3 %collective-permute-start.16 = (f32[72,128]{1,0:T(8,128)S(1)}, f32[72,128]{1,0:T(8,128)S(1)}, u32[]{:S(2)}, u32[]{:S(2)}) collective-permute-start(f32[72,128]{1,0:T(8,128)S(1)} %add.60), channel_id=1, source_target_pairs={{0,7},{1,6},{2,5},{3,4},{4,3},{5,2},{6,1},{7,0},{8,15},{9,14},{10,... | collective-permute-start | bytes 110600 | tf_op jit(solution)/shard_map/ppermute | solution.py:28
  82.0 4.6 %collective-permute-start.14 = (f32[72,128]{1,0:T(8,128)S(1)}, f32[72,128]{1,0:T(8,128)S(1)}, u32[]{:S(2)}, u32[]{:S(2)}) collective-permute-start(f32[72,128]{1,0:T(8,128)S(1)} %add.60), channel_id=1, source_target_pairs={{0,3},{1,2},{2,1},{3,0},{4,7},{5,6},{6,5},{7,4},{8,11},{9,10},{10,... | collective-permute-start | bytes 110600 | tf_op jit(solution)/shard_map/ppermute | solution.py:28

commit v11 on v10

--- a/solution.py
+++ b/solution.py
@@ -435,7 +435,7 @@
     copy.wait()
 
 
-def finish(part, got, basis, core, room, *, share, half, count):
+def finish(part, got, basis, core, room, block, sems, *, share, half, count):
     size, rank = room.shape
     whole, rest = laid(size)
     pitch = got.shape[0] // count
@@ -446,7 +446,12 @@
     value = orthonormal(jnp.concatenate(value, axis=1))
     room[...] = value.T
     depth = basis.shape[0]
-    basis[...] = room[pl.ds(pl.multiple_of(lax.axis_index("wide") * depth, 8), depth), :]
+    start = pl.multiple_of(lax.axis_index("wide") * depth, 8)
+    copies = [
+        pltpu.make_async_copy(room.at[pl.ds(start, depth), :], basis, sems.at[0]),
+        pltpu.make_async_copy(block, core, sems.at[1]),
+    ]
+    copies[0].start()
     rows = []
     for b in range(share):
         for s in range(share):
@@ -460,7 +465,10 @@
             rows.append(jnp.concatenate(pieces, axis=1))
     value = dot3(jnp.concatenate(rows), value, nt)
     for b in range(share):
-        core[:, b * rank : (b + 1) * rank] = value[b * rank : (b + 1) * rank]
+        block[:, b * rank : (b + 1) * rank] = value[b * rank : (b + 1) * rank]
+    copies[1].start()
+    for copy in copies:
+        copy.wait()
 
 
 def exchange(value, count):
@@ -578,7 +586,12 @@
         [far(depth, rank), far(rank, share * rank)],
         product,
         got,
-        scratch_shapes=[near(size, rank)],
+        away_out=(0, 1),
+        scratch_shapes=[
+            near(size, rank),
+            near(rank, share * rank),
+            pltpu.SemaphoreType.DMA((2,)),
+        ],
     )
     basis_one = lax.dynamic_slice_in_dim(one_t, core_at * rows, rows, 1).T
     return (basis_one, two_t.T, basis_three, core)

time: 90.3 us -> 90.3 us (level)
  no operation moved by 1% of the time
where the time goes in v11:
time: 90.3 us; the launch traced here: 89.9 us
  waiting for transfers between devices  43.9 us (49%)
  starting transfers between devices  29.6 us (33%)
  Pallas kernels  14 us (16%)
  local copies, waits for them, and re-layouts  1.48 us (2%)
    all_to_all x3, waiting for transfers between devices, exchange(): return lax.all_to_all(flat, group, 0, 0, tiled=True).reshape(rows, lanes)  25.6 us
    ppermute x15, waiting for transfers between devices, moved(): return lax.ppermute(part, group, [(at, at ^ mask) for at in range(count)])  18.3 us
    ppermute x15, starting transfers between devices, moved(): return lax.ppermute(part, group, [(at, at ^ mask) for at in range(count)])  14.5 us
    all_to_all x3, starting transfers between devices, exchange(): return lax.all_to_all(flat, group, 0, 0, tiled=True).reshape(rows, lanes)  14.1 us
    pallas_call x7, Pallas kernels, call(): pl.pallas_call(body, in_specs=[outside if at in away else inside for at i...  14 us
  transfers between devices with their start and end apart: 20, of which 16 were waited for; matrix products, arithmetic and copies ran while one was open for 2% of the time, Pallas kernels for 1%

profile of v11, /device:TPU:0, one launch (start us, length us, event | category | flops | bytes accessed | tf_op | source)
XLA Modules:
  0.0 89.9 jit_solution(8343347241576330145)
XLA Ops:
  0.6 2.7 %shard_map.75 = (f32[672,128]{1,0:T(8,128)}, f32[12,64,256]{2,1,0:T(8,128)}) custom-call(f32[24,64,256]{2,1,0:T(8,128)} %field.1, f32[48,256]{1,0:T(8,128)} %bitcast.16, f32[24,48]{1,0:T(8,128)} %refs_2_.1), custom_call_target="tpu_custom_call" | custom-call | tf_op jit(solution)/shard_map/pallas_call | solution.py:134
  3.4 0.6 collective-permute-start
  3.9 7.0 %all-to-all-start = ((f32[16,1,5376]{2,1,0:T(1,128)}), f32[16,1,5376]{2,1,0:T(1,128)S(1)}, u32[]{:S(2)}, u32[]{:S(2)}) async-start(f32[16,1,5376]{2,1,0:T(1,128)} %bitcast.15), calls=%async_computation | async-start | bytes 688128 | tf_op jit(solution)/shard_map/all_to_all | solution.py:477
  11.0 0.1 copy.13.refs_1_
  11.0 0.4 collective-permute-start.1
  11.5 0.0 collective-permute-done.other
  11.5 1.2 %shard_map.76 = (bf16[12,128,256]{2,1,0:T(8,128)(2,1)S(1)}, bf16[12,128,256]{2,1,0:T(8,128)(2,1)S(1)}) custom-call(f32[24,64,256]{2,1,0:T(8,128)} %field.1, f32[12,64,256]{2,1,0:T(8,128)S(1)} %collective-permute-done.other), custom_call_target="tpu_custom_call" | custom-call | tf_op jit(solution)/shard_map/pallas_call | solution.py:134
  12.7 9.5 %all-to-all-done = f32[16,1,5376]{2,1,0:T(1,128)S(1)} async-done(((f32[16,1,5376]{2,1,0:T(1,128)}), f32[16,1,5376]{2,1,0:T(1,128)S(1)}, u32[]{:S(2)}, u32[]{:S(2)}) %all-to-all-start) | async-done | bytes 344096 | tf_op jit(solution)/shard_map/all_to_all | solution.py:477
  22.3 1.0 %shard_map.77 = (f32[48,128]{1,0:T(8,128)S(1)}, f32[192,128]{1,0:T(8,128)S(1)}) custom-call(f32[672,128]{1,0:T(8,128)S(1)} %bitcast.12, f32[64,48]{1,0:T(8,128)S(1)} %copy.13.refs_1_, f32[64,48]{1,0:T(8,128)S(1)} %collective-permute-done.1.refs_2_), custom_call_target="tpu_custom_call" | custom-call | tf_op jit(solution)/shard_map/pallas_call | solution.py:134
  23.3 0.1 collective-permute-start.2
  23.4 1.1 %collective-permute-done.2 = f32[48,128]{1,0:T(8,128)S(1)} collective-permute-done((f32[48,128]{1,0:T(8,128)S(1)}, f32[48,128]{1,0:T(8,128)S(1)}, u32[]{:S(2)}, u32[]{:S(2)}) %collective-permute-start.2) | collective-permute-done | bytes 24608 | tf_op jit(solution)/shard_map/ppermute | solution.py:28
  24.5 1.3 %collective-permute-start.3 = (f32[48,128]{1,0:T(8,128)S(1)}, f32[48,128]{1,0:T(8,128)S(1)}, u32[]{:S(2)}, u32[]{:S(2)}) collective-permute-start(f32[48,128]{1,0:T(8,128)S(1)} %add.48), channel_id=1, source_target_pairs={{0,9},{1,8},{2,11},{3,10},{4,13},{5,12},{6,15},{7,14},{8,1},{9,0},... | collective-permute-start | bytes 73736 | tf_op jit(solution)/shard_map/ppermute | solution.py:28
  25.8 2.9 %collective-permute-done.3 = f32[48,128]{1,0:T(8,128)S(1)} collective-permute-done((f32[48,128]{1,0:T(8,128)S(1)}, f32[48,128]{1,0:T(8,128)S(1)}, u32[]{:S(2)}, u32[]{:S(2)}) %collective-permute-start.3) | collective-permute-done | bytes 24608 | tf_op jit(solution)/shard_map/ppermute | solution.py:28
  28.7 0.7 collective-permute-start.5
  29.3 1.0 %collective-permute-start.6 = (f32[48,128]{1,0:T(8,128)S(1)}, f32[48,128]{1,0:T(8,128)S(1)}, u32[]{:S(2)}, u32[]{:S(2)}) collective-permute-start(f32[48,128]{1,0:T(8,128)S(1)} %add.49), channel_id=1, source_target_pairs={{0,7},{1,6},{2,5},{3,4},{4,3},{5,2},{6,1},{7,0},{8,15},{9,14},{10,... | collective-permute-start | bytes 73736 | tf_op jit(solution)/shard_map/ppermute | solution.py:28
  30.3 1.7 %collective-permute-start.4 = (f32[48,128]{1,0:T(8,128)S(1)}, f32[48,128]{1,0:T(8,128)S(1)}, u32[]{:S(2)}, u32[]{:S(2)}) collective-permute-start(f32[48,128]{1,0:T(8,128)S(1)} %add.49), channel_id=1, source_target_pairs={{0,3},{1,2},{2,1},{3,0},{4,7},{5,6},{6,5},{7,4},{8,11},{9,10},{10,... | collective-permute-start | bytes 73736 | tf_op jit(solution)/shard_map/ppermute | solution.py:28
  32.1 0.0 collective-permute-done.5
  32.1 1.4 %collective-permute-done.6 = f32[48,128]{1,0:T(8,128)S(1)} collective-permute-done((f32[48,128]{1,0:T(8,128)S(1)}, f32[48,128]{1,0:T(8,128)S(1)}, u32[]{:S(2)}, u32[]{:S(2)}) %collective-permute-start.6) | collective-permute-done | bytes 24608 | tf_op jit(solution)/shard_map/ppermute | solution.py:28
  33.5 0.5 collective-permute-done.4
  34.0 2.7 %shard_map.78 = (f32[48,128]{1,0:T(8,128)S(1)}, f32[16,72,128]{2,1,0:T(8,128)}) custom-call(f32[48,128]{1,0:T(8,128)S(1)} %add_add_fusion.2.refs_0_, bf16[12,128,256]{2,1,0:T(8,128)(2,1)S(1)} %get-tuple-element.29.refs_1_, bf16[12,128,256]{2,1,0:T(8,128)(2,1)S(1)} %get-tuple-element.30.refs_2_), custom_call_target="tpu_custom_call" | custom-call | tf_op jit(solution)/shard_map/pallas_call | solution.py:134
  36.8 3.6 %all-to-all-start.1 = ((f32[16,1,9216]{2,1,0:T(1,128)}), f32[16,1,9216]{2,1,0:T(1,128)S(1)}, u32[]{:S(2)}, u32[]{:S(2)}) async-start(f32[16,1,9216]{2,1,0:T(1,128)} %bitcast.14), calls=%async_computation.1 | async-start | bytes 1179648 | tf_op jit(solution)/shard_map/all_to_all | solution.py:477
  40.4 0.1 copy.15.refs_1_
  40.5 15.4 %all-to-all-done.1 = f32[16,1,9216]{2,1,0:T(1,128)S(1)} async-done(((f32[16,1,9216]{2,1,0:T(1,128)}), f32[16,1,9216]{2,1,0:T(1,128)S(1)}, u32[]{:S(2)}, u32[]{:S(2)}) %all-to-all-start.1) | async-done | bytes 589856 | tf_op jit(solution)/shard_map/all_to_all | solution.py:477
  55.9 0.8 shard_map.79
  56.6 0.1 collective-permute-start.7
  56.8 1.2 %collective-permute-done.7 = f32[48,256]{1,0:T(8,128)S(1)} collective-permute-done((f32[48,256]{1,0:T(8,128)S(1)}, f32[48,256]{1,0:T(8,128)S(1)}, u32[]{:S(2)}, u32[]{:S(2)}) %collective-permute-start.7) | collective-permute-done | bytes 49184 | tf_op jit(solution)/shard_map/ppermute | solution.py:28
  58.0 1.1 %collective-permute-start.8 = (f32[48,256]{1,0:T(8,128)S(1)}, f32[48,256]{1,0:T(8,128)S(1)}, u32[]{:S(2)}, u32[]{:S(2)}) collective-permute-start(f32[48,256]{1,0:T(8,128)S(1)} %add.54), channel_id=1, source_target_pairs={{0,3},{1,2},{2,1},{3,0},{4,7},{5,6},{6,5},{7,4},{8,11},{9,10},{10,... | collective-permute-start | bytes 147464 | tf_op jit(solution)/shard_map/ppermute | solution.py:28
  59.0 2.7 %collective-permute-done.8 = f32[48,256]{1,0:T(8,128)S(1)} collective-permute-done((f32[48,256]{1,0:T(8,128)S(1)}, f32[48,256]{1,0:T(8,128)S(1)}, u32[]{:S(2)}, u32[]{:S(2)}) %collective-permute-start.8) | collective-permute-done | bytes 49184 | tf_op jit(solution)/shard_map/ppermute | solution.py:28
  61.8 2.3 %collective-permute-start.10 = (f32[48,256]{1,0:T(8,128)S(1)}, f32[48,256]{1,0:T(8,128)S(1)}, u32[]{:S(2)}, u32[]{:S(2)}) collective-permute-start(f32[48,256]{1,0:T(8,128)S(1)} %add.55), channel_id=1, source_target_pairs={{0,9},{1,8},{2,11},{3,10},{4,13},{5,12},{6,15},{7,14},{8,1},{9,0},... | collective-permute-start | bytes 147464 | tf_op jit(solution)/shard_map/ppermute | solution.py:28
  64.1 1.2 %collective-permute-start.11 = (f32[48,256]{1,0:T(8,128)S(1)}, f32[48,256]{1,0:T(8,128)S(1)}, u32[]{:S(2)}, u32[]{:S(2)}) collective-permute-start(f32[48,256]{1,0:T(8,128)S(1)} %add.55), channel_id=1, source_target_pairs={{0,13},{1,12},{2,15},{3,14},{4,9},{5,8},{6,11},{7,10},{8,5},{9,4},... | collective-permute-start | bytes 147464 | tf_op jit(solution)/shard_map/ppermute | solution.py:28
  65.3 1.1 %collective-permute-done.10 = f32[48,256]{1,0:T(8,128)S(1)} collective-permute-done((f32[48,256]{1,0:T(8,128)S(1)}, f32[48,256]{1,0:T(8,128)S(1)}, u32[]{:S(2)}, u32[]{:S(2)}) %collective-permute-start.10) | collective-permute-done | bytes 49184 | tf_op jit(solution)/shard_map/ppermute | solution.py:28
  66.5 3.0 %collective-permute-done.11 = f32[48,256]{1,0:T(8,128)S(1)} collective-permute-done((f32[48,256]{1,0:T(8,128)S(1)}, f32[48,256]{1,0:T(8,128)S(1)}, u32[]{:S(2)}, u32[]{:S(2)}) %collective-permute-start.11) | collective-permute-done | bytes 49184 | tf_op jit(solution)/shard_map/ppermute | solution.py:28
  69.5 3.0 %shard_map.80 = (f32[48,256]{1,0:T(8,128)S(1)}, f32[72,128]{1,0:T(8,128)S(1)}, f32[256,128]{1,0:T(8,128)}) custom-call(f32[48,256]{1,0:T(8,128)S(1)} %add_add_fusion.refs_0_, bf16[3,192,256]{2,1,0:T(8,128)(2,1)S(1)} %get-tuple-element.35.refs_1_, bf16[3,192,256]{2,1,0:T(8,128)(2,1)S(1)} %get-tuple-element.36.refs_2_, ...), custom_call_target="tpu_custom_call" | custom-call | tf_op jit(solution)/shard_map/pallas_call | solution.py:134
  72.5 0.9 collective-permute-start.12
  73.4 0.9 collective-permute-done.12
  74.3 1.0 %collective-permute-start.13 = (f32[72,128]{1,0:T(8,128)S(1)}, f32[72,128]{1,0:T(8,128)S(1)}, u32[]{:S(2)}, u32[]{:S(2)}) collective-permute-start(f32[72,128]{1,0:T(8,128)S(1)} %add.59), channel_id=1, source_target_pairs={{0,9},{1,8},{2,11},{3,10},{4,13},{5,12},{6,15},{7,14},{8,1},{9,0},... | collective-permute-start | bytes 110600 | tf_op jit(solution)/shard_map/ppermute | solution.py:28
  75.3 3.5 %all-to-all-start.2 = ((f32[16,1,2048]{2,1,0:T(1,128)}), f32[16,1,2048]{2,1,0:T(1,128)S(1)}, u32[]{:S(2)}, u32[]{:S(2)}) async-start(f32[16,1,2048]{2,1,0:T(1,128)} %bitcast.17), calls=%async_computation.2 | async-start | bytes 262144 | tf_op jit(solution)/shard_map/all_to_all | solution.py:477
  78.8 0.8 collective-permute-done.13
  79.6 1.0 %collective-permute-start.15 = (f32[72,128]{1,0:T(8,128)S(1)}, f32[72,128]{1,0:T(8,128)S(1)}, u32[]{:S(2)}, u32[]{:S(2)}) collective-permute-start(f32[72,128]{1,0:T(8,128)S(1)} %add.60), channel_id=1, source_target_pairs={{0,5},{1,4},{2,7},{3,6},{4,1},{5,0},{6,3},{7,2},{8,13},{9,12},{10,... | collective-permute-start | bytes 110600 | tf_op jit(solution)/shard_map/ppermute | solution.py:28
  80.6 1.4 %collective-permute-start.16 = (f32[72,128]{1,0:T(8,128)S(1)}, f32[72,128]{1,0:T(8,128)S(1)}, u32[]{:S(2)}, u32[]{:S(2)}) collective-permute-start(f32[72,128]{1,0:T(8,128)S(1)} %add.60), channel_id=1, source_target_pairs={{0,7},{1,6},{2,5},{3,4},{4,3},{5,2},{6,1},{7,0},{8,15},{9,14},{10,... | collective-permute-start | bytes 110600 | tf_op jit(solution)/shard_map/ppermute | solution.py:28
  82.0 0.5 collective-permute-start.14
  82.5 0.7 dynamic-slice_bitcast_fusion
  83.2 0.6 copy.17
  83.8 0.2 collective-permute-done.15
  84.1 1.8 %collective-permute-done.16 = f32[72,128]{1,0:T(8,128)S(1)} collective-permute-done((f32[72,128]{1,0:T(8,128)S(1)}, f32[72,128]{1,0:T(8,128)S(1)}, u32[]{:S(2)}, u32[]{:S(2)}) %collective-permute-start.16) | collective-permute-done | bytes 36896 | tf_op jit(solution)/shard_map/ppermute | solution.py:28
  85.9 0.7 collective-permute-done.14
  86.6 0.7 all-to-all-done.2
  87.3 2.6 %shard_map.81 = (f32[24,48]{1,0:T(8,128)}, f32[48,144]{1,0:T(8,128)}) custom-call(f32[72,128]{1,0:T(8,128)S(1)} %add_add_fusion.1.refs_0_, f32[256,128]{1,0:T(8,128)S(1)} %bitcast.13), custom_call_target="tpu_custom_call" | custom-call | tf_op jit(solution)/shard_map/pallas_call | solution.py:134
  (16 shorter events, 0.1 us)
Async XLA Ops:
  0.6 10.3 %copy-start.1 = (f32[64,48]{0,1:T(8,128)S(1)}, f32[64,48]{0,1:T(8,128)}, u32[]{:S(2)}) copy-start(f32[64,48]{0,1:T(8,128)} %param.5) | copy-start | bytes 36868
  3.4 8.1 %collective-permute-start = (f32[12,64,256]{2,1,0:T(8,128)}, f32[12,64,256]{2,1,0:T(8,128)S(1)}, u32[]{:S(2)}, u32[]{:S(2)}) collective-permute-start(f32[12,64,256]{2,1,0:T(8,128)} %get-tuple-element.24), channel_id=1, source_target_pairs={{0,1},{1,0},{2,3},{3,2},{4,5},{5,4},{6,7},{7,6},{8,9},{9,8},{10,11... | collective-permute-start | bytes 2359304 | tf_op jit(solution)/shard_map/ppermute | solution.py:50
  3.9 18.4 %all-to-all-start = ((f32[16,1,5376]{2,1,0:T(1,128)}), f32[16,1,5376]{2,1,0:T(1,128)S(1)}, u32[]{:S(2)}, u32[]{:S(2)}) async-start(f32[16,1,5376]{2,1,0:T(1,128)} %bitcast.15), calls=%async_computation | async-start | bytes 688128 | tf_op jit(solution)/shard_map/all_to_all | solution.py:477
  11.0 11.2 %collective-permute-start.1 = (f32[64,48]{1,0:T(8,128)S(1)}, f32[64,48]{1,0:T(8,128)S(1)}, u32[]{:S(2)}, u32[]{:S(2)}) collective-permute-start(f32[64,48]{1,0:T(8,128)S(1)} %copy.13.refs_1_), channel_id=1, source_target_pairs={{0,1},{1,0},{2,3},{3,2},{4,5},{5,4},{6,7},{7,6},{8,9},{9,8},{10,11... | collective-permute-start | bytes 36872 | tf_op jit(solution)/shard_map/ppermute | solution.py:50
  23.3 17.1 %copy-start = (f32[256,48]{0,1:T(8,128)S(1)}, f32[256,48]{0,1:T(8,128)}, u32[]{:S(2)}) copy-start(f32[256,48]{0,1:T(8,128)} %param.6) | copy-start | bytes 147460
  23.3 1.2 %collective-permute-start.2 = (f32[48,128]{1,0:T(8,128)S(1)}, f32[48,128]{1,0:T(8,128)S(1)}, u32[]{:S(2)}, u32[]{:S(2)}) collective-permute-start(f32[48,128]{1,0:T(8,128)S(1)} %get-tuple-element.28), channel_id=1, source_target_pairs={{0,1},{1,0},{2,3},{3,2},{4,5},{5,4},{6,7},{7,6},{8,9},{9,8},{10,11... | collective-permute-start | bytes 73736 | tf_op jit(solution)/shard_map/ppermute | solution.py:28
  24.5 4.2 %collective-permute-start.3 = (f32[48,128]{1,0:T(8,128)S(1)}, f32[48,128]{1,0:T(8,128)S(1)}, u32[]{:S(2)}, u32[]{:S(2)}) collective-permute-start(f32[48,128]{1,0:T(8,128)S(1)} %add.48), channel_id=1, source_target_pairs={{0,9},{1,8},{2,11},{3,10},{4,13},{5,12},{6,15},{7,14},{8,1},{9,0},... | collective-permute-start | bytes 73736 | tf_op jit(solution)/shard_map/ppermute | solution.py:28
  28.7 3.4 %collective-permute-start.5 = (f32[48,128]{1,0:T(8,128)S(1)}, f32[48,128]{1,0:T(8,128)S(1)}, u32[]{:S(2)}, u32[]{:S(2)}) collective-permute-start(f32[48,128]{1,0:T(8,128)S(1)} %add.49), channel_id=1, source_target_pairs={{0,5},{1,4},{2,7},{3,6},{4,1},{5,0},{6,3},{7,2},{8,13},{9,12},{10,... | collective-permute-start | bytes 73736 | tf_op jit(solution)/shard_map/ppermute | solution.py:28
  29.3 4.2 %collective-permute-start.6 = (f32[48,128]{1,0:T(8,128)S(1)}, f32[48,128]{1,0:T(8,128)S(1)}, u32[]{:S(2)}, u32[]{:S(2)}) collective-permute-start(f32[48,128]{1,0:T(8,128)S(1)} %add.49), channel_id=1, source_target_pairs={{0,7},{1,6},{2,5},{3,4},{4,3},{5,2},{6,1},{7,0},{8,15},{9,14},{10,... | collective-permute-start | bytes 73736 | tf_op jit(solution)/shard_map/ppermute | solution.py:28
  30.3 3.7 %collective-permute-start.4 = (f32[48,128]{1,0:T(8,128)S(1)}, f32[48,128]{1,0:T(8,128)S(1)}, u32[]{:S(2)}, u32[]{:S(2)}) collective-permute-start(f32[48,128]{1,0:T(8,128)S(1)} %add.49), channel_id=1, source_target_pairs={{0,3},{1,2},{2,1},{3,0},{4,7},{5,6},{6,5},{7,4},{8,11},{9,10},{10,... | collective-permute-start | bytes 73736 | tf_op jit(solution)/shard_map/ppermute | solution.py:28
  36.8 19.1 %all-to-all-start.1 = ((f32[16,1,9216]{2,1,0:T(1,128)}), f32[16,1,9216]{2,1,0:T(1,128)S(1)}, u32[]{:S(2)}, u32[]{:S(2)}) async-start(f32[16,1,9216]{2,1,0:T(1,128)} %bitcast.14), calls=%async_computation.1 | async-start | bytes 1179648 | tf_op jit(solution)/shard_map/all_to_all | solution.py:477
  56.6 1.3 %collective-permute-start.7 = (f32[48,256]{1,0:T(8,128)S(1)}, f32[48,256]{1,0:T(8,128)S(1)}, u32[]{:S(2)}, u32[]{:S(2)}) collective-permute-start(f32[48,256]{1,0:T(8,128)S(1)} %get-tuple-element.34), channel_id=1, source_target_pairs={{0,1},{1,0},{2,3},{3,2},{4,5},{5,4},{6,7},{7,6},{8,9},{9,8},{10,11... | collective-permute-start | bytes 147464 | tf_op jit(solution)/shard_map/ppermute | solution.py:28
  58.0 3.8 %collective-permute-start.8 = (f32[48,256]{1,0:T(8,128)S(1)}, f32[48,256]{1,0:T(8,128)S(1)}, u32[]{:S(2)}, u32[]{:S(2)}) collective-permute-start(f32[48,256]{1,0:T(8,128)S(1)} %add.54), channel_id=1, source_target_pairs={{0,3},{1,2},{2,1},{3,0},{4,7},{5,6},{6,5},{7,4},{8,11},{9,10},{10,... | collective-permute-start | bytes 147464 | tf_op jit(solution)/shard_map/ppermute | solution.py:28
  61.8 4.7 %collective-permute-start.10 = (f32[48,256]{1,0:T(8,128)S(1)}, f32[48,256]{1,0:T(8,128)S(1)}, u32[]{:S(2)}, u32[]{:S(2)}) collective-permute-start(f32[48,256]{1,0:T(8,128)S(1)} %add.55), channel_id=1, source_target_pairs={{0,9},{1,8},{2,11},{3,10},{4,13},{5,12},{6,15},{7,14},{8,1},{9,0},... | collective-permute-start | bytes 147464 | tf_op jit(solution)/shard_map/ppermute | solution.py:28
  64.1 5.4 %collective-permute-start.11 = (f32[48,256]{1,0:T(8,128)S(1)}, f32[48,256]{1,0:T(8,128)S(1)}, u32[]{:S(2)}, u32[]{:S(2)}) collective-permute-start(f32[48,256]{1,0:T(8,128)S(1)} %add.55), channel_id=1, source_target_pairs={{0,13},{1,12},{2,15},{3,14},{4,9},{5,8},{6,11},{7,10},{8,5},{9,4},... | collective-permute-start | bytes 147464 | tf_op jit(solution)/shard_map/ppermute | solution.py:28
  65.3 4.1 %collective-permute-start.9 = (f32[48,256]{1,0:T(8,128)S(1)}, f32[48,256]{1,0:T(8,128)S(1)}, u32[]{:S(2)}, u32[]{:S(2)}) collective-permute-start(f32[48,256]{1,0:T(8,128)S(1)} %add.55), channel_id=1, source_target_pairs={{0,5},{1,4},{2,7},{3,6},{4,1},{5,0},{6,3},{7,2},{8,13},{9,12},{10,... | collective-permute-start | bytes 147464 | tf_op jit(solution)/shard_map/ppermute | solution.py:28
  72.5 1.7 %collective-permute-start.12 = (f32[72,128]{1,0:T(8,128)S(1)}, f32[72,128]{1,0:T(8,128)S(1)}, u32[]{:S(2)}, u32[]{:S(2)}) collective-permute-start(f32[72,128]{1,0:T(8,128)S(1)} %get-tuple-element.38), channel_id=1, source_target_pairs={{0,1},{1,0},{2,3},{3,2},{4,5},{5,4},{6,7},{7,6},{8,9},{9,8},{10,11... | collective-permute-start | bytes 110600 | tf_op jit(solution)/shard_map/ppermute | solution.py:28
  74.3 5.3 %collective-permute-start.13 = (f32[72,128]{1,0:T(8,128)S(1)}, f32[72,128]{1,0:T(8,128)S(1)}, u32[]{:S(2)}, u32[]{:S(2)}) collective-permute-start(f32[72,128]{1,0:T(8,128)S(1)} %add.59), channel_id=1, source_target_pairs={{0,9},{1,8},{2,11},{3,10},{4,13},{5,12},{6,15},{7,14},{8,1},{9,0},... | collective-permute-start | bytes 110600 | tf_op jit(solution)/shard_map/ppermute | solution.py:28
  75.3 12.0 %all-to-all-start.2 = ((f32[16,1,2048]{2,1,0:T(1,128)}), f32[16,1,2048]{2,1,0:T(1,128)S(1)}, u32[]{:S(2)}, u32[]{:S(2)}) async-start(f32[16,1,2048]{2,1,0:T(1,128)} %bitcast.17), calls=%async_computation.2 | async-start | bytes 262144 | tf_op jit(solution)/shard_map/all_to_all | solution.py:477
  79.6 4.5 %collective-permute-start.15 = (f32[72,128]{1,0:T(8,128)S(1)}, f32[72,128]{1,0:T(8,128)S(1)}, u32[]{:S(2)}, u32[]{:S(2)}) collective-permute-start(f32[72,128]{1,0:T(8,128)S(1)} %add.60), channel_id=1, source_target_pairs={{0,5},{1,4},{2,7},{3,6},{4,1},{5,0},{6,3},{7,2},{8,13},{9,12},{10,... | collective-permute-start | bytes 110600 | tf_op jit(solution)/shard_map/ppermute | solution.py:28
  80.6 5.3 %collective-permute-start.16 = (f32[72,128]{1,0:T(8,128)S(1)}, f32[72,128]{1,0:T(8,128)S(1)}, u32[]{:S(2)}, u32[]{:S(2)}) collective-permute-start(f32[72,128]{1,0:T(8,128)S(1)} %add.60), channel_id=1, source_target_pairs={{0,7},{1,6},{2,5},{3,4},{4,3},{5,2},{6,1},{7,0},{8,15},{9,14},{10,... | collective-permute-start | bytes 110600 | tf_op jit(solution)/shard_map/ppermute | solution.py:28
  82.0 4.6 %collective-permute-start.14 = (f32[72,128]{1,0:T(8,128)S(1)}, f32[72,128]{1,0:T(8,128)S(1)}, u32[]{:S(2)}, u32[]{:S(2)}) collective-permute-start(f32[72,128]{1,0:T(8,128)S(1)} %add.60), channel_id=1, source_target_pairs={{0,3},{1,2},{2,1},{3,0},{4,7},{5,6},{6,5},{7,4},{8,11},{9,10},{10,... | collective-permute-start | bytes 110600 | tf_op jit(solution)/shard_map/ppermute | solution.py:28
